TPU v7x, 32 devices: a whole 2x2x4 slice. The times are simulated.
32 devices in a mesh: ctx: 8 (over z, y), fsdp: 4 (over x, core).
Axes of the slice: x: 2, y: 2, z: 4, core: 2. Of those that a mesh axis runs over, the one named last changes fastest.
Arguments:
- tokens: bfloat16 [4, 1024, 1536], P('fsdp', 'ctx'), may hold values from -6 to 6
- doc_lengths: int32 [4, 8], P('fsdp'), may hold values from 1 to 512, 1024 in all within a row
- attention_gain: bfloat16 [1536], P(('ctx', 'fsdp')), may hold values from 0.5 to 1.5
- query_weight: bfloat16 [1536, 1536], P(('ctx', 'fsdp')), may hold values from -0.21875 to 0.21875
- key_weight: bfloat16 [1536, 768], P(('ctx', 'fsdp')), may hold values from -0.21875 to 0.21875
- value_weight: bfloat16 [1536, 768], P(('ctx', 'fsdp')), may hold values from -0.15625 to 0.15625
- output_weight: bfloat16 [1536, 1536], P(('ctx', 'fsdp')), may hold values from -0.625 to 0.625
- feedforward_gain: bfloat16 [1536], P(('ctx', 'fsdp')), may hold values from 0.5 to 1.5
- gate_weight: bfloat16 [1536, 4096], P(('ctx', 'fsdp')), may hold values from -0.15625 to 0.15625
- up_weight: bfloat16 [1536, 4096], P(('ctx', 'fsdp')), may hold values from -0.15625 to 0.15625
- down_weight: bfloat16 [4096, 1536], P(('ctx', 'fsdp')), may hold values from -0.09375 to 0.09375
- cotangent: bfloat16 [4, 1024, 1536], P('fsdp', 'ctx'), may hold values from -6 to 6
Outputs:
- layer_out: bfloat16 [4, 1024, 1536], P('fsdp', 'ctx')
- tokens_grad: float32 [4, 1024, 1536], P('fsdp', 'ctx')
- attention_gain_grad: float32 [1536], P(('ctx', 'fsdp'))
- query_weight_grad: float32 [1536, 1536], P(('ctx', 'fsdp'))
- key_weight_grad: float32 [1536, 768], P(('ctx', 'fsdp'))
- value_weight_grad: float32 [1536, 768], P(('ctx', 'fsdp'))
- output_weight_grad: float32 [1536, 1536], P(('ctx', 'fsdp'))
- feedforward_gain_grad: float32 [1536], P(('ctx', 'fsdp'))
- gate_weight_grad: float32 [1536, 4096], P(('ctx', 'fsdp'))
- up_weight_grad: float32 [1536, 4096], P(('ctx', 'fsdp'))
- down_weight_grad: float32 [4096, 1536], P(('ctx', 'fsdp'))
Inputs may be any that keep to these rules, and one draw needn't show every extreme that they name: `doc_lengths`: each stream's row holds the lengths of its 8 documents in order; they sum to 1024 and the longest is exactly 512.
All inputs are finite; a program needn't handle non-finite values.
Results may differ from a plain program's by a relative error of at most 0.014.
The roundings to bfloat16 on the way count: a program that leaves them out, or rounds other values in their place, can miss the bound.
Values may be sent and summed in bfloat16 or wider, within the bound.
A program may use at most 384 MiB of HBM per device.

v0:
```python
import jax
import jax.numpy as jnp
from jax import lax
from jax.sharding import PartitionSpec as P

D = 1536
H = 16
KVH = 8
HD = 96
KBLK = 512
DOC_MOST = 4096
KVW = 768


EPSILON = 1e-05
ROPE_BASE = 100000.0
MASKED_SCORE = -1e30


def rms_scale(values):
    return lax.rsqrt(jnp.mean(values * values, axis=-1, keepdims=True) + EPSILON)


def document_layout(lengths, total):
    starts = jnp.cumsum(lengths) - lengths
    places = jnp.arange(total, dtype=jnp.int32)
    inside = places[:, None] >= starts[None, :]
    doc_ids = jnp.sum(inside.astype(jnp.int32), axis=1) - 1
    doc_starts = jnp.max(jnp.where(inside, starts[None, :], 0), axis=1)
    return (doc_ids, places - doc_starts)


def rotate(values, positions, head_count, direction):
    row_count = values.shape[0]
    half_dim = HD // 2
    inverse_freq = ROPE_BASE ** (-(jnp.arange(half_dim).astype(jnp.float32) * (2.0 / HD)))
    angles = positions.astype(jnp.float32)[:, None] * inverse_freq[None, :]
    cosine = jnp.cos(angles)[:, None, :]
    sine_part = direction * jnp.sin(angles)[:, None, :]
    grouped = values.reshape(row_count, head_count, HD)
    former = grouped[:, :, :half_dim]
    latter = grouped[:, :, half_dim:]
    turned = jnp.concatenate(
        [former * cosine - latter * sine_part, latter * cosine + former * sine_part], axis=2
    )
    return turned.reshape(row_count, head_count * HD)


def outer_rows(left, right):
    return lax.dot_general(
        left, right, (((0,), (0,)), ((), ())), preferred_element_type=jnp.float32
    )


def times_transposed(left, right):
    return lax.dot_general(
        left, right, (((1,), (1,)), ((), ())), preferred_element_type=jnp.float32
    )


def body(
    tokens,
    doc_lengths,
    attention_gain,
    query_weight,
    key_weight,
    value_weight,
    output_weight,
    feedforward_gain,
    gate_weight,
    up_weight,
    down_weight,
    cotangent,
):
    local_tokens = tokens[0].astype(jnp.float32)
    tok_rows = local_tokens.shape[0]
    stream_len = tok_rows * lax.axis_size("ctx")
    my_first = lax.axis_index("ctx") * tok_rows
    key_docs_all, places_all = document_layout(doc_lengths[0], stream_len)
    query_docs = lax.dynamic_slice_in_dim(key_docs_all, my_first, tok_rows, 0)
    query_positions = lax.dynamic_slice_in_dim(places_all, my_first, tok_rows, 0)
    query_places = my_first + jnp.arange(tok_rows, dtype=jnp.int32)
    group_size = H // KVH
    score_scale = HD ** (-0.5)
    attention_set = (
        lax.all_gather(attention_gain, ("ctx", "fsdp"), axis=0, tiled=True),
        lax.all_gather(query_weight, ("ctx", "fsdp"), axis=0, tiled=True),
        lax.all_gather(key_weight, ("ctx", "fsdp"), axis=0, tiled=True),
        lax.all_gather(value_weight, ("ctx", "fsdp"), axis=0, tiled=True),
        lax.all_gather(output_weight, ("ctx", "fsdp"), axis=0, tiled=True),
    )
    gain_one, query_full, key_full, value_full, output_full = attention_set
    scale_one = rms_scale(local_tokens)
    normed_one = local_tokens * scale_one
    gain_one_f = gain_one.astype(jnp.float32)
    normed_low = (normed_one * gain_one_f).astype(jnp.bfloat16)
    queries = jnp.dot(normed_low, query_full, preferred_element_type=jnp.float32)
    keys_new = jnp.dot(normed_low, key_full, preferred_element_type=jnp.float32)
    values_new = jnp.dot(normed_low, value_full, preferred_element_type=jnp.float32)
    query_low = rotate(queries, query_positions, H, 1.0).astype(jnp.bfloat16)
    key_low = rotate(keys_new, query_positions, KVH, 1.0).astype(jnp.bfloat16)
    value_low = values_new.astype(jnp.bfloat16)
    key_all, value_all = (
        lax.all_gather(key_low, "ctx", axis=0, tiled=True),
        lax.all_gather(value_low, "ctx", axis=0, tiled=True),
    )
    max_doc = min(DOC_MOST, KBLK * (stream_len // (2 * KBLK)))
    block_total = stream_len // KBLK
    window = min(max_doc // KBLK + 2, block_total)
    first_block = jnp.clip((my_first - max_doc) // KBLK, 0, block_total - window)
    query_grouped = query_low.reshape(tok_rows, KVH, group_size, HD)

    def block_scores(block_index):
        key_start = block_index * KBLK
        key_block = lax.dynamic_slice_in_dim(key_all, key_start, KBLK, 0).reshape(KBLK, KVH, HD)
        value_block = lax.dynamic_slice_in_dim(value_all, key_start, KBLK, 0).reshape(KBLK, KVH, HD)
        key_docs = lax.dynamic_slice_in_dim(key_docs_all, key_start, KBLK, 0)
        key_places = key_start + jnp.arange(KBLK, dtype=jnp.int32)
        allowed = (
            (key_docs[None, :] == query_docs[:, None])
            & (key_places[None, :] <= query_places[:, None])
        )[:, None, None, :]
        scores = (
            jnp.einsum(
                "qgrd,kgd->qgrk", query_grouped, key_block, preferred_element_type=jnp.float32
            )
            * score_scale
        )
        return (jnp.where(allowed, scores, MASKED_SCORE), allowed, key_block, value_block)

    def stats_step(carried, offset):
        block_index = first_block + offset
        running_max, running_sum = carried
        scores, allowed, key_block, value_block = block_scores(block_index)
        new_max = jnp.maximum(running_max, jnp.max(scores, axis=-1, keepdims=True))
        weights = jnp.where(allowed, jnp.exp(scores - new_max), 0.0)
        return (
            (
                new_max,
                running_sum * jnp.exp(running_max - new_max)
                + jnp.sum(weights, axis=-1, keepdims=True),
            ),
            None,
        )

    stat_shape = (tok_rows, KVH, group_size, 1)
    start_stats = (
        jnp.full(stat_shape, MASKED_SCORE, jnp.float32),
        jnp.zeros(stat_shape, jnp.float32),
    )
    (final_max, final_sum), unused_stats = lax.scan(
        stats_step, start_stats, jnp.arange(window, dtype=jnp.int32)
    )
    log_total = final_max + jnp.log(final_sum)

    def mix_step(carried, offset):
        block_index = first_block + offset
        scores, allowed, key_block, value_block = block_scores(block_index)
        probs_low = jnp.where(allowed, jnp.exp(scores - log_total), 0.0).astype(jnp.bfloat16)
        return (
            carried
            + jnp.einsum(
                "qgrk,kgd->qgrd", probs_low, value_block, preferred_element_type=jnp.float32
            ),
            None,
        )

    attended_sum, unused_mix = lax.scan(
        mix_step,
        jnp.zeros((tok_rows, KVH, group_size, HD), jnp.float32),
        jnp.arange(window, dtype=jnp.int32),
    )
    attended_low = attended_sum.reshape(tok_rows, D).astype(jnp.bfloat16)
    middle = local_tokens + jnp.dot(attended_low, output_full, preferred_element_type=jnp.float32)
    feedforward_set = (
        lax.all_gather(feedforward_gain, ("ctx", "fsdp"), axis=0, tiled=True),
        lax.all_gather(gate_weight, ("ctx", "fsdp"), axis=0, tiled=True),
        lax.all_gather(up_weight, ("ctx", "fsdp"), axis=0, tiled=True),
        lax.all_gather(down_weight, ("ctx", "fsdp"), axis=0, tiled=True),
    )
    gain_two, gate_full, up_full, down_full = feedforward_set
    gain_two_f = gain_two.astype(jnp.float32)
    scale_two = rms_scale(middle)
    normed_two = middle * scale_two
    normed_two_low = (normed_two * gain_two_f).astype(jnp.bfloat16)
    gate_pre = jnp.dot(normed_two_low, gate_full, preferred_element_type=jnp.float32)
    up_pre = jnp.dot(normed_two_low, up_full, preferred_element_type=jnp.float32)
    sigmoid = jax.nn.sigmoid(gate_pre)
    hidden_low = (gate_pre * sigmoid * up_pre).astype(jnp.bfloat16)
    layer_out = middle + jnp.dot(hidden_low, down_full, preferred_element_type=jnp.float32)
    grad_out = cotangent[0]
    piece = hidden_low
    down_weight_grad = lax.psum_scatter(
        outer_rows(piece, grad_out), ("ctx", "fsdp"), scatter_dimension=0, tiled=True
    )
    hidden_grad = times_transposed(grad_out, down_full)
    gate_grad = (hidden_grad * up_pre * sigmoid * (1.0 + gate_pre * (1.0 - sigmoid))).astype(
        jnp.bfloat16
    )
    up_grad = (hidden_grad * gate_pre * sigmoid).astype(jnp.bfloat16)
    gate_up_cat = jnp.concatenate([gate_grad, up_grad], axis=1)
    piece = normed_two_low
    gate_up_sum = lax.psum_scatter(
        outer_rows(piece, gate_up_cat), ("ctx", "fsdp"), scatter_dimension=0, tiled=True
    )
    ff_width = gate_full.shape[1]
    normed_two_grad = times_transposed(gate_grad, gate_full) + times_transposed(up_grad, up_full)
    gain_two_term = jnp.sum(normed_two_grad * normed_two, axis=0)
    scaled_two = normed_two_grad * gain_two_f
    middle_grad = grad_out.astype(jnp.float32) + scale_two * (
        scaled_two - normed_two * jnp.mean(scaled_two * normed_two, axis=-1, keepdims=True)
    )
    branch_grad = middle_grad.astype(jnp.bfloat16)
    attended_grad_low = (
        times_transposed(branch_grad, output_full)
        .astype(jnp.bfloat16)
        .reshape(tok_rows, KVH, group_size, HD)
    )
    row_delta = jnp.sum(
        attended_grad_low.astype(jnp.float32) * attended_sum, axis=-1, keepdims=True
    )

    def back_step(carried, offset):
        block_index = first_block + offset
        scores, allowed, key_block, value_block = block_scores(block_index)
        probs = jnp.where(allowed, jnp.exp(scores - log_total), 0.0)
        probs_low = probs.astype(jnp.bfloat16)
        prob_grad = jnp.einsum(
            "qgrd,kgd->qgrk", attended_grad_low, value_block, preferred_element_type=jnp.float32
        )
        score_grad = (probs * (prob_grad - row_delta)).astype(jnp.bfloat16)
        new_accum = carried + jnp.einsum(
            "qgrk,kgd->qgrd", score_grad, key_block, preferred_element_type=jnp.float32
        )
        key_term = jnp.einsum(
            "qgrk,qgrd->kgd", score_grad, query_grouped, preferred_element_type=jnp.float32
        )
        value_term = jnp.einsum(
            "qgrk,qgrd->kgd", probs_low, attended_grad_low, preferred_element_type=jnp.float32
        )
        return (new_accum, (key_term, value_term))

    query_accum, (key_terms, value_terms) = lax.scan(
        back_step,
        jnp.zeros((tok_rows, KVH, group_size, HD), jnp.float32),
        jnp.arange(window, dtype=jnp.int32),
    )
    window_start = first_block * KBLK
    key_window = lax.dynamic_update_slice_in_dim(
        jnp.zeros((stream_len, KVW), jnp.float32),
        key_terms.reshape(window * KBLK, KVW),
        window_start,
        0,
    )
    value_window = lax.dynamic_update_slice_in_dim(
        jnp.zeros((stream_len, KVW), jnp.float32),
        value_terms.reshape(window * KBLK, KVW),
        window_start,
        0,
    )
    key_sum, value_sum = (
        lax.psum_scatter(key_window, "ctx", scatter_dimension=0, tiled=True),
        lax.psum_scatter(value_window, "ctx", scatter_dimension=0, tiled=True),
    )
    key_grad_low = rotate(key_sum * score_scale, query_positions, KVH, -1.0).astype(jnp.bfloat16)
    value_grad_low = value_sum.astype(jnp.bfloat16)
    query_grad_low = rotate(
        query_accum.reshape(tok_rows, D) * score_scale, query_positions, H, -1.0
    ).astype(jnp.bfloat16)
    projection_cat = jnp.concatenate([query_grad_low, key_grad_low, value_grad_low], axis=1)
    attention_sum = lax.psum_scatter(
        jnp.concatenate(
            [outer_rows(normed_low, projection_cat), outer_rows(attended_low, branch_grad)], axis=1
        ),
        ("ctx", "fsdp"),
        scatter_dimension=0,
        tiled=True,
    )
    normed_grad = (
        times_transposed(query_grad_low, query_full)
        + times_transposed(key_grad_low, key_full)
        + times_transposed(value_grad_low, value_full)
    )
    gain_one_term = jnp.sum(normed_grad * normed_one, axis=0)
    scaled_one = normed_grad * gain_one_f
    tokens_grad = middle_grad + scale_one * (
        scaled_one - normed_one * jnp.mean(scaled_one * normed_one, axis=-1, keepdims=True)
    )
    gain_parts = (
        lax.psum_scatter(gain_one_term, ("ctx", "fsdp"), scatter_dimension=0, tiled=True),
        lax.psum_scatter(gain_two_term, ("ctx", "fsdp"), scatter_dimension=0, tiled=True),
    )
    width_q = query_full.shape[1]
    width_k = key_full.shape[1]
    return (
        layer_out.astype(jnp.bfloat16)[None],
        tokens_grad[None],
        gain_parts[0],
        attention_sum[:, :width_q],
        attention_sum[:, width_q : width_q + width_k],
        attention_sum[:, width_q + width_k : width_q + 2 * width_k],
        attention_sum[:, width_q + 2 * width_k :],
        gain_parts[1],
        gate_up_sum[:, :ff_width],
        gate_up_sum[:, ff_width:],
        down_weight_grad,
    )


def solution(mesh):
    return jax.shard_map(
        body,
        mesh=mesh,
        in_specs=(
            P("fsdp", "ctx", None),
            P("fsdp", None),
            P(("ctx", "fsdp")),
            P(("ctx", "fsdp"), None),
            P(("ctx", "fsdp"), None),
            P(("ctx", "fsdp"), None),
            P(("ctx", "fsdp"), None),
            P(("ctx", "fsdp")),
            P(("ctx", "fsdp"), None),
            P(("ctx", "fsdp"), None),
            P(("ctx", "fsdp"), None),
            P("fsdp", "ctx", None),
        ),
        out_specs=(
            P("fsdp", "ctx", None),
            P("fsdp", "ctx", None),
            P(("ctx", "fsdp")),
            P(("ctx", "fsdp"), None),
            P(("ctx", "fsdp"), None),
            P(("ctx", "fsdp"), None),
            P(("ctx", "fsdp"), None),
            P(("ctx", "fsdp")),
            P(("ctx", "fsdp"), None),
            P(("ctx", "fsdp"), None),
            P(("ctx", "fsdp"), None),
        ),
        check_vma=False,
    )
```

profile of v0, /device:TPU:0, one launch (start us, length us, event | category | flops | bytes accessed | tf_op | source)
XLA Modules:
  0.0 1970.3 jit_solution(9254830339892357664)
XLA Ops:
  10.4 42.1 %all-reduce.5 = (bf16[1536]{0:T(1024)(128)(2,1)S(1)}, bf16[1536]{0:T(1024)(128)(2,1)S(1)}) all-reduce(bf16[1536]{0:T(1024)(128)(2,1)S(1)} %dynamic-update-slice, bf16[1536]{0:T(1024)(128)(2,1)S(1)} %dynamic-update-slice.1), channel_id=1, replica_groups=mesh['ctx'=8,'fsdp'=4] {'ctx','fsdp'}, use_global_device_ids=true, to_apply=%add | all-reduce | flops 3072 | bytes 12288
  53.8 17.1 all-gather.10.cloned.1.call-done
  77.0 52.9 %all-gather.14.cloned.1.call-done = bf16[1536,768]{1,0:T(8,128)(2,1)} async-done(((bf16[48,768]{1,0:T(8,128)(2,1)}), bf16[1536,768]{1,0:T(8,128)(2,1)}) %all-gather.14.cloned.1.call-update) | async-done | bytes 2359312 | tf_op jit(solution)/shard_map/all_gather | solution.py:88
  137.5 38.4 %all-gather.12.cloned.1.call-done = bf16[1024,768]{1,0:T(8,128)(2,1)} async-done(((bf16[128,768]{1,0:T(8,128)(2,1)}), bf16[1024,768]{1,0:T(8,128)(2,1)}) %all-gather.12.cloned.1.call-update) | async-done | bytes 1572880 | tf_op jit(solution)/shard_map/all_gather | solution.py:105
  178.5 62.6 %all-gather.18.cloned.1.call-done = bf16[1536,1536]{1,0:T(8,128)(2,1)} async-done(((bf16[48,1536]{1,0:T(8,128)(2,1)}), bf16[1536,1536]{1,0:T(8,128)(2,1)}) %all-gather.18.cloned.1.call-update) | async-done | bytes 4718608 | tf_op jit(solution)/shard_map/all_gather | solution.py:87
  251.8 35.9 %all-gather.16.cloned.1.call-done = bf16[1024,768]{0,1:T(8,128)(2,1)} async-done(((bf16[128,768]{0,1:T(8,128)(2,1)}), bf16[1024,768]{0,1:T(8,128)(2,1)}) %all-gather.16.cloned.1.call-update) | async-done | bytes 1572880 | tf_op jit(solution)/shard_map/all_gather | solution.py:104
  287.7 17.6 while.39
  315.4 36.9 %all-gather.20.cloned.1.call-done = bf16[1536,1536]{1,0:T(8,128)(2,1)} async-done(((bf16[48,1536]{1,0:T(8,128)(2,1)}), bf16[1536,1536]{1,0:T(8,128)(2,1)}) %all-gather.20.cloned.1.call-update) | async-done | bytes 4718608 | tf_op jit(solution)/shard_map/all_gather | solution.py:90
  355.7 94.2 %all-gather.22.cloned.1.call-done = bf16[1536,4096]{1,0:T(8,128)(2,1)} async-done(((bf16[48,4096]{1,0:T(8,128)(2,1)}), bf16[1536,4096]{1,0:T(8,128)(2,1)}) %all-gather.22.cloned.1.call-update) | async-done | bytes 12582928 | tf_op jit(solution)/shard_map/all_gather | solution.py:177
  457.6 89.4 %all-gather.24.cloned.1.call-done = bf16[1536,4096]{1,0:T(8,128)(2,1)} async-done(((bf16[48,4096]{1,0:T(8,128)(2,1)}), bf16[1536,4096]{1,0:T(8,128)(2,1)}) %all-gather.24.cloned.1.call-update) | async-done | bytes 12582928 | tf_op jit(solution)/shard_map/all_gather | solution.py:178
  554.7 89.4 %all-gather.26.cloned.1.call-done = bf16[4096,1536]{1,0:T(8,128)(2,1)} async-done(((bf16[128,1536]{1,0:T(8,128)(2,1)}), bf16[4096,1536]{1,0:T(8,128)(2,1)}) %all-gather.26.cloned.1.call-update) | async-done | bytes 12582928 | tf_op jit(solution)/shard_map/all_gather | solution.py:179
  679.6 147.4 %while.41 = (s32[]{:T(128)}, f32[128,8,2,96]{0,3,2,1:T(8,128)}, f32[2,512,8,96]{1,0,3,2:T(2,128)}, f32[2,512,8,96]{1,0,3,2:T(2,128)}, s32[2]{0:T(128)S(1)}, /*in...) while((s32[]{:T(128)}, f32[128,8,2,96]{0,3,2,1:T(8,128)}, ...), condition=%wide.region_14.15_spmd.clone, body=%wide.region_13.14_spmd.clone.sunk | while | flops 1019806336 | bytes 60264248 | solution.py:243
  690.1 28.8 %dynamic_update_slice.13 = f32[2,512,8,96]{1,0,3,2:T(2,128)} dynamic-update-slice(f32[2,512,8,96]{1,0,3,2:T(2,128)} %get-tuple-element.887, f32[1,512,8,96]{1,0,3,2:T(1,128)S(1)} %copy.98, s32[]{:T(128)S(6)} %copy.123, s32[]{:T(128)} %constant.51.clone.1..sunk.2, s32[]{:T(128)} %constant.51.clone.1..sunk.2, s32[]{:T(128)} %constant.51.clone.1..sunk.2) | dynamic-update-slice | bytes 3145732 | tf_op jit(solution)/shard_map/while/body/jit(dynamic_update_index_in_dim)/dynamic_update_slice | solution.py:243
  723.9 28.8 %dynamic_update_slice.14 = f32[2,512,8,96]{1,0,3,2:T(2,128)} dynamic-update-slice(f32[2,512,8,96]{1,0,3,2:T(2,128)} %get-tuple-element.888, f32[1,512,8,96]{1,0,3,2:T(1,128)S(1)} %copy.99, s32[]{:T(128)S(6)} %copy.123, s32[]{:T(128)} %constant.51.clone.1..sunk.2, s32[]{:T(128)} %constant.51.clone.1..sunk.2, s32[]{:T(128)} %constant.51.clone.1..sunk.2) | dynamic-update-slice | bytes 3145732 | tf_op jit(solution)/shard_map/while/body/jit(dynamic_update_index_in_dim)/dynamic_update_slice | solution.py:243
  764.4 28.8 %dynamic_update_slice.13 = f32[2,512,8,96]{1,0,3,2:T(2,128)} dynamic-update-slice(f32[2,512,8,96]{1,0,3,2:T(2,128)} %get-tuple-element.887, f32[1,512,8,96]{1,0,3,2:T(1,128)S(1)} %copy.98, s32[]{:T(128)S(6)} %copy.123, s32[]{:T(128)} %constant.51.clone.1..sunk.2, s32[]{:T(128)} %constant.51.clone.1..sunk.2, s32[]{:T(128)} %constant.51.clone.1..sunk.2) | dynamic-update-slice | bytes 3145732 | tf_op jit(solution)/shard_map/while/body/jit(dynamic_update_index_in_dim)/dynamic_update_slice | solution.py:243
  798.2 28.8 %dynamic_update_slice.14 = f32[2,512,8,96]{1,0,3,2:T(2,128)} dynamic-update-slice(f32[2,512,8,96]{1,0,3,2:T(2,128)} %get-tuple-element.888, f32[1,512,8,96]{1,0,3,2:T(1,128)S(1)} %copy.99, s32[]{:T(128)S(6)} %copy.123, s32[]{:T(128)} %constant.51.clone.1..sunk.2, s32[]{:T(128)} %constant.51.clone.1..sunk.2, s32[]{:T(128)} %constant.51.clone.1..sunk.2) | dynamic-update-slice | bytes 3145732 | tf_op jit(solution)/shard_map/while/body/jit(dynamic_update_index_in_dim)/dynamic_update_slice | solution.py:243
  842.5 62.3 %reduce-scatter.6.cloned.1.call-done = f32[128,768]{0,1:T(8,128)} async-done(((f32[1024,768]{0,1:T(8,128)}), f32[128,768]{0,1:T(8,128)}) %reduce-scatter.6.cloned.1.call-update) | async-done | bytes 393232 | tf_op jit(solution)/shard_map/reduce_scatter | solution.py:262
  906.6 76.1 %reduce-scatter.8.cloned.1.call-done = f32[128,768]{0,1:T(8,128)} async-done(((f32[1024,768]{0,1:T(8,128)}), f32[128,768]{0,1:T(8,128)}) %reduce-scatter.8.cloned.1.call-update) | async-done | bytes 393232 | tf_op jit(solution)/shard_map/reduce_scatter | solution.py:263
  993.8 16.8 pad_maximum_fusion
  1012.3 25.7 %fusion.39 = f32[1536,8192]{1,0:T(8,128)} fusion(bf16[128,1536]{1,0:T(8,128)(2,1)S(1)} %copy-done.12, bf16[128,4096]{1,0:T(8,128)(2,1)S(1)} %copy-done.17, bf16[128,4096]{1,0:T(8,128)(2,1)S(1)} %copy-done.19), kind=kOutput, calls=%fused_computation.65 | convolution fusion | flops 3225419776 | bytes 52822016 | tf_op jit(solution)/shard_map/dot_general | solution.py:50
  1069.6 43.4 %all-reduce.4 = (f32[1536]{0:T(1024)S(1)}, f32[1536]{0:T(1024)S(1)}) all-reduce(f32[1536]{0:T(1024)S(1)} %get-tuple-element.438, f32[1536]{0:T(1024)S(1)} %copy-done.27), channel_id=4, replica_groups=mesh['ctx'=8,'fsdp'=4] {'ctx','fsdp'}, use_global_device_ids=true, to_apply=%region_19.20.clone | all-reduce | flops 3072 | bytes 24576
  1115.3 159.3 %reduce-scatter.10.cloned.1.call-done = f32[48,4608]{1,0:T(8,128)} async-done(((f32[1536,4608]{1,0:T(8,128)}), f32[48,4608]{1,0:T(8,128)}) %reduce-scatter.10.cloned.1.call-update) | async-done | bytes 884752 | tf_op jit(solution)/shard_map/reduce_scatter | solution.py:271
  1278.3 433.9 %reduce-scatter.12.cloned.1.call-done = f32[48,8192]{1,0:T(8,128)} async-done(((f32[1536,8192]{1,0:T(8,128)}), f32[48,8192]{1,0:T(8,128)}) %reduce-scatter.12.cloned.1.call-update) | async-done | bytes 1572880 | tf_op jit(solution)/shard_map/reduce_scatter | solution.py:203
  1714.7 248.6 %reduce-scatter.14.cloned.1.call-done = f32[128,1536]{1,0:T(8,128)} async-done(((f32[4096,1536]{1,0:T(8,128)}), f32[128,1536]{1,0:T(8,128)}) %reduce-scatter.14.cloned.1.call-update) | async-done | bytes 786448 | tf_op jit(solution)/shard_map/reduce_scatter | solution.py:193
  (235 shorter events, 220.4 us)
Async XLA Ops:
  7.2 63.7 %all-gather.10.cloned.1.call-start = ((), (), s32[]{:S(2)}) async-start(), calls=%async_computation.5 | async-start | bytes 2433024 | tf_op jit(solution)/shard_map/all_gather | solution.py:89
  7.9 122.1 %all-gather.14.cloned.1.call-start = ((), (), s32[]{:S(2)}) async-start(), calls=%async_computation.7 | async-start | bytes 2433024 | tf_op jit(solution)/shard_map/all_gather | solution.py:88
  8.7 167.2 %all-gather.12.cloned.1.call-start = ((), (), s32[]{:S(2)}) async-start(), calls=%async_computation.6 | async-start | bytes 1769472 | tf_op jit(solution)/shard_map/all_gather | solution.py:105
  52.5 80.3 %copy-start.2 = (bf16[1,128,1536]{2,1,0:T(8,128)(2,1)S(1)}, bf16[1,128,1536]{2,1,0:T(8,128)(2,1)}, u32[]{:S(2)}) copy-start(bf16[1,128,1536]{2,1,0:T(8,128)(2,1)} %param.18) | copy-start | bytes 1179652
  73.9 167.2 %all-gather.18.cloned.1.call-start = ((), (), s32[]{:S(2)}) async-start(), calls=%async_computation.9 | async-start | bytes 4866048 | tf_op jit(solution)/shard_map/all_gather | solution.py:87
  74.5 213.2 %all-gather.16.cloned.1.call-start = ((), (), s32[]{:S(2)}) async-start(), calls=%async_computation.8 | async-start | bytes 1769472 | tf_op jit(solution)/shard_map/all_gather | solution.py:104
  134.4 217.8 %all-gather.20.cloned.1.call-start = ((), (), s32[]{:S(2)}) async-start(), calls=%async_computation.10 | async-start | bytes 4866048 | tf_op jit(solution)/shard_map/all_gather | solution.py:90
  135.0 314.9 %all-gather.22.cloned.1.call-start = ((), (), s32[]{:S(2)}) async-start(), calls=%async_computation.11 | async-start | bytes 12976128 | tf_op jit(solution)/shard_map/all_gather | solution.py:177
  135.8 411.2 %all-gather.24.cloned.1.call-start = ((), (), s32[]{:S(2)}) async-start(), calls=%async_computation.12 | async-start | bytes 12976128 | tf_op jit(solution)/shard_map/all_gather | solution.py:178
  136.5 507.6 %all-gather.26.cloned.1.call-start = ((), (), s32[]{:S(2)}) async-start(), calls=%async_computation.13 | async-start | bytes 12976128 | tf_op jit(solution)/shard_map/all_gather | solution.py:179
  137.3 767.5 %reduce-scatter.6.cloned.1.call-start = ((), (), s32[]{:S(2)}) async-start(), calls=%async_computation.14 | async-start | bytes 3538944 | tf_op jit(solution)/shard_map/reduce_scatter | solution.py:262
  315.4 142.2 %copy-start.14 = (bf16[128,8,2,96]{0,3,2,1:T(8,128)(2,1)}, bf16[128,8,2,96]{0,3,2,1:T(8,128)(2,1)S(1)}, u32[]{:S(2)}) copy-start(bf16[128,8,2,96]{0,3,2,1:T(8,128)(2,1)S(1)} %convert_element_type.122) | copy-start | bytes 1179652
  355.5 319.2 %copy-start.4 = (f32[128,1536]{1,0:T(8,128)}, f32[128,1536]{1,0:T(8,128)S(1)}, u32[]{:S(2)}) copy-start(f32[128,1536]{1,0:T(8,128)S(1)} %get-tuple-element.545) | copy-start | bytes 2359300
  355.7 191.3 %copy-start.11 = (bf16[128,1536]{1,0:T(8,128)(2,1)}, bf16[128,1536]{1,0:T(8,128)(2,1)S(1)}, u32[]{:S(2)}) copy-start(bf16[128,1536]{1,0:T(8,128)(2,1)S(1)} %multiply_convert_fusion.3) | copy-start | bytes 1179652
  457.6 186.6 %copy-start.24 = (bf16[1,128,1536]{2,1,0:T(8,128)(2,1)S(1)}, bf16[1,128,1536]{2,1,0:T(8,128)(2,1)}, u32[]{:S(2)}) copy-start(bf16[1,128,1536]{2,1,0:T(8,128)(2,1)} %param.29) | copy-start | bytes 1179652
  655.3 20.6 %slice-start.3 = ((s8[4718592]{0:T(1024)(128)(4,1)}), s8[4194304]{0:T(1024)(128)(4,1)S(1)}, s32[]{:S(2)}) async-start(s8[4718592]{0:T(1024)(128)(4,1)} %bitcast.307), calls=%async_computation.22 | async-start | bytes 8388608
  664.9 11.0 slice-start.4
  831.4 151.4 %reduce-scatter.8.cloned.1.call-start = ((), (), s32[]{:S(2)}) async-start(), calls=%async_computation.15 | async-start | bytes 3538944 | tf_op jit(solution)/shard_map/reduce_scatter | solution.py:263
  836.0 438.6 %reduce-scatter.10.cloned.1.call-start = ((), (), s32[]{:S(2)}) async-start(), calls=%async_computation.16 | async-start | bytes 29196288 | tf_op jit(solution)/shard_map/reduce_scatter | solution.py:271
  837.5 147.1 %copy-start.3 = (bf16[1,128,1536]{2,1,0:T(8,128)(2,1)S(1)}, bf16[1,128,1536]{2,1,0:T(8,128)(2,1)}, u32[]{:S(2)}) copy-start(bf16[1,128,1536]{2,1,0:T(8,128)(2,1)} %param.18) | copy-start | bytes 1179652
  982.7 11.1 slice-start
  1010.7 701.5 %reduce-scatter.12.cloned.1.call-start = ((), (), s32[]{:S(2)}) async-start(), calls=%async_computation.17 | async-start | bytes 51904512 | tf_op jit(solution)/shard_map/reduce_scatter | solution.py:203
  1038.0 925.3 %reduce-scatter.14.cloned.1.call-start = ((), (), s32[]{:S(2)}) async-start(), calls=%async_computation.18 | async-start | bytes 25952256 | tf_op jit(solution)/shard_map/reduce_scatter | solution.py:193
  1066.9 47.3 %copy-start.8 = (f32[128,1536]{1,0:T(8,128)S(1)}, f32[128,1536]{1,0:T(8,128)}, u32[]{:S(2)}) copy-start(f32[128,1536]{1,0:T(8,128)} %copy-done.6) | copy-start | bytes 2359300
  (24 other events, 94.9 us)
Sparse Core Ops, SparseCore 0:
  10.9 59.9 all-gather.9
  73.8 56.1 all-gather.13
  132.7 43.0 all-gather.11
  178.6 62.4 all-gather.17
  243.6 44.0 all-gather.15
  290.5 61.7 all-gather.19
  355.1 94.7 all-gather.21
  452.8 94.2 all-gather.23
  549.9 94.2 all-gather.25
  831.5 73.2 reduce-scatter.5
  908.4 74.2 reduce-scatter.7
  1010.8 263.8 reduce-scatter.9
  1281.1 431.0 reduce-scatter.11
  1719.0 244.3 reduce-scatter.13
where the time goes:
time: 1990 us; the launch traced here: 1970 us
  waiting for transfers between devices  1500 us (75%)
  local copies, waits for them, and re-layouts  171 us (9%)
  matrix products  155 us (8%)
  blocking collectives  85.5 us (4%)
  other arithmetic  35.8 us (2%)
    reduce_scatter x1, waiting for transfers between devices, body(): lax.psum_scatter(outer_rows(piece, gate_up_cat), ('ctx', 'fsdp'), scatter...  434 us
    reduce_scatter x1, waiting for transfers between devices, body(): lax.psum_scatter(outer_rows(piece, grad_out), ('ctx', 'fsdp'), scatter_di...  249 us
    reduce_scatter x1, waiting for transfers between devices, body(): lax.psum_scatter(jnp.concatenate([outer_rows(normed_low, projection_cat),...  159 us
    dynamic_update_slice x8, local copies, waits for them, and re-layouts, body(): lax.scan(back_step, jnp.zeros((tok_rows, KVH, group_size, HD), jnp.float3...  122 us
    all_gather x1, waiting for transfers between devices, body(): lax.all_gather(gate_weight, ('ctx', 'fsdp'), axis=0, tiled=True)  94.2 us
    all_gather x1, waiting for transfers between devices, body(): lax.all_gather(up_weight, ('ctx', 'fsdp'), axis=0, tiled=True)  89.4 us
    all_gather x1, waiting for transfers between devices, body(): lax.all_gather(down_weight, ('ctx', 'fsdp'), axis=0, tiled=True)  89.4 us
    unnamed x2, blocking collectives  85.5 us
  transfers between devices with their start and end apart: 14, of which 14 were waited for; matrix products, arithmetic and copies ran while one was open for 7% of the time, Pallas kernels for 0%

commit v1 on v0

v1 whole, which is shorter than its diff:
```python
import jax
import jax.numpy as jnp
from jax import lax
from jax.sharding import PartitionSpec as P

D = 1536
H = 16
KVH = 8
HD = 96
KBLK = 512
DOC_MOST = 4096
KVW = 768
GAIN_PAD = 128

EPSILON = 1e-05
ROPE_BASE = 100000.0
MASKED_SCORE = -1e30
ALL = ("ctx", "fsdp")


def rms_scale(values):
    return lax.rsqrt(jnp.mean(values * values, axis=-1, keepdims=True) + EPSILON)


def document_layout(lengths, total):
    starts = jnp.cumsum(lengths) - lengths
    places = jnp.arange(total, dtype=jnp.int32)
    inside = places[:, None] >= starts[None, :]
    doc_ids = jnp.sum(inside.astype(jnp.int32), axis=1) - 1
    doc_starts = jnp.max(jnp.where(inside, starts[None, :], 0), axis=1)
    return (doc_ids, places - doc_starts)


def rotate(values, positions, head_count, direction):
    row_count = values.shape[0]
    half_dim = HD // 2
    inverse_freq = ROPE_BASE ** (-(jnp.arange(half_dim).astype(jnp.float32) * (2.0 / HD)))
    angles = positions.astype(jnp.float32)[:, None] * inverse_freq[None, :]
    cosine = jnp.cos(angles)[:, None, :]
    sine_part = direction * jnp.sin(angles)[:, None, :]
    grouped = values.reshape(row_count, head_count, HD)
    former = grouped[:, :, :half_dim]
    latter = grouped[:, :, half_dim:]
    turned = jnp.concatenate(
        [former * cosine - latter * sine_part, latter * cosine + former * sine_part], axis=2
    )
    return turned.reshape(row_count, head_count * HD)


def outer_rows(left, right):
    return lax.dot_general(
        left, right, (((0,), (0,)), ((), ())), preferred_element_type=jnp.float32
    )


def times_transposed(left, right):
    return lax.dot_general(
        left, right, (((1,), (1,)), ((), ())), preferred_element_type=jnp.float32
    )


def body(
    tokens,
    doc_lengths,
    attention_gain,
    query_weight,
    key_weight,
    value_weight,
    output_weight,
    feedforward_gain,
    gate_weight,
    up_weight,
    down_weight,
    cotangent,
):
    n_dev = lax.axis_size(ALL)
    rows = query_weight.shape[0]
    ff_rows = down_weight.shape[0]
    ff = gate_weight.shape[1]
    local_tokens = tokens[0].astype(jnp.float32)
    tok_rows = local_tokens.shape[0]
    stream_len = tok_rows * lax.axis_size("ctx")
    my_first = lax.axis_index("ctx") * tok_rows

    gain_cols = jnp.pad(
        jnp.stack([attention_gain, feedforward_gain], axis=1), ((0, 0), (0, GAIN_PAD - 2))
    )
    att_full = lax.all_gather(
        jnp.concatenate([query_weight, key_weight, value_weight, output_weight, gain_cols], axis=1),
        ALL,
        axis=0,
        tiled=True,
    )
    c_k = D
    c_v = D + KVW
    c_o = D + 2 * KVW
    c_g = 2 * D + 2 * KVW
    query_full = att_full[:, :c_k]
    key_full = att_full[:, c_k:c_v]
    value_full = att_full[:, c_v:c_o]
    qkv_full = att_full[:, :c_o]
    output_full = att_full[:, c_o:c_g]
    gain_one_f = att_full[:, c_g].astype(jnp.float32)
    gain_two_f = att_full[:, c_g + 1].astype(jnp.float32)

    key_docs_all, places_all = document_layout(doc_lengths[0], stream_len)
    query_docs = lax.dynamic_slice_in_dim(key_docs_all, my_first, tok_rows, 0)
    query_positions = lax.dynamic_slice_in_dim(places_all, my_first, tok_rows, 0)
    query_places = my_first + jnp.arange(tok_rows, dtype=jnp.int32)
    group_size = H // KVH
    score_scale = HD ** (-0.5)

    scale_one = rms_scale(local_tokens)
    normed_one = local_tokens * scale_one
    normed_low = (normed_one * gain_one_f).astype(jnp.bfloat16)
    qkv = jnp.dot(normed_low, qkv_full, preferred_element_type=jnp.float32)
    queries = qkv[:, :D]
    keys_new = qkv[:, D : D + KVW]
    values_new = qkv[:, D + KVW :]
    query_low = rotate(queries, query_positions, H, 1.0).astype(jnp.bfloat16)
    key_low = rotate(keys_new, query_positions, KVH, 1.0).astype(jnp.bfloat16)
    value_low = values_new.astype(jnp.bfloat16)

    ff_full = lax.all_gather(
        jnp.concatenate([gate_weight, up_weight, down_weight.reshape(rows, ff)], axis=1),
        ALL,
        axis=0,
        tiled=True,
    )
    kv_all = lax.all_gather(
        jnp.concatenate([key_low, value_low], axis=1), "ctx", axis=0, tiled=True
    )

    max_doc = min(DOC_MOST, KBLK * (stream_len // (2 * KBLK)))
    win = min(max_doc + tok_rows, stream_len)
    if win == stream_len:
        win_start = 0
        kv_win = kv_all
        key_docs = key_docs_all
        key_places = jnp.arange(stream_len, dtype=jnp.int32)
    else:
        win_start = jnp.clip(my_first + tok_rows - win, 0, stream_len - win)
        kv_win = lax.dynamic_slice_in_dim(kv_all, win_start, win, 0)
        key_docs = lax.dynamic_slice_in_dim(key_docs_all, win_start, win, 0)
        key_places = win_start + jnp.arange(win, dtype=jnp.int32)
    key_block = kv_win[:, :KVW].reshape(win, KVH, HD)
    value_block = kv_win[:, KVW:].reshape(win, KVH, HD)
    query_grouped = query_low.reshape(tok_rows, KVH, group_size, HD)
    allowed = (
        (key_docs[None, :] == query_docs[:, None]) & (key_places[None, :] <= query_places[:, None])
    )[:, None, None, :]
    scores = (
        jnp.einsum("qgrd,kgd->qgrk", query_grouped, key_block, preferred_element_type=jnp.float32)
        * score_scale
    )
    scores = jnp.where(allowed, scores, MASKED_SCORE)
    row_max = jnp.max(scores, axis=-1, keepdims=True)
    exponent = jnp.where(allowed, jnp.exp(scores - row_max), 0.0)
    probs = exponent / jnp.sum(exponent, axis=-1, keepdims=True)
    probs_low = probs.astype(jnp.bfloat16)
    attended_sum = jnp.einsum(
        "qgrk,kgd->qgrd", probs_low, value_block, preferred_element_type=jnp.float32
    )
    attended_low = attended_sum.reshape(tok_rows, D).astype(jnp.bfloat16)
    middle = local_tokens + jnp.dot(attended_low, output_full, preferred_element_type=jnp.float32)

    gate_up_full = ff_full[:, : 2 * ff]
    gate_full = ff_full[:, :ff]
    up_full = ff_full[:, ff : 2 * ff]
    down_full = ff_full[:, 2 * ff :].reshape(n_dev, rows, ff).reshape(n_dev * ff_rows, D)
    scale_two = rms_scale(middle)
    normed_two = middle * scale_two
    normed_two_low = (normed_two * gain_two_f).astype(jnp.bfloat16)
    gate_up = jnp.dot(normed_two_low, gate_up_full, preferred_element_type=jnp.float32)
    gate_pre = gate_up[:, :ff]
    up_pre = gate_up[:, ff:]
    sigmoid = jax.nn.sigmoid(gate_pre)
    hidden_low = (gate_pre * sigmoid * up_pre).astype(jnp.bfloat16)
    layer_out = middle + jnp.dot(hidden_low, down_full, preferred_element_type=jnp.float32)

    grad_out = cotangent[0]
    down_term = outer_rows(hidden_low, grad_out)
    hidden_grad = times_transposed(grad_out, down_full)
    gate_grad = (hidden_grad * up_pre * sigmoid * (1.0 + gate_pre * (1.0 - sigmoid))).astype(
        jnp.bfloat16
    )
    up_grad = (hidden_grad * gate_pre * sigmoid).astype(jnp.bfloat16)
    gate_up_cat = jnp.concatenate([gate_grad, up_grad], axis=1)
    gate_up_term = outer_rows(normed_two_low, gate_up_cat)
    ff_sum = lax.psum_scatter(
        jnp.concatenate(
            [
                gate_up_term.astype(jnp.bfloat16),
                down_term.reshape(n_dev, ff_rows, D).reshape(n_dev * rows, ff).astype(jnp.bfloat16),
            ],
            axis=1,
        ),
        ALL,
        scatter_dimension=0,
        tiled=True,
    )
    normed_two_grad = times_transposed(gate_up_cat, gate_up_full)
    gain_two_term = jnp.sum(normed_two_grad * normed_two, axis=0)
    scaled_two = normed_two_grad * gain_two_f
    middle_grad = grad_out.astype(jnp.float32) + scale_two * (
        scaled_two - normed_two * jnp.mean(scaled_two * normed_two, axis=-1, keepdims=True)
    )
    branch_grad = middle_grad.astype(jnp.bfloat16)
    attended_grad_low = (
        times_transposed(branch_grad, output_full)
        .astype(jnp.bfloat16)
        .reshape(tok_rows, KVH, group_size, HD)
    )
    row_delta = jnp.sum(
        attended_grad_low.astype(jnp.float32) * attended_sum, axis=-1, keepdims=True
    )
    prob_grad = jnp.einsum(
        "qgrd,kgd->qgrk", attended_grad_low, value_block, preferred_element_type=jnp.float32
    )
    score_grad = (probs * (prob_grad - row_delta)).astype(jnp.bfloat16)
    query_accum = jnp.einsum(
        "qgrk,kgd->qgrd", score_grad, key_block, preferred_element_type=jnp.float32
    )
    key_term = jnp.einsum(
        "qgrk,qgrd->kgd", score_grad, query_grouped, preferred_element_type=jnp.float32
    ).reshape(win, KVW)
    value_term = jnp.einsum(
        "qgrk,qgrd->kgd", probs_low, attended_grad_low, preferred_element_type=jnp.float32
    ).reshape(win, KVW)
    kv_term = jnp.concatenate([key_term, value_term], axis=1)
    if win != stream_len:
        kv_term = lax.dynamic_update_slice_in_dim(
            jnp.zeros((stream_len, 2 * KVW), jnp.float32), kv_term, win_start, 0
        )
    kv_sum = lax.psum_scatter(kv_term, "ctx", scatter_dimension=0, tiled=True)
    key_grad_low = rotate(kv_sum[:, :KVW] * score_scale, query_positions, KVH, -1.0).astype(
        jnp.bfloat16
    )
    value_grad_low = kv_sum[:, KVW:].astype(jnp.bfloat16)
    query_grad_low = rotate(
        query_accum.reshape(tok_rows, D) * score_scale, query_positions, H, -1.0
    ).astype(jnp.bfloat16)
    projection_cat = jnp.concatenate([query_grad_low, key_grad_low, value_grad_low], axis=1)
    normed_grad = times_transposed(projection_cat, qkv_full)
    gain_one_term = jnp.sum(normed_grad * normed_one, axis=0)
    scaled_one = normed_grad * gain_one_f
    tokens_grad = middle_grad + scale_one * (
        scaled_one - normed_one * jnp.mean(scaled_one * normed_one, axis=-1, keepdims=True)
    )
    gain_term_cols = jnp.pad(
        jnp.stack([gain_one_term, gain_two_term], axis=1), ((0, 0), (0, GAIN_PAD - 2))
    )
    attention_sum = lax.psum_scatter(
        jnp.concatenate(
            [
                outer_rows(normed_low, projection_cat).astype(jnp.bfloat16),
                outer_rows(attended_low, branch_grad).astype(jnp.bfloat16),
                gain_term_cols.astype(jnp.bfloat16),
            ],
            axis=1,
        ),
        ALL,
        scatter_dimension=0,
        tiled=True,
    ).astype(jnp.float32)
    ff_sum = ff_sum.astype(jnp.float32)
    return (
        layer_out.astype(jnp.bfloat16)[None],
        tokens_grad[None],
        attention_sum[:, c_g],
        attention_sum[:, :c_k],
        attention_sum[:, c_k:c_v],
        attention_sum[:, c_v:c_o],
        attention_sum[:, c_o:c_g],
        attention_sum[:, c_g + 1],
        ff_sum[:, :ff],
        ff_sum[:, ff : 2 * ff],
        ff_sum[:, 2 * ff :].reshape(ff_rows, D),
    )


def solution(mesh):
    weight = P(ALL, None)
    stream = P("fsdp", "ctx", None)
    return jax.shard_map(
        body,
        mesh=mesh,
        in_specs=(
            stream,
            P("fsdp", None),
            P(ALL),
            weight,
            weight,
            weight,
            weight,
            P(ALL),
            weight,
            weight,
            weight,
            stream,
        ),
        out_specs=(
            stream,
            stream,
            P(ALL),
            weight,
            weight,
            weight,
            weight,
            P(ALL),
            weight,
            weight,
            weight,
        ),
        check_vma=False,
    )
```

time: 1990 us -> 1200 us (0.60)
  waiting for transfers between devices: 1500 us -> 900 us
  blocking collectives: 85.5 us -> 0 us
  local copies, waits for them, and re-layouts: 171 us -> 104 us
  matrix products: 155 us -> 112 us
  other arithmetic: 35.8 us -> 58.9 us
    reduce_scatter x5 -> x3, waiting for transfers between devices: 980 us -> 543 us  [the longest x1 349 us: body(): lax.psum_scatter(jnp.concatenate([gate_up_term.astype(jnp.bfloat16), down...]
    all_gather x9 -> x3, waiting for transfers between devices: 517 us -> 357 us  [the longest x1 199 us: body(): lax.all_gather(jnp.concatenate([gate_weight, up_weight, down_weight.resha...]
    dynamic_update_slice x8 -> x1, local copies, waits for them, and re-layouts: 122 us -> 19.3 us  [body(): lax.dynamic_update_slice_in_dim(jnp.zeros((stream_len, 2 * KVW), jnp.floa...]
    unnamed x2 -> x0, blocking collectives: 85.5 us -> none
    concatenate x1 -> x5, other arithmetic: 16.8 us -> 44 us  [the longest x1 26.2 us: body(): jnp.concatenate([gate_up_term.astype(jnp.bfloat16), down_term.reshape(n_d...]
    dot_general x19 -> x7, matrix products: 51.6 us -> 27.9 us  [the longest x1 12.5 us: body(): jnp.dot(normed_two_low, gate_up_full, preferred_element_type=jnp.float32)]
    convert_element_type x0 -> x2, local copies, waits for them, and re-layouts: none -> 23.6 us  [the longest x1 23.4 us: body(): down_term.reshape(n_dev, ff_rows, D).reshape(n_dev * rows, ff)]
    another operation x0 -> x4, local copies, waits for them, and re-layouts: none -> 23.2 us  [the longest x1 22.9 us: body(): ff_full[:, 2 * ff:].reshape(n_dev, rows, ff).reshape(n_dev * ff_rows, D)]
  transfers between devices with their start and end apart: 14 -> 6, of which waited for: 14 -> 6; matrix products, arithmetic and copies ran while one was open for 7% -> 10% of each run, Pallas kernels for 0% -> 0%
where the time goes in v1:
time: 1200 us; the launch traced here: 1190 us
  waiting for transfers between devices  900 us (75%)
  matrix products  112 us (9%)
  local copies, waits for them, and re-layouts  104 us (9%)
  other arithmetic  58.9 us (5%)
  between operations  14.8 us (1%)
    reduce_scatter x1, waiting for transfers between devices, body(): lax.psum_scatter(jnp.concatenate([gate_up_term.astype(jnp.bfloat16), down...  349 us
    all_gather x1, waiting for transfers between devices, body(): lax.all_gather(jnp.concatenate([gate_weight, up_weight, down_weight.resha...  199 us
    reduce_scatter x1, waiting for transfers between devices, body(): kv_sum = lax.psum_scatter(kv_term, 'ctx', scatter_dimension=0, tiled=True)  111 us
    all_gather x1, waiting for transfers between devices, body(): lax.all_gather(jnp.concatenate([query_weight, key_weight, value_weight, o...  105 us
    reduce_scatter x1, waiting for transfers between devices, body(): lax.psum_scatter(jnp.concatenate([outer_rows(normed_low, projection_cat)....  83.2 us
    all_gather x1, waiting for transfers between devices, body(): lax.all_gather(jnp.concatenate([key_low, value_low], axis=1), 'ctx', axis...  54 us
    dot_general x4, matrix products, times_transposed(): lax.dot_general(left, right, (((1,), (1,)), ((), ())), preferred_element_...  35.8 us
    dot_general x4, matrix products, outer_rows(): lax.dot_general(left, right, (((0,), (0,)), ((), ())), preferred_element_...  32.2 us
  transfers between devices with their start and end apart: 6, of which 6 were waited for; matrix products, arithmetic and copies ran while one was open for 10% of the time, Pallas kernels for 0%

profile of v1, /device:TPU:0, one launch (start us, length us, event | category | flops | bytes accessed | tf_op | source)
XLA Modules:
  0.0 1190.6 jit_solution(18242834477617427819)
XLA Ops:
  15.5 104.7 %all-gather.4.cloned.1.call-done = bf16[1536,4736]{1,0:T(8,128)(2,1)} async-done(((bf16[48,4736]{1,0:T(8,128)(2,1)}), bf16[1536,4736]{1,0:T(8,128)(2,1)}) %all-gather.4.cloned.1.call-update) | async-done | bytes 14549008 | tf_op jit(solution)/shard_map/all_gather | solution.py:88
  121.9 5.3 fusion.9
  133.3 54.0 %all-gather.6.cloned.1.call-done = bf16[1024,1536]{1,0:T(8,128)(2,1)} async-done(((bf16[128,1536]{1,0:T(8,128)(2,1)}), bf16[1024,1536]{1,0:T(8,128)(2,1)}) %all-gather.6.cloned.1.call-update) | async-done | bytes 3145744 | tf_op jit(solution)/shard_map/all_gather | solution.py:130
  190.8 4.4 fusion.59
  200.9 4.2 multiply_reduce_fusion.3
  205.1 198.7 %all-gather.8.cloned.1.call-done = bf16[1536,12288]{1,0:T(8,128)(2,1)} async-done(((bf16[48,12288]{1,0:T(8,128)(2,1)}), bf16[1536,12288]{1,0:T(8,128)(2,1)}) %all-gather.8.cloned.1.call-update) | async-done | bytes 37748752 | tf_op jit(solution)/shard_map/all_gather | solution.py:124
  403.8 10.7 slice.144
  414.5 22.9 %reshape_reshape.4 = bf16[4096,1536]{1,0:T(8,128)(2,1)} reshape(bf16[1536,4096]{1,0:T(8,128)(2,1)} %slice.144) | data formatting | bytes 25165824 | tf_op jit(solution)/shard_map/reshape;reshape | solution.py:170
  437.4 12.5 %fusion.4 = f32[128,8192]{1,0:T(8,128)} fusion(bf16[1536,12288]{1,0:T(8,128)(2,1)} %all-gather.8.cloned.1.call-done, f32[128,1536]{1,0:T(8,128)} %get-tuple-element.49, f32[1536]{0:T(1024)S(1)} %get-tuple-element.11, f32[128]{0:T(128)S(1)} %add_rsqrt_fusion), kind=kOutput, calls=%fused_computation.7 | convolution fusion | flops 3221815296 | bytes 30153216 | tf_op jit(solution)/shard_map/dot_general | solution.py:174
  450.8 8.2 multiply_convert_fusion.1
  459.0 15.1 %multiply_reduce_fusion = (bf16[1536]{0:T(1024)(128)(2,1)S(1)}, f32[128]{0:T(128)S(1)}, f32[128,1536]{1,0:T(8,128)}) fusion(f32[128,1536]{1,0:T(8,128)} %get-tuple-element.49, f32[128]{0:T(128)S(1)} %add_rsqrt_fusion, f32[1536]{0:T(1024)S(1)} %get-tuple-element.11, bf16[1536,12288]{1,0:T(8,128)(2,1)} %all-gather.8.cloned.1.call-done, ...), kind=kOutput, calls=%fused_computation.64 | convolution fusion | flops 3226597888 | bytes 28846080 | tf_op jit(solution)/shard_map/dot_general | solution.py:57
  476.7 4.7 fusion.24
  495.5 19.3 %dynamic_update_slice.3 = f32[1024,1536]{0,1:T(8,128)} dynamic-update-slice(f32[1024,1536]{0,1:T(8,128)} %broadcast_in_dim.39, f32[640,1536]{0,1:T(8,128)} %pad_maximum_fusion.1, s32[]{:T(128)S(6)} %min.4, s32[]{:T(128)} %constant.16.clone.1) | dynamic-update-slice | bytes 7864324 | tf_op jit(solution)/shard_map/dynamic_update_slice | solution.py:232
  520.4 110.9 %reduce-scatter.4.cloned.1.call-done = f32[128,1536]{0,1:T(8,128)} async-done(((f32[1024,1536]{0,1:T(8,128)}), f32[128,1536]{0,1:T(8,128)}) %reduce-scatter.4.cloned.1.call-update) | async-done | bytes 786448 | tf_op jit(solution)/shard_map/reduce_scatter | solution.py:235
  633.5 7.3 convolution_convert_fusion.2
  640.9 7.8 fusion.40
  649.0 12.8 %fusion.6 = bf16[1536,4736]{1,0:T(8,128)(2,1)} fusion(bf16[1536,2]{1,0:T(8,128)(2,1)S(1)} %copy.81, bf16[1536,1536]{1,0:T(8,128)(2,1)} %convolution_convert_fusion.3, bf16[1536,3072]{1,0:T(8,128)(2,1)} %convolution_convert_fusion.2), kind=kLoop, calls=%fused_computation.10 | loop fusion | flops 58195968 | bytes 28710912 | tf_op jit(solution)/shard_map/concatenate | solution.py:254
  663.1 6.6 convolution_convert_fusion.1
  669.7 23.4 %convert_element_type.164 = bf16[1536,4096]{1,0:T(8,128)(2,1)} reshape(bf16[4096,1536]{1,0:T(8,128)(2,1)} %convolution_convert_fusion.1) | data formatting | bytes 25165824 | tf_op jit(solution)/shard_map/convert_element_type | solution.py:194
  693.2 14.7 %convolution_convert_fusion = bf16[1536,8192]{1,0:T(8,128)(2,1)} fusion(bf16[128,4096]{1,0:T(8,128)(2,1)} %get-tuple-element.22, bf16[128,4096]{1,0:T(8,128)(2,1)} %get-tuple-element.21, f32[128,1536]{1,0:T(8,128)S(1)} %copy-done.4, f32[1536]{0:T(1024)S(1)} %get-tuple-element.11, f32[128]{0:T(128)S(1)} %add_rsqrt_fusion), kind=kOutput, calls=%fused_computation.2 | convolution fusion | flops 3238592512 | bytes 28056064 | tf_op jit(solution)/shard_map/dot_general | solution.py:51
  707.9 26.2 %pad_maximum_fusion = bf16[1536,12288]{1,0:T(8,128)(2,1)} fusion(bf16[1536,4096]{1,0:T(8,128)(2,1)} %convert_element_type.164, bf16[1536,8192]{1,0:T(8,128)(2,1)} %convolution_convert_fusion), kind=kLoop, calls=%fused_computation.1 | loop fusion | flops 75497472 | bytes 75497472 | tf_op jit(solution)/shard_map/concatenate | solution.py:191
  734.2 7.4 fusion.28
  742.8 83.2 %reduce-scatter.6.cloned.1.call-done = bf16[48,4736]{1,0:T(8,128)(2,1)} async-done(((bf16[1536,4736]{1,0:T(8,128)(2,1)}), bf16[48,4736]{1,0:T(8,128)(2,1)}) %reduce-scatter.6.cloned.1.call-update) | async-done | bytes 454672 | tf_op jit(solution)/shard_map/reduce_scatter | solution.py:253
  831.3 348.7 %reduce-scatter.8.cloned.1.call-done = bf16[48,12288]{1,0:T(8,128)(2,1)} async-done(((bf16[1536,12288]{1,0:T(8,128)(2,1)}), bf16[48,12288]{1,0:T(8,128)(2,1)}) %reduce-scatter.8.cloned.1.call-update) | async-done | bytes 1179664 | tf_op jit(solution)/shard_map/reduce_scatter | solution.py:190
  (130 shorter events, 62.0 us)
Async XLA Ops:
  7.2 113.1 %all-gather.4.cloned.1.call-start = ((), (), s32[]{:S(2)}) async-start(), calls=%async_computation.3 | async-start | bytes 15003648 | tf_op jit(solution)/shard_map/all_gather | solution.py:88
  12.5 174.8 %all-gather.6.cloned.1.call-start = ((), (), s32[]{:S(2)}) async-start(), calls=%async_computation.4 | async-start | bytes 3538944 | tf_op jit(solution)/shard_map/all_gather | solution.py:130
  127.2 2.8 copy-start.23
  128.5 275.3 %all-gather.8.cloned.1.call-start = ((), (), s32[]{:S(2)}) async-start(), calls=%async_computation.5 | async-start | bytes 38928384 | tf_op jit(solution)/shard_map/all_gather | solution.py:124
  132.1 499.3 %reduce-scatter.4.cloned.1.call-start = ((), (), s32[]{:S(2)}) async-start(), calls=%async_computation.6 | async-start | bytes 7077888 | tf_op jit(solution)/shard_map/reduce_scatter | solution.py:235
  133.2 62.0 %copy-start.17 = (bf16[128,16,96]{0,2,1:T(8,128)(2,1)}, bf16[128,16,96]{0,2,1:T(8,128)(2,1)S(1)}, u32[]{:S(2)}) copy-start(bf16[128,16,96]{0,2,1:T(8,128)(2,1)S(1)} %pad_maximum_fusion.8) | copy-start | bytes 1179652
  190.1 9.0 copy-start.10
  190.8 4.5 copy-start.12
  195.2 5.6 copy-start.8
  199.1 5.9 copy-start.1
  200.9 4.2 copy-start.15
  437.4 13.5 %copy-start = (bf16[4096,1536]{1,0:T(8,128)(2,1)S(1)}, bf16[4096,1536]{1,0:T(8,128)(2,1)}, u32[]{:S(2)}) copy-start(bf16[4096,1536]{1,0:T(8,128)(2,1)} %reshape_reshape.4) | copy-start | bytes 37748740
  437.4 13.5 %copy-start.19 = (bf16[1,128,1536]{2,1,0:T(8,128)(2,1)S(1)}, bf16[1,128,1536]{2,1,0:T(8,128)(2,1)}, u32[]{:S(2)}) copy-start(bf16[1,128,1536]{2,1,0:T(8,128)(2,1)} %param.23) | copy-start | bytes 1179652
  459.0 15.1 %copy-start.4 = (f32[128,1536]{1,0:T(8,128)S(1)}, f32[128,1536]{1,0:T(8,128)}, u32[]{:S(2)}) copy-start(f32[128,1536]{1,0:T(8,128)} %get-tuple-element.49) | copy-start | bytes 2359300
  474.1 9.2 copy-start.2
  483.3 2.2 copy-start.11
  485.5 3.6 copy-start.18
  514.8 311.2 %reduce-scatter.6.cloned.1.call-start = ((), (), s32[]{:S(2)}) async-start(), calls=%async_computation.7 | async-start | bytes 15003648 | tf_op jit(solution)/shard_map/reduce_scatter | solution.py:253
  514.8 2.1 copy-start.6
  514.9 2.1 copy-start.16
  516.9 116.6 %copy-start.9 = (bf16[1,128,1536]{2,1,0:T(8,128)(2,1)S(1)}, bf16[1,128,1536]{2,1,0:T(8,128)(2,1)}, u32[]{:S(2)}) copy-start(bf16[1,128,1536]{2,1,0:T(8,128)(2,1)} %param.12) | copy-start | bytes 1179652
  661.8 518.1 %reduce-scatter.8.cloned.1.call-start = ((), (), s32[]{:S(2)}) async-start(), calls=%async_computation.8 | async-start | bytes 38928384 | tf_op jit(solution)/shard_map/reduce_scatter | solution.py:190
  734.2 7.5 copy-start.7
  734.2 7.4 copy-start.22
  (6 other events, 8.3 us)
Sparse Core Ops, SparseCore 0:
  12.6 107.6 all-gather.3
  128.6 58.5 all-gather.5
  190.1 213.5 all-gather.7
  514.9 116.4 reduce-scatter.3
  661.9 163.9 reduce-scatter.5
  832.3 347.6 reduce-scatter.7

commit v2 on v1

--- a/solution.py
+++ b/solution.py
@@ -1,7 +1,13 @@
+import functools
+
 import jax
 import jax.numpy as jnp
 from jax import lax
+from jax.experimental import pallas as pl
+from jax.experimental.pallas import tpu as pltpu
 from jax.sharding import PartitionSpec as P
+
+MESH = pl.DeviceIdType.MESH
 
 D = 1536
 H = 16
@@ -57,6 +63,115 @@
     return lax.dot_general(
         left, right, (((1,), (1,)), ((), ())), preferred_element_type=jnp.float32
     )
+
+
+def neighbour_barrier(n_ctx, back, c, f):
+    barrier = pltpu.get_barrier_semaphore()
+    for s in range(1, back + 1):
+        for peer in ((c + s) % n_ctx, (c + n_ctx - s) % n_ctx):
+            pl.semaphore_signal(barrier, inc=1, device_id=(peer, f), device_id_type=MESH)
+    pl.semaphore_wait(barrier, 2 * back)
+
+
+def kv_share_kernel(n_ctx, back, kv_ref, out_ref, send_sem, recv_sem):
+    c = lax.axis_index("ctx")
+    f = lax.axis_index("fsdp")
+    neighbour_barrier(n_ctx, back, c, f)
+
+    def copy(s, dest):
+        return pltpu.make_async_remote_copy(
+            src_ref=kv_ref,
+            dst_ref=out_ref.at[back - s],
+            send_sem=send_sem.at[s - 1],
+            recv_sem=recv_sem.at[back - s],
+            device_id=(dest, f),
+            device_id_type=MESH,
+        )
+
+    for s in range(1, back + 1):
+
+        @pl.when(c + s < n_ctx)
+        def _():
+            copy(s, c + s).start()
+
+    out_ref[back] = kv_ref[...]
+    for s in range(1, back + 1):
+
+        @pl.when(c - s < 0)
+        def _():
+            out_ref[back - s] = jnp.zeros(kv_ref.shape, kv_ref.dtype)
+
+    for s in range(1, back + 1):
+
+        @pl.when(c + s < n_ctx)
+        def _():
+            copy(s, c + s).wait_send()
+
+        @pl.when(c - s >= 0)
+        def _():
+            copy(s, c).wait_recv()
+
+
+def kv_share(kv, n_ctx, back):
+    return pl.pallas_call(
+        functools.partial(kv_share_kernel, n_ctx, back),
+        out_shape=jax.ShapeDtypeStruct((back + 1,) + kv.shape, kv.dtype),
+        in_specs=[pl.BlockSpec(memory_space=pltpu.VMEM)],
+        out_specs=pl.BlockSpec(memory_space=pltpu.VMEM),
+        scratch_shapes=[pltpu.SemaphoreType.DMA((back,)), pltpu.SemaphoreType.DMA((back + 1,))],
+        compiler_params=pltpu.CompilerParams(collective_id=0, has_side_effects=True),
+    )(kv)
+
+
+def kv_return_kernel(n_ctx, back, g_ref, out_ref, recv_buf, send_sem, recv_sem):
+    c = lax.axis_index("ctx")
+    f = lax.axis_index("fsdp")
+    neighbour_barrier(n_ctx, back, c, f)
+
+    def copy(s, dest):
+        return pltpu.make_async_remote_copy(
+            src_ref=g_ref.at[back - s],
+            dst_ref=recv_buf.at[s - 1],
+            send_sem=send_sem.at[s - 1],
+            recv_sem=recv_sem.at[s - 1],
+            device_id=(dest, f),
+            device_id_type=MESH,
+        )
+
+    for s in range(1, back + 1):
+
+        @pl.when(c - s >= 0)
+        def _():
+            copy(s, c - s).start()
+
+    out_ref[...] = g_ref[back]
+    for s in range(1, back + 1):
+
+        @pl.when(c + s < n_ctx)
+        def _():
+            copy(s, c).wait_recv()
+            out_ref[...] += recv_buf[s - 1]
+
+    for s in range(1, back + 1):
+
+        @pl.when(c - s >= 0)
+        def _():
+            copy(s, c - s).wait_send()
+
+
+def kv_return(g, n_ctx, back):
+    return pl.pallas_call(
+        functools.partial(kv_return_kernel, n_ctx, back),
+        out_shape=jax.ShapeDtypeStruct(g.shape[1:], g.dtype),
+        in_specs=[pl.BlockSpec(memory_space=pltpu.VMEM)],
+        out_specs=pl.BlockSpec(memory_space=pltpu.VMEM),
+        scratch_shapes=[
+            pltpu.VMEM((back,) + g.shape[1:], g.dtype),
+            pltpu.SemaphoreType.DMA((back,)),
+            pltpu.SemaphoreType.DMA((back,)),
+        ],
+        compiler_params=pltpu.CompilerParams(collective_id=1, has_side_effects=True),
+    )(g)
 
 
 def body(
@@ -127,22 +242,18 @@
         axis=0,
         tiled=True,
     )
-    kv_all = lax.all_gather(
-        jnp.concatenate([key_low, value_low], axis=1), "ctx", axis=0, tiled=True
-    )
-
+    n_ctx = lax.axis_size("ctx")
     max_doc = min(DOC_MOST, KBLK * (stream_len // (2 * KBLK)))
-    win = min(max_doc + tok_rows, stream_len)
-    if win == stream_len:
-        win_start = 0
-        kv_win = kv_all
-        key_docs = key_docs_all
-        key_places = jnp.arange(stream_len, dtype=jnp.int32)
-    else:
-        win_start = jnp.clip(my_first + tok_rows - win, 0, stream_len - win)
-        kv_win = lax.dynamic_slice_in_dim(kv_all, win_start, win, 0)
-        key_docs = lax.dynamic_slice_in_dim(key_docs_all, win_start, win, 0)
-        key_places = win_start + jnp.arange(win, dtype=jnp.int32)
+    back = min(-(-(max_doc - 1) // tok_rows), n_ctx - 1)
+    win = (back + 1) * tok_rows
+    kv_win = kv_share(
+        jnp.concatenate([key_low, value_low], axis=1), n_ctx, back
+    ).reshape(win, 2 * KVW)
+    docs_pad = jnp.concatenate(
+        [jnp.full((back * tok_rows,), -1, jnp.int32), key_docs_all.astype(jnp.int32)]
+    )
+    key_docs = lax.dynamic_slice_in_dim(docs_pad, my_first, win, 0)
+    key_places = my_first - back * tok_rows + jnp.arange(win, dtype=jnp.int32)
     key_block = kv_win[:, :KVW].reshape(win, KVH, HD)
     value_block = kv_win[:, KVW:].reshape(win, KVH, HD)
     query_grouped = query_low.reshape(tok_rows, KVH, group_size, HD)
@@ -187,18 +298,15 @@
     up_grad = (hidden_grad * gate_pre * sigmoid).astype(jnp.bfloat16)
     gate_up_cat = jnp.concatenate([gate_grad, up_grad], axis=1)
     gate_up_term = outer_rows(normed_two_low, gate_up_cat)
-    ff_sum = lax.psum_scatter(
-        jnp.concatenate(
-            [
-                gate_up_term.astype(jnp.bfloat16),
-                down_term.reshape(n_dev, ff_rows, D).reshape(n_dev * rows, ff).astype(jnp.bfloat16),
-            ],
-            axis=1,
-        ),
-        ALL,
-        scatter_dimension=0,
-        tiled=True,
-    )
+    ff_pack = jnp.concatenate(
+        [
+            gate_up_term.astype(jnp.bfloat16),
+            down_term.reshape(n_dev, ff_rows, D).reshape(n_dev * rows, ff).astype(jnp.bfloat16),
+        ],
+        axis=1,
+    )
+    ff_pack, gate_up_cat = lax.optimization_barrier((ff_pack, gate_up_cat))
+    ff_sum = lax.psum_scatter(ff_pack, ALL, scatter_dimension=0, tiled=True)
     normed_two_grad = times_transposed(gate_up_cat, gate_up_full)
     gain_two_term = jnp.sum(normed_two_grad * normed_two, axis=0)
     scaled_two = normed_two_grad * gain_two_f
@@ -227,12 +335,11 @@
     value_term = jnp.einsum(
         "qgrk,qgrd->kgd", probs_low, attended_grad_low, preferred_element_type=jnp.float32
     ).reshape(win, KVW)
-    kv_term = jnp.concatenate([key_term, value_term], axis=1)
-    if win != stream_len:
-        kv_term = lax.dynamic_update_slice_in_dim(
-            jnp.zeros((stream_len, 2 * KVW), jnp.float32), kv_term, win_start, 0
-        )
-    kv_sum = lax.psum_scatter(kv_term, "ctx", scatter_dimension=0, tiled=True)
+    kv_sum = kv_return(
+        jnp.concatenate([key_term, value_term], axis=1).reshape(back + 1, tok_rows, 2 * KVW),
+        n_ctx,
+        back,
+    )
     key_grad_low = rotate(kv_sum[:, :KVW] * score_scale, query_positions, KVH, -1.0).astype(
         jnp.bfloat16
     )
@@ -250,6 +357,7 @@
     gain_term_cols = jnp.pad(
         jnp.stack([gain_one_term, gain_two_term], axis=1), ((0, 0), (0, GAIN_PAD - 2))
     )
+    gain_term_cols = gain_term_cols.at[0, GAIN_PAD - 1].set(ff_sum[0, 0].astype(jnp.float32) * 0.0)
     attention_sum = lax.psum_scatter(
         jnp.concatenate(
             [

time: 1200 us -> 1140 us (0.950)
  waiting for transfers between devices: 900 us -> 569 us
  Pallas kernels: 0 us -> 265 us
    reduce_scatter x2 -> x1, waiting for transfers between devices: 460 us -> 140 us  [body(): ff_sum = lax.psum_scatter(ff_pack, ALL, scatter_dimension=0, tiled=True)]
    pallas_call x0 -> x2, Pallas kernels: none -> 265 us  [the longest x1 211 us: kv_return(): pl.pallas_call(functools.partial(kv_return_kernel, n_ctx, back), out_shap...]
    reduce_scatter x1, waiting for transfers between devices: 83.2 us -> 152 us  [body(): lax.psum_scatter(jnp.concatenate([outer_rows(normed_low, projection_cat)....]
    all_gather x1 -> x0, waiting for transfers between devices: 54 us -> none  [body(): lax.all_gather(jnp.concatenate([key_low, value_low], axis=1), 'ctx', axis...]
    all_gather x1, waiting for transfers between devices: 199 us -> 175 us  [body(): lax.all_gather(jnp.concatenate([gate_weight, up_weight, down_weight.resha...]
    dynamic_update_slice x1 -> x0, local copies, waits for them, and re-layouts: 19.3 us -> none  [body(): lax.dynamic_update_slice_in_dim(jnp.zeros((stream_len, 2 * KVW), jnp.floa...]
  transfers between devices with their start and end apart: 6 -> 4, of which waited for: 6 -> 4; matrix products, arithmetic and copies ran while one was open for 10% -> 12% of each run, Pallas kernels for 0% -> 23%
where the time goes in v2:
time: 1140 us
  waiting for transfers between devices  569 us (50%)
  Pallas kernels  265 us (23%)
  matrix products  118 us (10%)
  local copies, waits for them, and re-layouts  102 us (9%)
  other arithmetic  65 us (6%)
  between operations  16.5 us (1%)
    pallas_call x1, Pallas kernels, kv_return(): pl.pallas_call(functools.partial(kv_return_kernel, n_ctx, back), out_shap...  211 us
    all_gather x1, waiting for transfers between devices, body(): lax.all_gather(jnp.concatenate([gate_weight, up_weight, down_weight.resha...  175 us
    reduce_scatter x1, waiting for transfers between devices, body(): lax.psum_scatter(jnp.concatenate([outer_rows(normed_low, projection_cat)....  152 us
    reduce_scatter x1, waiting for transfers between devices, body(): ff_sum = lax.psum_scatter(ff_pack, ALL, scatter_dimension=0, tiled=True)  140 us
    all_gather x1, waiting for transfers between devices, body(): lax.all_gather(jnp.concatenate([query_weight, key_weight, value_weight, o...  103 us
    pallas_call x1, Pallas kernels, kv_share(): pl.pallas_call(functools.partial(kv_share_kernel, n_ctx, back), out_shape...  54.1 us
    dot_general x4, matrix products, times_transposed(): lax.dot_general(left, right, (((1,), (1,)), ((), ())), preferred_element_...  39.1 us
    dot_general x4, matrix products, outer_rows(): lax.dot_general(left, right, (((0,), (0,)), ((), ())), preferred_element_...  30.8 us
  transfers between devices with their start and end apart: 4, of which 4 were waited for; matrix products, arithmetic and copies ran while one was open for 12% of the time, Pallas kernels for 23%

profile of v2, /device:TPU:0, one launch (start us, length us, event | category | flops | bytes accessed | tf_op | source)
XLA Modules:
  0.0 1136.3 jit_solution(9940216949184199972)
XLA Ops:
  17.5 102.8 %all-gather.3.cloned.1.call-done = bf16[1536,4736]{1,0:T(8,128)(2,1)} async-done(((bf16[48,4736]{1,0:T(8,128)(2,1)}), bf16[1536,4736]{1,0:T(8,128)(2,1)}) %all-gather.3.cloned.1.call-update) | async-done | bytes 14549008 | tf_op jit(solution)/shard_map/all_gather | solution.py:203
  122.0 5.2 fusion.7
  129.4 54.1 %shard_map.203 = bf16[5,128,1536]{2,1,0:T(8,128)(2,1)} custom-call(bf16[128,1536]{1,0:T(8,128)(2,1)} %pad_maximum_fusion.6.kv_ref), custom_call_target="tpu_custom_call" | custom-call | tf_op jit(solution)/shard_map/pallas_call | solution.py:116
  188.4 4.5 fusion.57
  202.0 174.9 %all-gather.5.cloned.1.call-done = bf16[1536,12288]{1,0:T(8,128)(2,1)} async-done(((bf16[48,12288]{1,0:T(8,128)(2,1)}), bf16[1536,12288]{1,0:T(8,128)(2,1)}) %all-gather.5.cloned.1.call-update) | async-done | bytes 37748752 | tf_op jit(solution)/shard_map/all_gather | solution.py:239
  376.9 10.6 slice.174
  387.4 22.9 %reshape_reshape.4 = bf16[4096,1536]{1,0:T(8,128)(2,1)} reshape(bf16[1536,4096]{1,0:T(8,128)(2,1)} %slice.174) | data formatting | bytes 25165824 | tf_op jit(solution)/shard_map/reshape;reshape | solution.py:281
  410.3 12.6 %fusion.3 = f32[128,8192]{1,0:T(8,128)} fusion(bf16[1536,12288]{1,0:T(8,128)(2,1)} %all-gather.5.cloned.1.call-done, f32[128,1536]{1,0:T(8,128)} %get-tuple-element.67, f32[1536]{0:T(1024)S(1)} %get-tuple-element.27, f32[128]{0:T(128)S(1)} %add_rsqrt_fusion), kind=kOutput, calls=%fused_computation.5 | convolution fusion | flops 3221815296 | bytes 30153216 | tf_op jit(solution)/shard_map/dot_general | solution.py:285
  423.8 8.1 multiply_convert_fusion.1
  432.0 13.8 %convolution_convert_fusion = bf16[1536,8192]{1,0:T(8,128)(2,1)} fusion(f32[128,1536]{1,0:T(8,128)} %get-tuple-element.67, f32[1536]{0:T(1024)S(1)} %get-tuple-element.27, f32[128]{0:T(128)S(1)} %add_rsqrt_fusion, bf16[128,4096]{1,0:T(8,128)(2,1)} %get-tuple-element.38, bf16[128,4096]{1,0:T(8,128)(2,1)} %get-tuple-element.37), kind=kOutput, calls=%fused_computation.2 | convolution fusion | flops 3238592512 | bytes 28056064 | tf_op jit(solution)/shard_map/dot_general | solution.py:57
  447.4 6.3 convolution_convert_fusion.1
  453.6 23.0 %convert_element_type.161 = bf16[1536,4096]{1,0:T(8,128)(2,1)} reshape(bf16[4096,1536]{1,0:T(8,128)(2,1)} %convolution_convert_fusion.1) | data formatting | bytes 25165824 | tf_op jit(solution)/shard_map/convert_element_type | solution.py:304
  476.6 25.5 %pad_maximum_fusion = bf16[1536,12288]{1,0:T(8,128)(2,1)} fusion(bf16[1536,4096]{1,0:T(8,128)(2,1)} %convert_element_type.161, bf16[1536,8192]{1,0:T(8,128)(2,1)} %convolution_convert_fusion), kind=kLoop, calls=%fused_computation.1 | loop fusion | flops 75497472 | bytes 75497472 | tf_op jit(solution)/shard_map/concatenate | solution.py:301
  504.0 17.1 %multiply_reduce_fusion = (bf16[1536]{0:T(1024)(128)(2,1)S(1)}, f32[128]{0:T(128)S(1)}, f32[128,1536]{1,0:T(8,128)}) fusion(f32[128,1536]{1,0:T(8,128)S(1)} %copy-done.5, f32[128]{0:T(128)S(1)} %add_rsqrt_fusion, f32[1536]{0:T(1024)S(1)} %get-tuple-element.27, bf16[128,8192]{1,0:T(8,128)(2,1)S(1)} %copy-done.18, ...), kind=kOutput, calls=%fused_computation.64 | convolution fusion | flops 3222403584 | bytes 28846080 | tf_op jit(solution)/shard_map/dot_general | solution.py:63
  523.5 5.6 fusion.22
  540.4 5.0 fusion.10
  554.9 5.1 pad_maximum_fusion.2.g_ref
  560.0 210.7 %shard_map.204 = f32[128,1536]{1,0:T(8,128)} custom-call(f32[5,128,1536]{2,1,0:T(8,128)} %pad_maximum_fusion.2.g_ref), custom_call_target="tpu_custom_call" | custom-call | tf_op jit(solution)/shard_map/pallas_call | solution.py:163
  781.1 8.3 fusion.38
  795.3 7.2 convolution_convert_fusion.2
  802.5 140.0 %reduce-scatter.3.cloned.1.call-done = bf16[48,12288]{1,0:T(8,128)(2,1)} async-done(((bf16[1536,12288]{1,0:T(8,128)(2,1)}), bf16[48,12288]{1,0:T(8,128)(2,1)}) %reduce-scatter.3.cloned.1.call-update) | async-done | bytes 1179664 | tf_op jit(solution)/shard_map/reduce_scatter | solution.py:309
  947.1 13.0 %pad_maximum_fusion.1 = bf16[1536,4736]{1,0:T(8,128)(2,1)} fusion(bf16[1536,128]{1,0:T(8,128)(2,1)S(1)} %scatter.4, bf16[1536,1536]{1,0:T(8,128)(2,1)} %convolution_convert_fusion.3, bf16[1536,3072]{1,0:T(8,128)(2,1)} %convolution_convert_fusion.2), kind=kLoop, calls=%fused_computation.8 | loop fusion | flops 43646976 | bytes 29097984 | tf_op jit(solution)/shard_map/concatenate | solution.py:362
  962.5 7.8 fusion.26
  972.7 151.5 %reduce-scatter.5.cloned.1.call-done = bf16[48,4736]{1,0:T(8,128)(2,1)} async-done(((bf16[1536,4736]{1,0:T(8,128)(2,1)}), bf16[48,4736]{1,0:T(8,128)(2,1)}) %reduce-scatter.5.cloned.1.call-update) | async-done | bytes 454672 | tf_op jit(solution)/shard_map/reduce_scatter | solution.py:361
  (150 shorter events, 84.4 us)
Async XLA Ops:
  7.2 9.2 copy-start.28
  7.2 9.7 copy-start.9
  7.2 113.1 %all-gather.3.cloned.1.call-start = ((), (), s32[]{:S(2)}) async-start(), calls=%async_computation.2 | async-start | bytes 15003648 | tf_op jit(solution)/shard_map/all_gather | solution.py:203
  12.5 364.4 %all-gather.5.cloned.1.call-start = ((), (), s32[]{:S(2)}) async-start(), calls=%async_computation.3 | async-start | bytes 38928384 | tf_op jit(solution)/shard_map/all_gather | solution.py:239
  16.3 926.2 %reduce-scatter.3.cloned.1.call-start = ((), (), s32[]{:S(2)}) async-start(), calls=%async_computation.4 | async-start | bytes 38928384 | tf_op jit(solution)/shard_map/reduce_scatter | solution.py:309
  185.8 10.3 copy-start.14
  186.5 6.5 copy-start.15
  188.4 4.5 copy-start.19
  196.0 5.9 copy-start.1
  197.8 4.2 copy-start.16
  410.3 13.5 %copy-start = (bf16[4096,1536]{1,0:T(8,128)(2,1)S(1)}, bf16[4096,1536]{1,0:T(8,128)(2,1)}, u32[]{:S(2)}) copy-start(bf16[4096,1536]{1,0:T(8,128)(2,1)} %reshape_reshape.4) | copy-start | bytes 37748740
  410.3 13.5 %copy-start.21 = (bf16[1,128,1536]{2,1,0:T(8,128)(2,1)S(1)}, bf16[1,128,1536]{2,1,0:T(8,128)(2,1)}, u32[]{:S(2)}) copy-start(bf16[1,128,1536]{2,1,0:T(8,128)(2,1)} %param.25) | copy-start | bytes 1179652
  432.0 13.8 %copy-start.12 = (bf16[128,4096]{1,0:T(8,128)(2,1)S(1)}, bf16[128,4096]{1,0:T(8,128)(2,1)}, u32[]{:S(2)}) copy-start(bf16[128,4096]{1,0:T(8,128)(2,1)} %get-tuple-element.37) | copy-start | bytes 3145732
  432.0 13.8 %copy-start.13 = (bf16[128,4096]{1,0:T(8,128)(2,1)S(1)}, bf16[128,4096]{1,0:T(8,128)(2,1)}, u32[]{:S(2)}) copy-start(bf16[128,4096]{1,0:T(8,128)(2,1)} %get-tuple-element.38) | copy-start | bytes 3145732
  502.2 622.0 %reduce-scatter.5.cloned.1.call-start = ((), (), s32[]{:S(2)}) async-start(), calls=%async_computation.5 | async-start | bytes 15003648 | tf_op jit(solution)/shard_map/reduce_scatter | solution.py:361
  504.0 17.1 %copy-start.22 = (bf16[1,128,1536]{2,1,0:T(8,128)(2,1)S(1)}, bf16[1,128,1536]{2,1,0:T(8,128)(2,1)}, u32[]{:S(2)}) copy-start(bf16[1,128,1536]{2,1,0:T(8,128)(2,1)} %param.25) | copy-start | bytes 1179652
  523.5 7.5 copy-start.2
  540.4 5.0 copy-start.20
  779.0 10.4 copy-start.26
  781.1 10.7 copy-start.7
  781.1 10.6 copy-start.17
  791.8 3.6 copy-start.11
  791.8 3.6 copy-start.25
  962.5 7.8 copy-start.8
  (10 other events, 19.7 us)
Sparse Core Ops, SparseCore 0:
  12.6 107.6 all-gather.2
  123.2 253.6 all-gather.4
  502.3 440.1 reduce-scatter.2
  960.2 164.0 reduce-scatter.4

commit v3 on v2

--- a/solution.py
+++ b/solution.py
@@ -123,7 +123,7 @@
     )(kv)
 
 
-def kv_return_kernel(n_ctx, back, g_ref, out_ref, recv_buf, send_sem, recv_sem):
+def kv_return_kernel(n_ctx, back, own_ref, g_ref, out_ref, recv_buf, send_sem, recv_sem):
     c = lax.axis_index("ctx")
     f = lax.axis_index("fsdp")
     neighbour_barrier(n_ctx, back, c, f)
@@ -144,13 +144,13 @@
         def _():
             copy(s, c - s).start()
 
-    out_ref[...] = g_ref[back]
+    out_ref[...] = own_ref[...]
     for s in range(1, back + 1):
 
         @pl.when(c + s < n_ctx)
         def _():
             copy(s, c).wait_recv()
-            out_ref[...] += recv_buf[s - 1]
+            out_ref[...] += recv_buf[s - 1].astype(jnp.float32)
 
     for s in range(1, back + 1):
 
@@ -159,19 +159,19 @@
             copy(s, c - s).wait_send()
 
 
-def kv_return(g, n_ctx, back):
+def kv_return(own, g, n_ctx, back):
     return pl.pallas_call(
         functools.partial(kv_return_kernel, n_ctx, back),
-        out_shape=jax.ShapeDtypeStruct(g.shape[1:], g.dtype),
-        in_specs=[pl.BlockSpec(memory_space=pltpu.VMEM)],
+        out_shape=jax.ShapeDtypeStruct(own.shape, own.dtype),
+        in_specs=[pl.BlockSpec(memory_space=pltpu.VMEM)] * 2,
         out_specs=pl.BlockSpec(memory_space=pltpu.VMEM),
         scratch_shapes=[
-            pltpu.VMEM((back,) + g.shape[1:], g.dtype),
+            pltpu.VMEM(g.shape, g.dtype),
             pltpu.SemaphoreType.DMA((back,)),
             pltpu.SemaphoreType.DMA((back,)),
         ],
         compiler_params=pltpu.CompilerParams(collective_id=1, has_side_effects=True),
-    )(g)
+    )(own, g)
 
 
 def body(
@@ -236,12 +236,10 @@
     key_low = rotate(keys_new, query_positions, KVH, 1.0).astype(jnp.bfloat16)
     value_low = values_new.astype(jnp.bfloat16)
 
-    ff_full = lax.all_gather(
-        jnp.concatenate([gate_weight, up_weight, down_weight.reshape(rows, ff)], axis=1),
-        ALL,
-        axis=0,
-        tiled=True,
-    )
+    gate_up_full = lax.all_gather(
+        jnp.concatenate([gate_weight, up_weight], axis=1), ALL, axis=0, tiled=True
+    )
+    down_full = lax.all_gather(down_weight, ALL, axis=0, tiled=True)
     n_ctx = lax.axis_size("ctx")
     max_doc = min(DOC_MOST, KBLK * (stream_len // (2 * KBLK)))
     back = min(-(-(max_doc - 1) // tok_rows), n_ctx - 1)
@@ -275,10 +273,6 @@
     attended_low = attended_sum.reshape(tok_rows, D).astype(jnp.bfloat16)
     middle = local_tokens + jnp.dot(attended_low, output_full, preferred_element_type=jnp.float32)
 
-    gate_up_full = ff_full[:, : 2 * ff]
-    gate_full = ff_full[:, :ff]
-    up_full = ff_full[:, ff : 2 * ff]
-    down_full = ff_full[:, 2 * ff :].reshape(n_dev, rows, ff).reshape(n_dev * ff_rows, D)
     scale_two = rms_scale(middle)
     normed_two = middle * scale_two
     normed_two_low = (normed_two * gain_two_f).astype(jnp.bfloat16)
@@ -290,7 +284,9 @@
     layer_out = middle + jnp.dot(hidden_low, down_full, preferred_element_type=jnp.float32)
 
     grad_out = cotangent[0]
-    down_term = outer_rows(hidden_low, grad_out)
+    down_sum = lax.psum_scatter(
+        outer_rows(hidden_low, grad_out).astype(jnp.bfloat16), ALL, scatter_dimension=0, tiled=True
+    )
     hidden_grad = times_transposed(grad_out, down_full)
     gate_grad = (hidden_grad * up_pre * sigmoid * (1.0 + gate_pre * (1.0 - sigmoid))).astype(
         jnp.bfloat16
@@ -298,14 +294,7 @@
     up_grad = (hidden_grad * gate_pre * sigmoid).astype(jnp.bfloat16)
     gate_up_cat = jnp.concatenate([gate_grad, up_grad], axis=1)
     gate_up_term = outer_rows(normed_two_low, gate_up_cat)
-    ff_pack = jnp.concatenate(
-        [
-            gate_up_term.astype(jnp.bfloat16),
-            down_term.reshape(n_dev, ff_rows, D).reshape(n_dev * rows, ff).astype(jnp.bfloat16),
-        ],
-        axis=1,
-    )
-    ff_pack, gate_up_cat = lax.optimization_barrier((ff_pack, gate_up_cat))
+    ff_pack, gate_up_cat = lax.optimization_barrier((gate_up_term.astype(jnp.bfloat16), gate_up_cat))
     ff_sum = lax.psum_scatter(ff_pack, ALL, scatter_dimension=0, tiled=True)
     normed_two_grad = times_transposed(gate_up_cat, gate_up_full)
     gain_two_term = jnp.sum(normed_two_grad * normed_two, axis=0)
@@ -335,11 +324,8 @@
     value_term = jnp.einsum(
         "qgrk,qgrd->kgd", probs_low, attended_grad_low, preferred_element_type=jnp.float32
     ).reshape(win, KVW)
-    kv_sum = kv_return(
-        jnp.concatenate([key_term, value_term], axis=1).reshape(back + 1, tok_rows, 2 * KVW),
-        n_ctx,
-        back,
-    )
+    kv_term = jnp.concatenate([key_term, value_term], axis=1).reshape(back + 1, tok_rows, 2 * KVW)
+    kv_sum = kv_return(kv_term[back], kv_term[:back].astype(jnp.bfloat16), n_ctx, back)
     key_grad_low = rotate(kv_sum[:, :KVW] * score_scale, query_positions, KVH, -1.0).astype(
         jnp.bfloat16
     )
@@ -383,7 +369,7 @@
         attention_sum[:, c_g + 1],
         ff_sum[:, :ff],
         ff_sum[:, ff : 2 * ff],
-        ff_sum[:, 2 * ff :].reshape(ff_rows, D),
+        down_sum.astype(jnp.float32),
     )
 
 

time: 1140 us -> 1080 us (0.947)
  waiting for transfers between devices: 569 us -> 684 us
  Pallas kernels: 265 us -> 171 us
  local copies, waits for them, and re-layouts: 102 us -> 37.9 us
  other arithmetic: 65 us -> 42.5 us
    reduce_scatter x0 -> x1, waiting for transfers between devices: none -> 134 us  [body(): lax.psum_scatter(outer_rows(hidden_low, grad_out).astype(jnp.bfloat16), A...]
    pallas_call x1, Pallas kernels: 211 us -> 122 us  [kv_return(): pl.pallas_call(functools.partial(kv_return_kernel, n_ctx, back), out_shap...]
    reduce_scatter x1, waiting for transfers between devices: 140 us -> 75.1 us  [body(): ff_sum = lax.psum_scatter(ff_pack, ALL, scatter_dimension=0, tiled=True)]
    all_gather x1 -> x2, waiting for transfers between devices: 175 us -> 205 us  [the longest x1 122 us: body(): lax.all_gather(jnp.concatenate([gate_weight, up_weight], axis=1), ALL, ax...]
    concatenate x2 -> x1, other arithmetic: 27.7 us -> 2.05 us  [body(): jnp.concatenate([gate_weight, up_weight], axis=1)]
    convert_element_type x1 -> x0, local copies, waits for them, and re-layouts: 23 us -> none  [body(): down_term.reshape(n_dev, ff_rows, D).reshape(n_dev * rows, ff)]
    another operation x3 -> x2, local copies, waits for them, and re-layouts: 25.4 us -> 2.47 us  [the longest x1 22.9 us: body(): ff_full[:, 2 * ff:].reshape(n_dev, rows, ff).reshape(n_dev * ff_rows, D)]
    reduce_scatter x1, waiting for transfers between devices: 152 us -> 167 us  [body(): lax.psum_scatter(jnp.concatenate([outer_rows(normed_low, projection_cat)....]
  transfers between devices with their start and end apart: 4 -> 6, of which waited for: 4 -> 6; matrix products, arithmetic and copies ran while one was open for 12% -> 15% of each run, Pallas kernels for 23% -> 16%
where the time goes in v3:
time: 1080 us
  waiting for transfers between devices  684 us (63%)
  Pallas kernels  171 us (16%)
  matrix products  124 us (11%)
  other arithmetic  42.5 us (4%)
  local copies, waits for them, and re-layouts  37.9 us (4%)
  between operations  16.8 us (2%)
    reduce_scatter x1, waiting for transfers between devices, body(): lax.psum_scatter(jnp.concatenate([outer_rows(normed_low, projection_cat)....  167 us
    reduce_scatter x1, waiting for transfers between devices, body(): lax.psum_scatter(outer_rows(hidden_low, grad_out).astype(jnp.bfloat16), A...  134 us
    pallas_call x1, Pallas kernels, kv_return(): pl.pallas_call(functools.partial(kv_return_kernel, n_ctx, back), out_shap...  122 us
    all_gather x1, waiting for transfers between devices, body(): lax.all_gather(jnp.concatenate([gate_weight, up_weight], axis=1), ALL, ax...  122 us
    all_gather x1, waiting for transfers between devices, body(): lax.all_gather(jnp.concatenate([query_weight, key_weight, value_weight, o...  102 us
    all_gather x1, waiting for transfers between devices, body(): down_full = lax.all_gather(down_weight, ALL, axis=0, tiled=True)  83.2 us
    reduce_scatter x1, waiting for transfers between devices, body(): ff_sum = lax.psum_scatter(ff_pack, ALL, scatter_dimension=0, tiled=True)  75.1 us
    pallas_call x1, Pallas kernels, kv_share(): pl.pallas_call(functools.partial(kv_share_kernel, n_ctx, back), out_shape...  48.4 us
  transfers between devices with their start and end apart: 6, of which 6 were waited for; matrix products, arithmetic and copies ran while one was open for 15% of the time, Pallas kernels for 16%

profile of v3, /device:TPU:0, one launch (start us, length us, event | category | flops | bytes accessed | tf_op | source)
XLA Modules:
  0.0 1076.6 jit_solution(2453505394523563767)
XLA Ops:
  17.9 102.4 %all-gather.4.cloned.1.call-done = bf16[1536,4736]{1,0:T(8,128)(2,1)} async-done(((bf16[48,4736]{1,0:T(8,128)(2,1)}), bf16[1536,4736]{1,0:T(8,128)(2,1)}) %all-gather.4.cloned.1.call-update) | async-done | bytes 14549008 | tf_op jit(solution)/shard_map/all_gather | solution.py:203
  121.9 5.2 fusion.3
  129.5 48.4 %shard_map.203 = bf16[5,128,1536]{2,1,0:T(8,128)(2,1)} custom-call(bf16[128,1536]{1,0:T(8,128)(2,1)} %pad_maximum_fusion.5.kv_ref), custom_call_target="tpu_custom_call" | custom-call | tf_op jit(solution)/shard_map/pallas_call | solution.py:116
  182.8 4.4 fusion.57
  187.3 3.2 fusion.24
  192.0 3.4 multiply_reduce_fusion.3
  195.4 121.6 %all-gather.6.cloned.1.call-done = bf16[1536,8192]{1,0:T(8,128)(2,1)} async-done(((bf16[48,8192]{1,0:T(8,128)(2,1)}), bf16[1536,8192]{1,0:T(8,128)(2,1)}) %all-gather.6.cloned.1.call-update) | async-done | bytes 25165840 | tf_op jit(solution)/shard_map/all_gather | solution.py:239
  317.0 13.8 %fusion.51 = f32[128,8192]{1,0:T(8,128)} fusion(bf16[1536,8192]{1,0:T(8,128)(2,1)} %all-gather.6.cloned.1.call-done, f32[128,1536]{1,0:T(8,128)S(1)} %get-tuple-element.66, f32[1536]{0:T(1024)S(1)} %get-tuple-element.27, f32[128]{0:T(128)S(1)} %add_rsqrt_fusion), kind=kOutput, calls=%fused_computation.122 | convolution fusion | flops 3221815296 | bytes 30153216 | tf_op jit(solution)/shard_map/dot_general | solution.py:279
  330.8 83.2 %all-gather.8.cloned.1.call-done = bf16[4096,1536]{1,0:T(8,128)(2,1)} async-done(((bf16[128,1536]{1,0:T(8,128)(2,1)}), bf16[4096,1536]{1,0:T(8,128)(2,1)}) %all-gather.8.cloned.1.call-update) | async-done | bytes 12582928 | tf_op jit(solution)/shard_map/all_gather | solution.py:242
  414.1 11.1 %multiply_convert_fusion.1 = (bf16[128,4096]{1,0:T(8,128)(2,1)S(1)}, bf16[128,4096]{1,0:T(8,128)(2,1)S(1)}, bf16[128,4096]{1,0:T(8,128)(2,1)}) fusion(f32[128,8192]{1,0:T(8,128)} %fusion.51, bf16[4096,1536]{1,0:T(8,128)(2,1)} %all-gather.8.cloned.1.call-done, bf16[1,128,1536]{2,1,0:T(8,128)(2,1)} %param.25), kind=kOutput, calls=%fused_computation.36 | convolution fusion | flops 1619001344 | bytes 20316160 | tf_op jit(solution)/shard_map/dot_general | solution.py:63
  428.1 13.5 %convolution_convert_fusion = bf16[1536,8192]{1,0:T(8,128)(2,1)} fusion(f32[128,1536]{1,0:T(8,128)S(1)} %get-tuple-element.66, f32[1536]{0:T(1024)S(1)} %get-tuple-element.27, f32[128]{0:T(128)S(1)} %add_rsqrt_fusion, bf16[128,4096]{1,0:T(8,128)(2,1)} %copy-done.12, bf16[128,4096]{1,0:T(8,128)(2,1)} %copy-done.11), kind=kOutput, calls=%fused_computation.1 | convolution fusion | flops 3238592512 | bytes 28056064 | tf_op jit(solution)/shard_map/dot_general | solution.py:57
  441.6 10.6 convolution_convert_fusion.1
  453.5 16.9 %multiply_reduce_fusion = (bf16[1536]{0:T(1024)(128)(2,1)S(1)}, f32[128]{0:T(128)S(1)}, f32[128,1536]{1,0:T(8,128)}) fusion(f32[128,1536]{1,0:T(8,128)S(1)} %get-tuple-element.66, f32[128]{0:T(128)S(1)} %add_rsqrt_fusion, f32[1536]{0:T(1024)S(1)} %get-tuple-element.27, bf16[128,8192]{1,0:T(8,128)(2,1)} %pad_maximum_fusion.2, ...), kind=kOutput, calls=%fused_computation.60 | convolution fusion | flops 3222403584 | bytes 28846080 | tf_op jit(solution)/shard_map/dot_general | solution.py:63
  472.9 5.2 fusion.19
  481.6 4.8 fusion.6
  502.7 122.3 %shard_map.204 = f32[128,1536]{1,0:T(8,128)} custom-call(f32[128,1536]{1,0:T(8,128)} %fusion.37.own_ref, bf16[4,128,1536]{2,1,0:T(8,128)(2,1)} %bitcast.110), custom_call_target="tpu_custom_call" | custom-call | tf_op jit(solution)/shard_map/pallas_call | solution.py:163
  635.5 8.4 fusion.35
  646.2 3.6 convolution_convert_fusion.3
  649.8 7.0 convolution_convert_fusion.2
  656.8 75.1 %reduce-scatter.4.cloned.1.call-done = bf16[48,8192]{1,0:T(8,128)(2,1)} async-done(((bf16[1536,8192]{1,0:T(8,128)(2,1)}), bf16[48,8192]{1,0:T(8,128)(2,1)}) %reduce-scatter.4.cloned.1.call-update) | async-done | bytes 786448 | tf_op jit(solution)/shard_map/reduce_scatter | solution.py:298
  736.5 13.2 %pad_maximum_fusion = bf16[1536,4736]{1,0:T(8,128)(2,1)} fusion(bf16[1536,128]{1,0:T(8,128)(2,1)S(1)} %scatter.4, bf16[1536,1536]{1,0:T(8,128)(2,1)} %convolution_convert_fusion.3, bf16[1536,3072]{1,0:T(8,128)(2,1)} %convolution_convert_fusion.2), kind=kLoop, calls=%fused_computation.3 | loop fusion | flops 43646976 | bytes 29097984 | tf_op jit(solution)/shard_map/concatenate | solution.py:348
  752.2 7.9 fusion.23
  760.1 134.1 %reduce-scatter.8.cloned.1.call-done = bf16[128,1536]{1,0:T(8,128)(2,1)} async-done(((bf16[4096,1536]{1,0:T(8,128)(2,1)}), bf16[128,1536]{1,0:T(8,128)(2,1)}) %reduce-scatter.8.cloned.1.call-update) | async-done | bytes 393232 | tf_op jit(solution)/shard_map/reduce_scatter | solution.py:287
  897.4 166.8 %reduce-scatter.6.cloned.1.call-done = bf16[48,4736]{1,0:T(8,128)(2,1)} async-done(((bf16[1536,4736]{1,0:T(8,128)(2,1)}), bf16[48,4736]{1,0:T(8,128)(2,1)}) %reduce-scatter.6.cloned.1.call-update) | async-done | bytes 454672 | tf_op jit(solution)/shard_map/reduce_scatter | solution.py:347
  (142 shorter events, 73.7 us)
Async XLA Ops:
  7.2 10.1 copy-start.7
  7.2 113.1 %all-gather.4.cloned.1.call-start = ((), (), s32[]{:S(2)}) async-start(), calls=%async_computation.3 | async-start | bytes 15003648 | tf_op jit(solution)/shard_map/all_gather | solution.py:203
  12.5 304.5 %all-gather.6.cloned.1.call-start = ((), (), s32[]{:S(2)}) async-start(), calls=%async_computation.4 | async-start | bytes 25952256 | tf_op jit(solution)/shard_map/all_gather | solution.py:239
  14.6 399.4 %all-gather.8.cloned.1.call-start = ((), (), s32[]{:S(2)}) async-start(), calls=%async_computation.5 | async-start | bytes 12976128 | tf_op jit(solution)/shard_map/all_gather | solution.py:242
  15.4 716.6 %reduce-scatter.4.cloned.1.call-start = ((), (), s32[]{:S(2)}) async-start(), calls=%async_computation.6 | async-start | bytes 25952256 | tf_op jit(solution)/shard_map/reduce_scatter | solution.py:298
  180.2 7.1 copy-start.14
  182.8 4.5 copy-start.18
  187.3 3.2 copy-start.13
  192.0 3.4 copy-start.16
  441.6 452.6 %reduce-scatter.8.cloned.1.call-start = ((), (), s32[]{:S(2)}) async-start(), calls=%async_computation.8 | async-start | bytes 12976128 | tf_op jit(solution)/shard_map/reduce_scatter | solution.py:287
  452.2 612.0 %reduce-scatter.6.cloned.1.call-start = ((), (), s32[]{:S(2)}) async-start(), calls=%async_computation.7 | async-start | bytes 15003648 | tf_op jit(solution)/shard_map/reduce_scatter | solution.py:347
  481.6 6.4 copy-start.19
  496.3 3.0 copy-start
  502.7 130.7 %copy-start.3 = (bf16[128,8,2,640]{0,3,2,1:T(8,128)(2,1)S(1)}, bf16[128,8,2,640]{0,3,2,1:T(8,128)(2,1)}, u32[]{:S(2)}) copy-start(bf16[128,8,2,640]{0,3,2,1:T(8,128)(2,1)} %copy-done.2) | copy-start | bytes 7864324
  632.2 3.3 copy-start.9
  632.2 3.3 copy-start.21
  633.4 10.5 copy-start.23
  635.5 10.7 copy-start.6
  635.5 10.7 copy-start.17
  646.2 3.6 copy-start.10
  646.2 3.6 copy-start.22
  646.2 3.6 copy-start.24
  749.7 2.5 copy-start.4
  752.2 143.9 %copy-start.15 = (bf16[48,8192]{1,0:T(8,128)(2,1)S(1)}, bf16[48,8192]{1,0:T(8,128)(2,1)}, u32[]{:S(2)}) copy-start(bf16[48,8192]{1,0:T(8,128)(2,1)} %reduce-scatter.4.cloned.1.call-done) | copy-start | bytes 2359300
  (8 other events, 9.8 us)
Sparse Core Ops, SparseCore 0:
  12.6 107.6 all-gather.3
  123.7 193.2 all-gather.5
  319.9 94.1 all-gather.7
  441.7 290.2 reduce-scatter.3
  738.9 155.2 reduce-scatter.7
  900.1 164.0 reduce-scatter.5

commit v4 on v3

--- a/solution.py
+++ b/solution.py
@@ -172,6 +172,94 @@
         ],
         compiler_params=pltpu.CompilerParams(collective_id=1, has_side_effects=True),
     )(own, g)
+
+
+def peer_barrier(n_f, c, f):
+    barrier = pltpu.get_barrier_semaphore()
+    for k in range(1, n_f):
+        pl.semaphore_signal(barrier, inc=1, device_id=(c, (f + k) % n_f), device_id_type=MESH)
+    pl.semaphore_wait(barrier, n_f - 1)
+
+
+def group_gather_kernel(n_f, x_ref, out_ref, send_sem, recv_sem):
+    c = lax.axis_index("ctx")
+    f = lax.axis_index("fsdp")
+    peer_barrier(n_f, c, f)
+    copies = []
+    for k in range(1, n_f):
+        copy = pltpu.make_async_remote_copy(
+            src_ref=x_ref,
+            dst_ref=out_ref.at[f],
+            send_sem=send_sem.at[k - 1],
+            recv_sem=recv_sem.at[k - 1],
+            device_id=(c, (f + k) % n_f),
+            device_id_type=MESH,
+        )
+        copy.start()
+        copies.append(copy)
+    out_ref[f] = x_ref[...]
+    for k in range(1, n_f):
+        pltpu.make_async_remote_copy(
+            src_ref=x_ref,
+            dst_ref=out_ref.at[(f + n_f - k) % n_f],
+            send_sem=send_sem.at[k - 1],
+            recv_sem=recv_sem.at[k - 1],
+            device_id=(c, f),
+            device_id_type=MESH,
+        ).wait_recv()
+    for copy in copies:
+        copy.wait_send()
+
+
+def group_gather(x, n_f):
+    return pl.pallas_call(
+        functools.partial(group_gather_kernel, n_f),
+        out_shape=jax.ShapeDtypeStruct((n_f,) + x.shape, x.dtype),
+        in_specs=[pl.BlockSpec(memory_space=pltpu.VMEM)],
+        out_specs=pl.BlockSpec(memory_space=pltpu.VMEM),
+        scratch_shapes=[pltpu.SemaphoreType.DMA((n_f - 1,)), pltpu.SemaphoreType.DMA((n_f - 1,))],
+        compiler_params=pltpu.CompilerParams(collective_id=2, has_side_effects=True),
+    )(x)
+
+
+def group_reduce_kernel(n_f, p_ref, out_ref, recv_buf, send_sem, recv_sem):
+    c = lax.axis_index("ctx")
+    f = lax.axis_index("fsdp")
+    peer_barrier(n_f, c, f)
+    copies = []
+    for k in range(1, n_f):
+        dest = (f + k) % n_f
+        copy = pltpu.make_async_remote_copy(
+            src_ref=p_ref.at[dest],
+            dst_ref=recv_buf.at[k - 1],
+            send_sem=send_sem.at[k - 1],
+            recv_sem=recv_sem.at[k - 1],
+            device_id=(c, dest),
+            device_id_type=MESH,
+        )
+        copy.start()
+        copies.append(copy)
+    out_ref[...] = p_ref[f]
+    for k in range(1, n_f):
+        copies[k - 1].wait_recv()
+        out_ref[...] += recv_buf[k - 1]
+    for copy in copies:
+        copy.wait_send()
+
+
+def group_reduce(p, n_f):
+    return pl.pallas_call(
+        functools.partial(group_reduce_kernel, n_f),
+        out_shape=jax.ShapeDtypeStruct(p.shape[1:], p.dtype),
+        in_specs=[pl.BlockSpec(memory_space=pltpu.VMEM)],
+        out_specs=pl.BlockSpec(memory_space=pltpu.VMEM),
+        scratch_shapes=[
+            pltpu.VMEM((n_f - 1,) + p.shape[1:], p.dtype),
+            pltpu.SemaphoreType.DMA((n_f - 1,)),
+            pltpu.SemaphoreType.DMA((n_f - 1,)),
+        ],
+        compiler_params=pltpu.CompilerParams(collective_id=3, has_side_effects=True),
+    )(p)
 
 
 def body(
@@ -236,11 +324,17 @@
     key_low = rotate(keys_new, query_positions, KVH, 1.0).astype(jnp.bfloat16)
     value_low = values_new.astype(jnp.bfloat16)
 
-    gate_up_full = lax.all_gather(
-        jnp.concatenate([gate_weight, up_weight], axis=1), ALL, axis=0, tiled=True
-    )
-    down_full = lax.all_gather(down_weight, ALL, axis=0, tiled=True)
     n_ctx = lax.axis_size("ctx")
+    n_f = lax.axis_size("fsdp")
+    chunk = ff_rows
+    units = n_ctx * chunk
+    gu_parts = jnp.transpose(
+        jnp.stack([gate_weight, up_weight], axis=1).reshape(rows, 2, n_ctx, n_f, chunk),
+        (3, 0, 1, 2, 4),
+    )
+    gu_parts = lax.all_to_all(gu_parts, "fsdp", 0, 0, tiled=True).reshape(n_f * rows, 2 * units)
+    gate_up_tp = lax.all_gather(gu_parts, "ctx", axis=0, tiled=True)
+    down_tp = lax.all_gather(down_weight, "ctx", axis=0, tiled=True)
     max_doc = min(DOC_MOST, KBLK * (stream_len // (2 * KBLK)))
     back = min(-(-(max_doc - 1) // tok_rows), n_ctx - 1)
     win = (back + 1) * tok_rows
@@ -276,27 +370,37 @@
     scale_two = rms_scale(middle)
     normed_two = middle * scale_two
     normed_two_low = (normed_two * gain_two_f).astype(jnp.bfloat16)
-    gate_up = jnp.dot(normed_two_low, gate_up_full, preferred_element_type=jnp.float32)
-    gate_pre = gate_up[:, :ff]
-    up_pre = gate_up[:, ff:]
+    group_tokens = n_f * tok_rows
+    xn2_all = group_gather(normed_two_low, n_f).reshape(group_tokens, D)
+    gate_up = jnp.dot(xn2_all, gate_up_tp, preferred_element_type=jnp.float32)
+    gate_pre = gate_up[:, :units]
+    up_pre = gate_up[:, units:]
     sigmoid = jax.nn.sigmoid(gate_pre)
     hidden_low = (gate_pre * sigmoid * up_pre).astype(jnp.bfloat16)
-    layer_out = middle + jnp.dot(hidden_low, down_full, preferred_element_type=jnp.float32)
+    ff_part = jnp.dot(hidden_low, down_tp, preferred_element_type=jnp.float32)
+    layer_out = middle + group_reduce(ff_part.reshape(n_f, tok_rows, D), n_f)
 
     grad_out = cotangent[0]
+    grad_all = group_gather(grad_out, n_f).reshape(group_tokens, D)
     down_sum = lax.psum_scatter(
-        outer_rows(hidden_low, grad_out).astype(jnp.bfloat16), ALL, scatter_dimension=0, tiled=True
-    )
-    hidden_grad = times_transposed(grad_out, down_full)
+        outer_rows(hidden_low, grad_all).astype(jnp.bfloat16), "ctx", scatter_dimension=0, tiled=True
+    )
+    hidden_grad = times_transposed(grad_all, down_tp)
     gate_grad = (hidden_grad * up_pre * sigmoid * (1.0 + gate_pre * (1.0 - sigmoid))).astype(
         jnp.bfloat16
     )
     up_grad = (hidden_grad * gate_pre * sigmoid).astype(jnp.bfloat16)
     gate_up_cat = jnp.concatenate([gate_grad, up_grad], axis=1)
-    gate_up_term = outer_rows(normed_two_low, gate_up_cat)
+    gate_up_term = outer_rows(xn2_all, gate_up_cat)
     ff_pack, gate_up_cat = lax.optimization_barrier((gate_up_term.astype(jnp.bfloat16), gate_up_cat))
-    ff_sum = lax.psum_scatter(ff_pack, ALL, scatter_dimension=0, tiled=True)
-    normed_two_grad = times_transposed(gate_up_cat, gate_up_full)
+    gu_sum = lax.psum_scatter(ff_pack, "ctx", scatter_dimension=0, tiled=True)
+    gu_sum = lax.all_to_all(gu_sum.reshape(n_f, rows, 2 * units), "fsdp", 0, 0, tiled=True)
+    ff_sum = jnp.transpose(
+        gu_sum.reshape(n_f, rows, 2, n_ctx, chunk), (1, 2, 3, 0, 4)
+    ).reshape(rows, 2 * ff)
+    normed_two_grad = group_reduce(
+        times_transposed(gate_up_cat, gate_up_tp).reshape(n_f, tok_rows, D), n_f
+    )
     gain_two_term = jnp.sum(normed_two_grad * normed_two, axis=0)
     scaled_two = normed_two_grad * gain_two_f
     middle_grad = grad_out.astype(jnp.float32) + scale_two * (

time: 1080 us -> 800 us (0.74)
  waiting for transfers between devices: 684 us -> 318 us
  Pallas kernels: 171 us -> 265 us
  matrix products: 124 us -> 88.9 us
  blocking collectives: 0 us -> 18.9 us
    reduce_scatter x2, waiting for transfers between devices: 209 us -> 0.01 us  [the longest x1 0.01 us: body(): gu_sum = lax.psum_scatter(ff_pack, 'ctx', scatter_dimension=0, tiled=True)]
    pallas_call x0 -> x4, Pallas kernels: none -> 128 us  [the longest x2 78 us: group_reduce(): pl.pallas_call(functools.partial(group_reduce_kernel, n_f), out_shape=jax...]
    all_gather x2, waiting for transfers between devices: 205 us -> 91.5 us  [the longest x1 72.8 us: body(): down_tp = lax.all_gather(down_weight, 'ctx', axis=0, tiled=True)]
    pallas_call x1, Pallas kernels: 122 us -> 84.5 us  [kv_return(): pl.pallas_call(functools.partial(kv_return_kernel, n_ctx, back), out_shap...]
    all_gather x1, waiting for transfers between devices: 102 us -> 66.5 us  [body(): lax.all_gather(jnp.concatenate([query_weight, key_weight, value_weight, o...]
    all_to_all x0 -> x1, blocking collectives: none -> 18.9 us  [body(): lax.all_to_all(gu_parts, 'fsdp', 0, 0, tiled=True)]
    dot_general x4, matrix products: 34.6 us -> 20.5 us  [outer_rows(): lax.dot_general(left, right, (((0,), (0,)), ((), ())), preferred_element_...]
    dot_general x4, matrix products: 41.6 us -> 28.4 us  [times_transposed(): lax.dot_general(left, right, (((1,), (1,)), ((), ())), preferred_element_...]
  transfers between devices with their start and end apart: 6 -> 7, of which waited for: 6 -> 5; matrix products, arithmetic and copies ran while one was open for 15% -> 18% of each run, Pallas kernels for 16% -> 33%
where the time goes in v4:
time: 800 us; the launch traced here: 795 us
  waiting for transfers between devices  318 us (40%)
  Pallas kernels  265 us (33%)
  matrix products  88.9 us (11%)
  local copies, waits for them, and re-layouts  41.3 us (5%)
  other arithmetic  41.3 us (5%)
  blocking collectives  18.9 us (2%)
  between operations  17.1 us (2%)
    reduce_scatter x1, waiting for transfers between devices, body(): lax.psum_scatter(jnp.concatenate([outer_rows(normed_low, projection_cat)....  156 us
    pallas_call x1, Pallas kernels, kv_return(): pl.pallas_call(functools.partial(kv_return_kernel, n_ctx, back), out_shap...  84.5 us
    pallas_call x2, Pallas kernels, group_reduce(): pl.pallas_call(functools.partial(group_reduce_kernel, n_f), out_shape=jax...  78 us
    all_gather x1, waiting for transfers between devices, body(): down_tp = lax.all_gather(down_weight, 'ctx', axis=0, tiled=True)  72.8 us
    all_gather x1, waiting for transfers between devices, body(): lax.all_gather(jnp.concatenate([query_weight, key_weight, value_weight, o...  66.5 us
    pallas_call x1, Pallas kernels, kv_share(): pl.pallas_call(functools.partial(kv_share_kernel, n_ctx, back), out_shape...  52.8 us
    pallas_call x2, Pallas kernels, group_gather(): pl.pallas_call(functools.partial(group_gather_kernel, n_f), out_shape=jax...  50.2 us
    dot_general x4, matrix products, times_transposed(): lax.dot_general(left, right, (((1,), (1,)), ((), ())), preferred_element_...  28.4 us
  transfers between devices with their start and end apart: 7, of which 5 were waited for; matrix products, arithmetic and copies ran while one was open for 18% of the time, Pallas kernels for 33%

profile of v4, /device:TPU:0, one launch (start us, length us, event | category | flops | bytes accessed | tf_op | source)
XLA Modules:
  0.0 794.6 jit_solution(2281477261171877501)
XLA Ops:
  14.4 18.9 %all_to_all.10 = bf16[4,48,2,8,128]{4,3,2,1,0:T(8,128)(2,1)S(1)} all-to-all(bf16[4,48,2,8,128]{4,3,2,1,0:T(8,128)(2,1)S(1)} %maximum_bitcast_fusion), channel_id=1, replica_groups=mesh['ctx'=8,'fsdp'=4] {'fsdp'}, dimensions={0} | all-to-all | bytes 1572864 | tf_op jit(solution)/shard_map/all_to_all | solution.py:335
  36.1 28.9 %shard_map.206 = bf16[4,128,1536]{2,1,0:T(8,128)(2,1)} custom-call(bf16[128,1536]{1,0:T(8,128)(2,1)} %bitcast.151), custom_call_target="tpu_custom_call" | custom-call | tf_op jit(solution)/shard_map/pallas_call | solution.py:215
  65.4 66.5 %all-gather.4.cloned.1.call-done = bf16[1536,4736]{1,0:T(8,128)(2,1)} async-done(((bf16[48,4736]{1,0:T(8,128)(2,1)}), bf16[1536,4736]{1,0:T(8,128)(2,1)}) %all-gather.4.cloned.1.call-update) | async-done | bytes 14549008 | tf_op jit(solution)/shard_map/all_gather | solution.py:291
  133.5 5.2 fusion.3
  141.1 52.8 %shard_map.203 = bf16[5,128,1536]{2,1,0:T(8,128)(2,1)} custom-call(bf16[128,1536]{1,0:T(8,128)(2,1)} %pad_maximum_fusion.4.kv_ref), custom_call_target="tpu_custom_call" | custom-call | tf_op jit(solution)/shard_map/pallas_call | solution.py:116
  198.9 4.4 fusion.52
  212.6 21.3 %shard_map.204 = bf16[4,128,1536]{2,1,0:T(8,128)(2,1)} custom-call(bf16[128,1536]{1,0:T(8,128)(2,1)} %multiply_convert_fusion.3.x_ref), custom_call_target="tpu_custom_call" | custom-call | tf_op jit(solution)/shard_map/pallas_call | solution.py:215
  233.8 18.7 %all-gather.6.cloned.1.call-done = bf16[1536,2048]{1,0:T(8,128)(2,1)} async-done(((bf16[192,2048]{1,0:T(8,128)(2,1)}), bf16[1536,2048]{1,0:T(8,128)(2,1)}) %all-gather.6.cloned.1.call-update) | async-done | bytes 6291472 | tf_op jit(solution)/shard_map/all_gather | solution.py:336
  252.6 8.6 %fusion.54 = f32[512,2048]{1,0:T(8,128)} fusion(bf16[512,1536]{1,0:T(8,128)(2,1)} %bitcast.149, bf16[1536,2048]{1,0:T(8,128)(2,1)} %all-gather.6.cloned.1.call-done), kind=kOutput, calls=%fused_computation.126 | convolution fusion | flops 3221225472 | bytes 12058624 | tf_op jit(solution)/shard_map/dot_general | solution.py:375
  261.2 72.8 %all-gather.8.cloned.1.call-done = bf16[1024,1536]{1,0:T(8,128)(2,1)} async-done(((bf16[128,1536]{1,0:T(8,128)(2,1)}), bf16[1024,1536]{1,0:T(8,128)(2,1)}) %all-gather.8.cloned.1.call-update) | async-done | bytes 3145744 | tf_op jit(solution)/shard_map/all_gather | solution.py:337
  334.0 7.1 multiply_convert_fusion.1
  343.2 5.5 convolution_convert_fusion.1
  350.2 5.6 fusion.55
  355.9 38.5 %shard_map.205 = f32[128,1536]{1,0:T(8,128)} custom-call(f32[4,128,1536]{2,1,0:T(8,128)} %bitcast.137), custom_call_target="tpu_custom_call" | custom-call | tf_op jit(solution)/shard_map/pallas_call | solution.py:251
  394.4 8.6 %fusion.56 = f32[512,1536]{1,0:T(8,128)} fusion(bf16[512,2048]{1,0:T(8,128)(2,1)} %pad_maximum_fusion.2, bf16[1536,2048]{1,0:T(8,128)(2,1)} %all-gather.6.cloned.1.call-done), kind=kOutput, calls=%fused_computation.128 | convolution fusion | flops 3221225472 | bytes 11534336 | tf_op jit(solution)/shard_map/dot_general | solution.py:63
  403.0 39.5 %shard_map.207 = f32[128,1536]{1,0:T(8,128)} custom-call(f32[4,128,1536]{2,1,0:T(8,128)} %bitcast.136), custom_call_target="tpu_custom_call" | custom-call | tf_op jit(solution)/shard_map/pallas_call | solution.py:251
  446.7 4.8 fusion.19
  453.4 5.3 convolution_convert_fusion.3
  460.1 4.1 fusion.6
  480.6 84.5 %shard_map.208 = f32[128,1536]{1,0:T(8,128)} custom-call(f32[128,1536]{1,0:T(8,128)} %fusion.35.own_ref, bf16[4,128,1536]{2,1,0:T(8,128)(2,1)} %bitcast.124), custom_call_target="tpu_custom_call" | custom-call | tf_op jit(solution)/shard_map/pallas_call | solution.py:163
  575.4 7.9 fusion.33
  592.9 6.1 convolution_convert_fusion
  607.9 13.0 %pad_maximum_fusion = bf16[1536,4736]{1,0:T(8,128)(2,1)} fusion(bf16[1536,128]{1,0:T(8,128)(2,1)S(1)} %scatter.4, bf16[1536,1536]{1,0:T(8,128)(2,1)} %convolution_convert_fusion.2, bf16[1536,3072]{1,0:T(8,128)(2,1)} %convolution_convert_fusion), kind=kLoop, calls=%fused_computation.1 | loop fusion | flops 43646976 | bytes 29097984 | tf_op jit(solution)/shard_map/concatenate | solution.py:452
  626.4 155.6 %reduce-scatter.6.cloned.1.call-done = bf16[48,4736]{1,0:T(8,128)(2,1)} async-done(((bf16[1536,4736]{1,0:T(8,128)(2,1)}), bf16[48,4736]{1,0:T(8,128)(2,1)}) %reduce-scatter.6.cloned.1.call-update) | async-done | bytes 454672 | tf_op jit(solution)/shard_map/reduce_scatter | solution.py:451
  (155 shorter events, 93.3 us)
Async XLA Ops:
  7.2 6.7 copy-start.21
  7.2 124.7 %all-gather.4.cloned.1.call-start = ((), (), s32[]{:S(2)}) async-start(), calls=%async_computation.5 | async-start | bytes 15003648 | tf_op jit(solution)/shard_map/all_gather | solution.py:291
  12.5 240.1 %all-gather.6.cloned.1.call-start = ((), (), s32[]{:S(2)}) async-start(), calls=%async_computation.6 | async-start | bytes 7077888 | tf_op jit(solution)/shard_map/all_gather | solution.py:336
  14.2 21.1 %copy-start.22 = (s32[1,8]{1,0:T(1,128)S(1)}, s32[1,8]{1,0:T(1,128)}, u32[]{:S(2)}) copy-start(s32[1,8]{1,0:T(1,128)} %param.15) | copy-start | bytes 100
  14.2 21.3 %copy-start.5 = (bf16[1,128,1536]{2,1,0:T(8,128)(2,1)S(1)}, bf16[1,128,1536]{2,1,0:T(8,128)(2,1)}, u32[]{:S(2)}) copy-start(bf16[1,128,1536]{2,1,0:T(8,128)(2,1)} %param.14) | copy-start | bytes 1179652
  34.5 299.5 %all-gather.8.cloned.1.call-start = ((), (), s32[]{:S(2)}) async-start(), calls=%async_computation.7 | async-start | bytes 3538944 | tf_op jit(solution)/shard_map/all_gather | solution.py:337
  35.3 551.7 %reduce-scatter.4.cloned.1.call-start = ((), (), s32[]{:S(2)}) async-start(), calls=%async_computation.8 | async-start | bytes 7077888 | tf_op jit(solution)/shard_map/reduce_scatter | solution.py:396
  196.2 7.2 copy-start.10
  198.9 4.5 copy-start.13
  203.4 3.2 copy-start.9
  208.1 3.4 copy-start.11
  211.5 231.0 %copy-start.4 = (f32[128,1536]{1,0:T(8,128)}, f32[128,1536]{1,0:T(8,128)S(1)}, u32[]{:S(2)}) copy-start(f32[128,1536]{1,0:T(8,128)S(1)} %get-tuple-element.68) | copy-start | bytes 2359300
  341.1 2.1 copy-start.15
  348.8 274.4 %reduce-scatter.8.cloned.1.call-start = ((), (), s32[]{:S(2)}) async-start(), calls=%async_computation.10 | async-start | bytes 3538944 | tf_op jit(solution)/shard_map/reduce_scatter | solution.py:385
  460.1 5.6 copy-start.14
  473.9 3.2 copy-start
  477.1 2.1 copy-start.1
  480.6 92.7 %copy-start.3 = (bf16[128,8,2,640]{0,3,2,1:T(8,128)(2,1)S(1)}, bf16[128,8,2,640]{0,3,2,1:T(8,128)(2,1)}, u32[]{:S(2)}) copy-start(bf16[128,8,2,640]{0,3,2,1:T(8,128)(2,1)} %copy-done.2) | copy-start | bytes 7864324
  573.3 2.1 copy-start.20
  575.4 7.9 copy-start.12
  586.9 6.0 copy-start.8
  586.9 6.0 copy-start.19
  586.9 15.3 %all-to-all-start.1 = ((bf16[4,48,2048]{2,1,0:T(8,128)(2,1)}), bf16[4,48,2048]{2,1,0:T(8,128)(2,1)S(1)}, u32[]{:S(2)}, u32[]{:S(2)}) async-start(bf16[4,48,2048]{2,1,0:T(8,128)(2,1)} %bitcast.152), calls=%async_computation.2 | async-start | bytes 1572864 | tf_op jit(solution)/shard_map/all_to_all | solution.py:397
  590.6 191.4 %reduce-scatter.6.cloned.1.call-start = ((), (), s32[]{:S(2)}) async-start(), calls=%async_computation.9 | async-start | bytes 15003648 | tf_op jit(solution)/shard_map/reduce_scatter | solution.py:451
  (7 other events, 9.9 us)
Sparse Core Ops, SparseCore 0:
  12.6 119.2 all-gather.3
  134.6 117.9 all-gather.5
  254.8 79.1 all-gather.7
  348.9 116.5 reduce-scatter.3
  468.9 99.6 reduce-scatter.7
  621.0 160.9 reduce-scatter.5

commit v5 on v4

--- a/solution.py
+++ b/solution.py
@@ -262,6 +262,123 @@
     )(p)
 
 
+def pair_barrier(c, partner, across):
+    barrier = pltpu.get_barrier_semaphore()
+    pl.semaphore_signal(barrier, inc=1, device_id=(c, partner), device_id_type=MESH)
+    pl.semaphore_signal(barrier, inc=1, device_id=(c, across), device_id_type=MESH)
+    pl.semaphore_wait(barrier, 2)
+
+
+def quad_ids():
+    c = lax.axis_index("ctx")
+    f = lax.axis_index("fsdp")
+    partner = f + 1 - 2 * (f % 2)
+    across = (f + 2) % 4
+    diagonal = (partner + 2) % 4
+    return c, f, partner, across, diagonal
+
+
+def quad_gather_kernel(x_ref, out_ref, send_sem, recv_sem):
+    c, f, partner, across, diagonal = quad_ids()
+    pair_barrier(c, partner, across)
+
+    def copy(src, slot, dest, k):
+        return pltpu.make_async_remote_copy(
+            src_ref=src,
+            dst_ref=out_ref.at[slot],
+            send_sem=send_sem.at[k],
+            recv_sem=recv_sem.at[slot],
+            device_id=(c, dest),
+            device_id_type=MESH,
+        )
+
+    first = copy(x_ref, f, across, 0)
+    first.start()
+    own = copy(x_ref, f, partner, 1)
+    own.start()
+    out_ref[f] = x_ref[...]
+    copy(x_ref, across, f, 0).wait_recv()
+    relay = copy(out_ref.at[across], across, partner, 2)
+    relay.start()
+    copy(x_ref, partner, f, 0).wait_recv()
+    copy(x_ref, diagonal, f, 0).wait_recv()
+    first.wait_send()
+    own.wait_send()
+    relay.wait_send()
+
+
+def quad_gather(x):
+    return pl.pallas_call(
+        quad_gather_kernel,
+        out_shape=jax.ShapeDtypeStruct((4,) + x.shape, x.dtype),
+        in_specs=[pl.BlockSpec(memory_space=pltpu.VMEM)],
+        out_specs=pl.BlockSpec(memory_space=pltpu.VMEM),
+        scratch_shapes=[pltpu.SemaphoreType.DMA((3,)), pltpu.SemaphoreType.DMA((4,))],
+        compiler_params=pltpu.CompilerParams(collective_id=4, has_side_effects=True),
+    )(x)
+
+
+def quad_reduce_kernel(p_ref, out_ref, near_buf, far_buf, sum_buf, send_sem, recv_sem):
+    c, f, partner, across, diagonal = quad_ids()
+    pair_barrier(c, partner, across)
+
+    def copy(src, dst, dest, k):
+        return pltpu.make_async_remote_copy(
+            src_ref=src,
+            dst_ref=dst,
+            send_sem=send_sem.at[k],
+            recv_sem=recv_sem.at[k],
+            device_id=(c, dest),
+            device_id_type=MESH,
+        )
+
+    to_partner = copy(p_ref.at[partner], near_buf.at[0], partner, 0)
+    to_partner.start()
+    to_diagonal = copy(p_ref.at[diagonal], near_buf.at[1], partner, 1)
+    to_diagonal.start()
+    to_partner.wait_recv()
+    to_diagonal.wait_recv()
+    sum_buf[...] = p_ref[across] + near_buf[1]
+    to_across = copy(sum_buf, far_buf, across, 2)
+    to_across.start()
+    out_ref[...] = p_ref[f] + near_buf[0]
+    to_across.wait_recv()
+    out_ref[...] += far_buf[...]
+    to_partner.wait_send()
+    to_diagonal.wait_send()
+    to_across.wait_send()
+
+
+def quad_reduce(p):
+    block = p.shape[1:]
+    return pl.pallas_call(
+        quad_reduce_kernel,
+        out_shape=jax.ShapeDtypeStruct(block, p.dtype),
+        in_specs=[pl.BlockSpec(memory_space=pltpu.VMEM)],
+        out_specs=pl.BlockSpec(memory_space=pltpu.VMEM),
+        scratch_shapes=[
+            pltpu.VMEM((2,) + block, p.dtype),
+            pltpu.VMEM(block, p.dtype),
+            pltpu.VMEM(block, p.dtype),
+            pltpu.SemaphoreType.DMA((3,)),
+            pltpu.SemaphoreType.DMA((3,)),
+        ],
+        compiler_params=pltpu.CompilerParams(collective_id=5, has_side_effects=True),
+    )(p)
+
+
+def fsdp_gather(x, n_f):
+    if n_f == 4:
+        return quad_gather(x)
+    return group_gather(x, n_f)
+
+
+def fsdp_reduce(p, n_f):
+    if n_f == 4:
+        return quad_reduce(p)
+    return group_reduce(p, n_f)
+
+
 def body(
     tokens,
     doc_lengths,
@@ -333,8 +450,15 @@
         (3, 0, 1, 2, 4),
     )
     gu_parts = lax.all_to_all(gu_parts, "fsdp", 0, 0, tiled=True).reshape(n_f * rows, 2 * units)
-    gate_up_tp = lax.all_gather(gu_parts, "ctx", axis=0, tiled=True)
-    down_tp = lax.all_gather(down_weight, "ctx", axis=0, tiled=True)
+    down_rows = D // (2 * n_ctx)
+    ff_stack = lax.all_gather(
+        jnp.concatenate([gu_parts, down_weight.reshape(down_rows, 2 * units)], axis=0),
+        "ctx",
+        axis=0,
+        tiled=False,
+    )
+    gate_up_tp = ff_stack[:, : n_f * rows].reshape(n_ctx * n_f * rows, 2 * units)
+    down_tp = ff_stack[:, n_f * rows :].reshape(n_ctx, ff_rows, D).reshape(units, D)
     max_doc = min(DOC_MOST, KBLK * (stream_len // (2 * KBLK)))
     back = min(-(-(max_doc - 1) // tok_rows), n_ctx - 1)
     win = (back + 1) * tok_rows
@@ -371,17 +495,17 @@
     normed_two = middle * scale_two
     normed_two_low = (normed_two * gain_two_f).astype(jnp.bfloat16)
     group_tokens = n_f * tok_rows
-    xn2_all = group_gather(normed_two_low, n_f).reshape(group_tokens, D)
+    xn2_all = fsdp_gather(normed_two_low, n_f).reshape(group_tokens, D)
     gate_up = jnp.dot(xn2_all, gate_up_tp, preferred_element_type=jnp.float32)
     gate_pre = gate_up[:, :units]
     up_pre = gate_up[:, units:]
     sigmoid = jax.nn.sigmoid(gate_pre)
     hidden_low = (gate_pre * sigmoid * up_pre).astype(jnp.bfloat16)
     ff_part = jnp.dot(hidden_low, down_tp, preferred_element_type=jnp.float32)
-    layer_out = middle + group_reduce(ff_part.reshape(n_f, tok_rows, D), n_f)
+    layer_out = middle + fsdp_reduce(ff_part.reshape(n_f, tok_rows, D), n_f)
 
     grad_out = cotangent[0]
-    grad_all = group_gather(grad_out, n_f).reshape(group_tokens, D)
+    grad_all = fsdp_gather(grad_out, n_f).reshape(group_tokens, D)
     down_sum = lax.psum_scatter(
         outer_rows(hidden_low, grad_all).astype(jnp.bfloat16), "ctx", scatter_dimension=0, tiled=True
     )
@@ -398,7 +522,7 @@
     ff_sum = jnp.transpose(
         gu_sum.reshape(n_f, rows, 2, n_ctx, chunk), (1, 2, 3, 0, 4)
     ).reshape(rows, 2 * ff)
-    normed_two_grad = group_reduce(
+    normed_two_grad = fsdp_reduce(
         times_transposed(gate_up_cat, gate_up_tp).reshape(n_f, tok_rows, D), n_f
     )
     gain_two_term = jnp.sum(normed_two_grad * normed_two, axis=0)

time: 800 us -> 838 us (1.048)
  waiting for transfers between devices: 318 us -> 385 us
  Pallas kernels: 265 us -> 224 us
  local copies, waits for them, and re-layouts: 41.3 us -> 65.6 us
  blocking collectives: 18.9 us -> 0 us
    pallas_call x4, Pallas kernels: 128 us -> 80.7 us  [the longest x2 52.6 us: quad_reduce(): pl.pallas_call(quad_reduce_kernel, out_shape=jax.ShapeDtypeStruct(block,...]
    all_gather x2 -> x1, waiting for transfers between devices: 91.5 us -> 121 us  [body(): lax.all_gather(jnp.concatenate([gu_parts, down_weight.reshape(down_rows,...]
    pallas_call x1, Pallas kernels: 84.5 us -> 113 us  [kv_return(): pl.pallas_call(functools.partial(kv_return_kernel, n_ctx, back), out_shap...]
    all_gather x1, waiting for transfers between devices: 66.5 us -> 94.2 us  [body(): lax.all_gather(jnp.concatenate([query_weight, key_weight, value_weight, o...]
    pallas_call x1, Pallas kernels: 52.8 us -> 30.4 us  [kv_share(): pl.pallas_call(functools.partial(kv_share_kernel, n_ctx, back), out_shape...]
    all_to_all x1 -> x0, blocking collectives: 18.9 us -> none  [body(): lax.all_to_all(gu_parts, 'fsdp', 0, 0, tiled=True)]
    all_to_all x0 -> x1, waiting for transfers between devices: none -> 11.2 us  [body(): lax.all_to_all(gu_parts, 'fsdp', 0, 0, tiled=True)]
    slice x0 -> x2, local copies, waits for them, and re-layouts: none -> 8.76 us  [the longest x1 6.65 us: body(): gate_up_tp = ff_stack[:, :n_f * rows].reshape(n_ctx * n_f * rows, 2 * units)]
  transfers between devices with their start and end apart: 7 -> 7, of which waited for: 5 -> 5; matrix products, arithmetic and copies ran while one was open for 18% -> 14% of each run, Pallas kernels for 33% -> 22%
where the time goes in v5:
time: 838 us; the launch traced here: 831 us
  waiting for transfers between devices  385 us (46%)
  Pallas kernels  224 us (27%)
  matrix products  83.2 us (10%)
  local copies, waits for them, and re-layouts  65.6 us (8%)
  other arithmetic  47.4 us (6%)
  between operations  16.9 us (2%)
    reduce_scatter x1, waiting for transfers between devices, body(): lax.psum_scatter(jnp.concatenate([outer_rows(normed_low, projection_cat)....  156 us
    all_gather x1, waiting for transfers between devices, body(): lax.all_gather(jnp.concatenate([gu_parts, down_weight.reshape(down_rows,...  121 us
    pallas_call x1, Pallas kernels, kv_return(): pl.pallas_call(functools.partial(kv_return_kernel, n_ctx, back), out_shap...  113 us
    all_gather x1, waiting for transfers between devices, body(): lax.all_gather(jnp.concatenate([query_weight, key_weight, value_weight, o...  94.2 us
    pallas_call x2, Pallas kernels, quad_reduce(): pl.pallas_call(quad_reduce_kernel, out_shape=jax.ShapeDtypeStruct(block,...  52.6 us
    pallas_call x1, Pallas kernels, kv_share(): pl.pallas_call(functools.partial(kv_share_kernel, n_ctx, back), out_shape...  30.4 us
    pallas_call x2, Pallas kernels, quad_gather(): pl.pallas_call(quad_gather_kernel, out_shape=jax.ShapeDtypeStruct((4,) +...  28 us
    dot_general x4, matrix products, times_transposed(): lax.dot_general(left, right, (((1,), (1,)), ((), ())), preferred_element_...  23.4 us
  transfers between devices with their start and end apart: 7, of which 5 were waited for; matrix products, arithmetic and copies ran while one was open for 14% of the time, Pallas kernels for 22%

profile of v5, /device:TPU:0, one launch (start us, length us, event | category | flops | bytes accessed | tf_op | source)
XLA Modules:
  0.0 830.6 jit_solution(4149562186774655815)
XLA Ops:
  10.9 4.2 all-to-all-start
  15.6 11.2 %all-to-all-done = bf16[4,48,2,8,128]{4,3,2,1,0:T(8,128)(2,1)S(1)} async-done(((bf16[4,48,2,8,128]{4,3,2,1,0:T(8,128)(2,1)}), bf16[4,48,2,8,128]{4,3,2,1,0:T(8,128)(2,1)S(1)}, u32[]{:S(2)}, u32[]{:S(2)}) %all-to-all-start) | async-done | bytes 786464 | tf_op jit(solution)/shard_map/all_to_all | solution.py:452
  29.7 14.0 %shard_map.206 = bf16[4,128,1536]{2,1,0:T(8,128)(2,1)} custom-call(bf16[128,1536]{1,0:T(8,128)(2,1)} %bitcast.171), custom_call_target="tpu_custom_call" | custom-call | tf_op jit(solution)/shard_map/pallas_call | solution.py:311
  46.4 121.2 %all-gather.6.cloned.1.call-done = bf16[2304,2048]{1,0:T(8,128)(2,1)} async-done(((bf16[288,2048]{1,0:T(8,128)(2,1)}), bf16[2304,2048]{1,0:T(8,128)(2,1)}) %all-gather.6.cloned.1.call-update) | async-done | bytes 9437200 | tf_op jit(solution)/shard_map/all_gather | solution.py:454
  169.7 6.6 slice.178
  180.0 94.2 %all-gather.4.cloned.1.call-done = bf16[1536,4736]{1,0:T(8,128)(2,1)} async-done(((bf16[48,4736]{1,0:T(8,128)(2,1)}), bf16[1536,4736]{1,0:T(8,128)(2,1)}) %all-gather.4.cloned.1.call-update) | async-done | bytes 14549008 | tf_op jit(solution)/shard_map/all_gather | solution.py:408
  275.7 5.2 fusion.3
  294.8 30.4 %shard_map.203 = bf16[5,128,1536]{2,1,0:T(8,128)(2,1)} custom-call(bf16[128,1536]{1,0:T(8,128)(2,1)} %pad_maximum_fusion.5.kv_ref), custom_call_target="tpu_custom_call" | custom-call | tf_op jit(solution)/shard_map/pallas_call | solution.py:116
  334.4 6.4 fusion.57
  350.9 14.1 %shard_map.204 = bf16[4,128,1536]{2,1,0:T(8,128)(2,1)} custom-call(bf16[128,1536]{1,0:T(8,128)(2,1)} %multiply_convert_fusion.1.x_ref), custom_call_target="tpu_custom_call" | custom-call | tf_op jit(solution)/shard_map/pallas_call | solution.py:311
  365.0 6.1 fusion.59
  376.7 5.5 convolution_convert_fusion.1
  387.4 5.7 fusion.60.p_ref
  393.1 26.3 %shard_map.205 = f32[128,1536]{1,0:T(8,128)} custom-call(f32[4,128,1536]{2,1,0:T(8,128)} %fusion.60.p_ref), custom_call_target="tpu_custom_call" | custom-call | tf_op jit(solution)/shard_map/pallas_call | solution.py:354
  419.5 7.9 fusion.61.p_ref
  427.4 26.3 %shard_map.207 = f32[128,1536]{1,0:T(8,128)} custom-call(f32[4,128,1536]{2,1,0:T(8,128)} %fusion.61.p_ref), custom_call_target="tpu_custom_call" | custom-call | tf_op jit(solution)/shard_map/pallas_call | solution.py:354
  457.4 4.1 fusion.19
  461.7 5.1 convolution_convert_fusion.3
  468.3 3.7 fusion.6
  488.6 112.8 %shard_map.208 = f32[128,1536]{1,0:T(8,128)} custom-call(f32[128,1536]{1,0:T(8,128)} %fusion.40.own_ref, bf16[4,128,1536]{2,1,0:T(8,128)(2,1)} %bitcast.145), custom_call_target="tpu_custom_call" | custom-call | tf_op jit(solution)/shard_map/pallas_call | solution.py:163
  611.9 7.9 fusion.38
  629.3 6.1 convolution_convert_fusion
  644.2 12.9 %pad_maximum_fusion = bf16[1536,4736]{1,0:T(8,128)(2,1)} fusion(bf16[1536,128]{1,0:T(8,128)(2,1)S(1)} %scatter.4, bf16[1536,1536]{1,0:T(8,128)(2,1)} %convolution_convert_fusion.2, bf16[1536,3072]{1,0:T(8,128)(2,1)} %convolution_convert_fusion), kind=kLoop, calls=%fused_computation.1 | loop fusion | flops 43646976 | bytes 29097984 | tf_op jit(solution)/shard_map/concatenate | solution.py:576
  662.7 155.6 %reduce-scatter.6.cloned.1.call-done = bf16[48,4736]{1,0:T(8,128)(2,1)} async-done(((bf16[1536,4736]{1,0:T(8,128)(2,1)}), bf16[48,4736]{1,0:T(8,128)(2,1)}) %reduce-scatter.6.cloned.1.call-update) | async-done | bytes 454672 | tf_op jit(solution)/shard_map/reduce_scatter | solution.py:575
  (197 shorter events, 120.1 us)
Async XLA Ops:
  7.2 8.0 copy-start.30
  10.9 15.9 %all-to-all-start = ((bf16[4,48,2,8,128]{4,3,2,1,0:T(8,128)(2,1)}), bf16[4,48,2,8,128]{4,3,2,1,0:T(8,128)(2,1)S(1)}, u32[]{:S(2)}, u32[]{:S(2)}) async-start(bf16[4,48,2,8,128]{4,3,2,1,0:T(8,128)(2,1)} %maximum_bitcast_fusion), calls=%async_computation | async-start | bytes 1572864 | tf_op jit(solution)/shard_map/all_to_all | solution.py:452
  15.1 13.3 %copy-start.38 = (bf16[48]{0:T(256)(128)(2,1)S(1)}, bf16[48]{0:T(256)(128)(2,1)}, u32[]{:S(2)}) copy-start(bf16[48]{0:T(256)(128)(2,1)} %param.21) | copy-start | bytes 292
  15.1 13.3 %copy-start.39 = (bf16[48]{0:T(256)(128)(2,1)S(1)}, bf16[48]{0:T(256)(128)(2,1)}, u32[]{:S(2)}) copy-start(bf16[48]{0:T(256)(128)(2,1)} %param.16) | copy-start | bytes 292
  15.1 13.4 %copy-start.32 = (bf16[48,1536]{1,0:T(8,128)(2,1)S(1)}, bf16[48,1536]{1,0:T(8,128)(2,1)}, u32[]{:S(2)}) copy-start(bf16[48,1536]{1,0:T(8,128)(2,1)} %param.17) | copy-start | bytes 442372
  15.1 13.4 %copy-start.34 = (bf16[48,768]{1,0:T(8,128)(2,1)S(1)}, bf16[48,768]{1,0:T(8,128)(2,1)}, u32[]{:S(2)}) copy-start(bf16[48,768]{1,0:T(8,128)(2,1)} %param.18) | copy-start | bytes 221188
  15.1 13.4 %copy-start.35 = (bf16[48,768]{1,0:T(8,128)(2,1)S(1)}, bf16[48,768]{1,0:T(8,128)(2,1)}, u32[]{:S(2)}) copy-start(bf16[48,768]{1,0:T(8,128)(2,1)} %param.19) | copy-start | bytes 221188
  15.1 13.4 %copy-start.33 = (bf16[48,1536]{1,0:T(8,128)(2,1)S(1)}, bf16[48,1536]{1,0:T(8,128)(2,1)}, u32[]{:S(2)}) copy-start(bf16[48,1536]{1,0:T(8,128)(2,1)} %param.20) | copy-start | bytes 442372
  15.2 152.4 %all-gather.6.cloned.1.call-start = ((), (), s32[]{:S(2)}) async-start(), calls=%async_computation.9 | async-start | bytes 10616832 | tf_op jit(solution)/shard_map/all_gather | solution.py:454
  15.5 13.9 %copy-start.40 = (s32[1,8]{1,0:T(1,128)S(1)}, s32[1,8]{1,0:T(1,128)}, u32[]{:S(2)}) copy-start(s32[1,8]{1,0:T(1,128)} %param.15) | copy-start | bytes 100
  27.1 16.9 %copy-start.8 = (bf16[1,128,1536]{2,1,0:T(8,128)(2,1)S(1)}, bf16[1,128,1536]{2,1,0:T(8,128)(2,1)}, u32[]{:S(2)}) copy-start(bf16[1,128,1536]{2,1,0:T(8,128)(2,1)} %param.14) | copy-start | bytes 1179652
  28.3 245.9 %all-gather.4.cloned.1.call-start = ((), (), s32[]{:S(2)}) async-start(), calls=%async_computation.5 | async-start | bytes 15003648 | tf_op jit(solution)/shard_map/all_gather | solution.py:408
  29.4 593.9 %reduce-scatter.4.cloned.1.call-start = ((), (), s32[]{:S(2)}) async-start(), calls=%async_computation.6 | async-start | bytes 7077888 | tf_op jit(solution)/shard_map/reduce_scatter | solution.py:520
  382.2 277.3 %reduce-scatter.8.cloned.1.call-start = ((), (), s32[]{:S(2)}) async-start(), calls=%async_computation.8 | async-start | bytes 3538944 | tf_op jit(solution)/shard_map/reduce_scatter | solution.py:509
  393.1 26.3 %copy-start.19 = (bf16[512,2048]{1,0:T(8,128)(2,1)S(1)}, bf16[512,2048]{1,0:T(8,128)(2,1)}, u32[]{:S(2)}) copy-start(bf16[512,2048]{1,0:T(8,128)(2,1)} %pad_maximum_fusion.2) | copy-start | bytes 6291460
  427.4 26.4 %copy-start.7 = (f32[128,1536]{1,0:T(8,128)S(1)}, f32[128,1536]{1,0:T(8,128)}, u32[]{:S(2)}) copy-start(f32[128,1536]{1,0:T(8,128)} %copy-done.6) | copy-start | bytes 2359300
  427.4 27.8 %copy-start.16 = (f32[128,1536]{1,0:T(8,128)S(1)}, f32[128,1536]{1,0:T(8,128)}, u32[]{:S(2)}) copy-start(f32[128,1536]{1,0:T(8,128)} %shard_map.205) | copy-start | bytes 2359300
  427.4 27.8 %copy-start.23 = (bf16[1,128,1536]{2,1,0:T(8,128)(2,1)S(1)}, bf16[1,128,1536]{2,1,0:T(8,128)(2,1)}, u32[]{:S(2)}) copy-start(bf16[1,128,1536]{2,1,0:T(8,128)(2,1)} %param.25) | copy-start | bytes 1179652
  488.6 119.9 %copy-start.29 = (f32[128,48]{0,1:T(8,128)S(1)}, f32[128,48]{0,1:T(8,128)}, u32[]{:S(2)}) copy-start(f32[128,48]{0,1:T(8,128)} %get-tuple-element.60) | copy-start | bytes 73732
  488.6 119.9 %copy-start.31 = (f32[128,48]{0,1:T(8,128)S(1)}, f32[128,48]{0,1:T(8,128)}, u32[]{:S(2)}) copy-start(f32[128,48]{0,1:T(8,128)} %get-tuple-element.58) | copy-start | bytes 73732
  488.6 121.1 %copy-start.5 = (bf16[128,8,2,640]{0,3,2,1:T(8,128)(2,1)S(1)}, bf16[128,8,2,640]{0,3,2,1:T(8,128)(2,1)}, u32[]{:S(2)}) copy-start(bf16[128,8,2,640]{0,3,2,1:T(8,128)(2,1)} %copy-done.4) | copy-start | bytes 7864324
  611.9 7.9 copy-start.18
  623.3 15.3 %all-to-all-start.1 = ((bf16[4,48,2048]{2,1,0:T(8,128)(2,1)}), bf16[4,48,2048]{2,1,0:T(8,128)(2,1)S(1)}, u32[]{:S(2)}, u32[]{:S(2)}) async-start(bf16[4,48,2048]{2,1,0:T(8,128)(2,1)} %bitcast.172), calls=%async_computation.2 | async-start | bytes 1572864 | tf_op jit(solution)/shard_map/all_to_all | solution.py:521
  626.9 191.4 %reduce-scatter.6.cloned.1.call-start = ((), (), s32[]{:S(2)}) async-start(), calls=%async_computation.7 | async-start | bytes 15003648 | tf_op jit(solution)/shard_map/reduce_scatter | solution.py:575
  (26 other events, 80.0 us)
Sparse Core Ops, SparseCore 0:
  28.4 139.0 all-gather.5
  171.0 103.1 all-gather.3
  382.4 143.7 reduce-scatter.3
  529.6 108.9 reduce-scatter.7
  657.3 160.9 reduce-scatter.5

commit v6 on v5

--- a/solution.py
+++ b/solution.py
@@ -451,8 +451,10 @@
     )
     gu_parts = lax.all_to_all(gu_parts, "fsdp", 0, 0, tiled=True).reshape(n_f * rows, 2 * units)
     down_rows = D // (2 * n_ctx)
+    ff_pack = jnp.concatenate([gu_parts, down_weight.reshape(down_rows, 2 * units)], axis=0)
+    ff_pack = ff_pack.at[0, 0].add(att_full[0, 0] * 0)
     ff_stack = lax.all_gather(
-        jnp.concatenate([gu_parts, down_weight.reshape(down_rows, 2 * units)], axis=0),
+        ff_pack,
         "ctx",
         axis=0,
         tiled=False,

time: 838 us -> 768 us (0.916)
  waiting for transfers between devices: 385 us -> 299 us
  Pallas kernels: 224 us -> 256 us
    all_gather x1, waiting for transfers between devices: 121 us -> 39.4 us  [body(): ff_stack = lax.all_gather(ff_pack, 'ctx', axis=0, tiled=False)]
    pallas_call x1, Pallas kernels: 30.4 us -> 48.8 us  [kv_share(): pl.pallas_call(functools.partial(kv_share_kernel, n_ctx, back), out_shape...]
    pallas_call x1, Pallas kernels: 113 us -> 125 us  [kv_return(): pl.pallas_call(functools.partial(kv_return_kernel, n_ctx, back), out_shap...]
  transfers between devices with their start and end apart: 7 -> 7, of which waited for: 5 -> 5; matrix products, arithmetic and copies ran while one was open for 14% -> 18% of each run, Pallas kernels for 22% -> 34%
where the time goes in v6:
time: 768 us; the launch traced here: 761 us
  waiting for transfers between devices  299 us (39%)
  Pallas kernels  256 us (33%)
  matrix products  79.5 us (10%)
  local copies, waits for them, and re-layouts  59.1 us (8%)
  other arithmetic  41.1 us (5%)
  between operations  18.3 us (2%)
  starting transfers between devices  8 us (1%)
    reduce_scatter x1, waiting for transfers between devices, body(): lax.psum_scatter(jnp.concatenate([outer_rows(normed_low, projection_cat)....  156 us
    pallas_call x1, Pallas kernels, kv_return(): pl.pallas_call(functools.partial(kv_return_kernel, n_ctx, back), out_shap...  125 us
    all_gather x1, waiting for transfers between devices, body(): lax.all_gather(jnp.concatenate([query_weight, key_weight, value_weight, o...  85.9 us
    pallas_call x2, Pallas kernels, quad_reduce(): pl.pallas_call(quad_reduce_kernel, out_shape=jax.ShapeDtypeStruct(block,...  52.3 us
    pallas_call x1, Pallas kernels, kv_share(): pl.pallas_call(functools.partial(kv_share_kernel, n_ctx, back), out_shape...  48.8 us
    all_gather x1, waiting for transfers between devices, body(): ff_stack = lax.all_gather(ff_pack, 'ctx', axis=0, tiled=False)  39.4 us
    pallas_call x2, Pallas kernels, quad_gather(): pl.pallas_call(quad_gather_kernel, out_shape=jax.ShapeDtypeStruct((4,) +...  29.9 us
    dot_general x4, matrix products, times_transposed(): lax.dot_general(left, right, (((1,), (1,)), ((), ())), preferred_element_...  23.4 us
  transfers between devices with their start and end apart: 7, of which 5 were waited for; matrix products, arithmetic and copies ran while one was open for 18% of the time, Pallas kernels for 34%

profile of v6, /device:TPU:0, one launch (start us, length us, event | category | flops | bytes accessed | tf_op | source)
XLA Modules:
  0.0 761.1 jit_solution(10716521596167144800)
XLA Ops:
  16.6 4.2 all-to-all-start
  21.2 14.6 %all-to-all-done = bf16[4,48,2,8,128]{4,3,1,2,0:T(8,128)(2,1)S(1)} async-done(((bf16[4,48,2,8,128]{4,3,1,2,0:T(8,128)(2,1)}), bf16[4,48,2,8,128]{4,3,1,2,0:T(8,128)(2,1)S(1)}, u32[]{:S(2)}, u32[]{:S(2)}) %all-to-all-start) | async-done | bytes 786464 | tf_op jit(solution)/shard_map/all_to_all | solution.py:452
  36.9 85.9 %all-gather.3.cloned.1.call-done = bf16[1536,4736]{1,0:T(8,128)(2,1)} async-done(((bf16[48,4736]{1,0:T(8,128)(2,1)}), bf16[1536,4736]{1,0:T(8,128)(2,1)}) %all-gather.3.cloned.1.call-update) | async-done | bytes 14549008 | tf_op jit(solution)/shard_map/all_gather | solution.py:408
  126.6 14.8 %shard_map.206 = bf16[4,128,1536]{2,1,0:T(8,128)(2,1)} custom-call(bf16[128,1536]{1,0:T(8,128)(2,1)} %bitcast.171), custom_call_target="tpu_custom_call" | custom-call | tf_op jit(solution)/shard_map/pallas_call | solution.py:311
  145.2 5.2 fusion.3
  152.9 48.8 %shard_map.203 = bf16[5,128,1536]{2,1,0:T(8,128)(2,1)} custom-call(bf16[128,1536]{1,0:T(8,128)(2,1)} %pad_maximum_fusion.4.kv_ref), custom_call_target="tpu_custom_call" | custom-call | tf_op jit(solution)/shard_map/pallas_call | solution.py:116
  206.3 5.6 fusion.57
  222.0 15.1 %shard_map.204 = bf16[4,128,1536]{2,1,0:T(8,128)(2,1)} custom-call(bf16[128,1536]{1,0:T(8,128)(2,1)} %multiply_convert_fusion.1.x_ref), custom_call_target="tpu_custom_call" | custom-call | tf_op jit(solution)/shard_map/pallas_call | solution.py:311
  237.1 39.4 %all-gather.5.cloned.1.call-done = bf16[8,288,2048]{2,1,0:T(8,128)(2,1)} async-done(((bf16[1,288,2048]{2,1,0:T(8,128)(2,1)}), bf16[8,288,2048]{2,1,0:T(8,128)(2,1)}) %all-gather.5.cloned.1.call-update) | async-done | bytes 9437200 | tf_op jit(solution)/shard_map/all_gather | solution.py:456
  278.6 3.7 reshape_reshape.3
  295.4 5.5 convolution_convert_fusion.1
  302.2 3.9 reshape.379
  306.1 5.6 fusion.60.p_ref
  311.8 26.3 %shard_map.205 = f32[128,1536]{1,0:T(8,128)} custom-call(f32[4,128,1536]{2,1,0:T(8,128)} %fusion.60.p_ref), custom_call_target="tpu_custom_call" | custom-call | tf_op jit(solution)/shard_map/pallas_call | solution.py:354
  338.1 7.9 %fusion.61.p_ref = f32[4,128,1536]{2,1,0:T(8,128)} fusion(bf16[4,128,2048]{2,1,0:T(8,128)(2,1)S(1)} %bitcast.160, bf16[1536,2048,1]{1,0,2:T(8,128)(2,1)} %bitcast.144), kind=kOutput, calls=%fused_computation.134 | convolution fusion | flops 3221225472 | bytes 11534336 | tf_op jit(solution)/shard_map/dot_general | solution.py:63
  345.9 26.1 %shard_map.207 = f32[128,1536]{1,0:T(8,128)} custom-call(f32[4,128,1536]{2,1,0:T(8,128)} %fusion.61.p_ref), custom_call_target="tpu_custom_call" | custom-call | tf_op jit(solution)/shard_map/pallas_call | solution.py:354
  375.7 4.1 fusion.19
  380.1 5.0 convolution_convert_fusion.3
  386.5 3.7 fusion.6
  406.7 125.2 %shard_map.208 = f32[128,1536]{1,0:T(8,128)} custom-call(f32[128,1536]{1,0:T(8,128)} %fusion.40.own_ref, bf16[4,128,1536]{2,1,0:T(8,128)(2,1)} %bitcast.145), custom_call_target="tpu_custom_call" | custom-call | tf_op jit(solution)/shard_map/pallas_call | solution.py:163
  542.3 7.9 %fusion.38 = (bf16[1536]{0:T(1024)(128)(2,1)S(1)}, f32[128]{0:T(128)S(1)}, f32[128,1536]{1,0:T(8,128)}) fusion(bf16[1,128,1536]{2,1,0:T(8,128)(2,1)S(1)} %copy-done.11, f32[128]{0:T(128)S(1)} %copy-done.39, f32[1536]{0:T(1024)S(1)} %get-tuple-element.40, bf16[1536,4736]{1,0:T(8,128)(2,1)} %all-gather.3.cloned.1.call-done, ...), kind=kOutput, calls=%fused_computation.56 | convolution fusion | flops 1211693440 | bytes 11413504 | tf_op jit(solution)/shard_map/dot_general | solution.py:63
  559.7 6.1 convolution_convert_fusion
  574.7 12.9 %pad_maximum_fusion = bf16[1536,4736]{1,0:T(8,128)(2,1)} fusion(bf16[1536,128]{1,0:T(8,128)(2,1)S(1)} %scatter.4, bf16[1536,1536]{1,0:T(8,128)(2,1)} %convolution_convert_fusion.2, bf16[1536,3072]{1,0:T(8,128)(2,1)} %convolution_convert_fusion), kind=kLoop, calls=%fused_computation.1 | loop fusion | flops 43646976 | bytes 29097984 | tf_op jit(solution)/shard_map/concatenate | solution.py:578
  593.2 155.7 %reduce-scatter.6.cloned.1.call-done = bf16[48,4736]{1,0:T(8,128)(2,1)} async-done(((bf16[1536,4736]{1,0:T(8,128)(2,1)}), bf16[48,4736]{1,0:T(8,128)(2,1)}) %reduce-scatter.6.cloned.1.call-update) | async-done | bytes 454672 | tf_op jit(solution)/shard_map/reduce_scatter | solution.py:577
  (200 shorter events, 109.6 us)
Async XLA Ops:
  7.2 115.6 %all-gather.3.cloned.1.call-start = ((), (), s32[]{:S(2)}) async-start(), calls=%async_computation.5 | async-start | bytes 15003648 | tf_op jit(solution)/shard_map/all_gather | solution.py:408
  12.5 8.4 %copy-start.35 = (bf16[128,1536]{1,0:T(8,128)(2,1)S(1)}, bf16[128,1536]{1,0:T(8,128)(2,1)}, u32[]{:S(2)}) copy-start(bf16[128,1536]{1,0:T(8,128)(2,1)} %param.26) | copy-start | bytes 1179652
  16.6 19.1 %all-to-all-start = ((bf16[4,48,2,8,128]{4,3,1,2,0:T(8,128)(2,1)}), bf16[4,48,2,8,128]{4,3,1,2,0:T(8,128)(2,1)S(1)}, u32[]{:S(2)}, u32[]{:S(2)}) async-start(bf16[4,48,2,8,128]{4,3,1,2,0:T(8,128)(2,1)} %copy.108), calls=%async_computation | async-start | bytes 1572864 | tf_op jit(solution)/shard_map/all_to_all | solution.py:452
  20.8 255.7 %all-gather.5.cloned.1.call-start = ((), (), s32[]{:S(2)}) async-start(), calls=%async_computation.6 | async-start | bytes 10616832 | tf_op jit(solution)/shard_map/all_gather | solution.py:456
  21.2 105.2 %copy-start.40 = (s32[1,8]{1,0:T(1,128)S(1)}, s32[1,8]{1,0:T(1,128)}, u32[]{:S(2)}) copy-start(s32[1,8]{1,0:T(1,128)} %param.17) | copy-start | bytes 100
  36.2 105.6 %copy-start.10 = (bf16[1,128,1536]{2,1,0:T(8,128)(2,1)S(1)}, bf16[1,128,1536]{2,1,0:T(8,128)(2,1)}, u32[]{:S(2)}) copy-start(bf16[1,128,1536]{2,1,0:T(8,128)(2,1)} %param.16) | copy-start | bytes 1179652
  126.4 427.4 %reduce-scatter.4.cloned.1.call-start = ((), (), s32[]{:S(2)}) async-start(), calls=%async_computation.7 | async-start | bytes 7077888 | tf_op jit(solution)/shard_map/reduce_scatter | solution.py:522
  142.7 9.1 %copy-start.33 = (f32[128,48]{0,1:T(8,128)}, f32[128,48]{0,1:T(8,128)S(1)}, u32[]{:S(2)}) copy-start(f32[128,48]{0,1:T(8,128)S(1)} %get-tuple-element.72) | copy-start | bytes 73732
  142.7 9.1 %copy-start.37 = (f32[128,48]{0,1:T(8,128)}, f32[128,48]{0,1:T(8,128)S(1)}, u32[]{:S(2)}) copy-start(f32[128,48]{0,1:T(8,128)S(1)} %get-tuple-element.71) | copy-start | bytes 73732
  204.0 7.9 %copy-start.15 = (bf16[640,768]{0,1:T(8,128)(2,1)}, bf16[640,768]{0,1:T(8,128)(2,1)S(1)}, u32[]{:S(2)}) copy-start(bf16[640,768]{0,1:T(8,128)(2,1)S(1)} %copy.105) | copy-start | bytes 2949124
  204.7 10.5 %copy-start.13 = (bf16[640,768]{0,1:T(8,128)(2,1)}, bf16[640,768]{0,1:T(8,128)(2,1)S(1)}, u32[]{:S(2)}) copy-start(bf16[640,768]{0,1:T(8,128)(2,1)S(1)} %copy.104) | copy-start | bytes 2949124
  300.9 289.0 %reduce-scatter.8.cloned.1.call-start = ((), (), s32[]{:S(2)}) async-start(), calls=%async_computation.9 | async-start | bytes 3538944 | tf_op jit(solution)/shard_map/reduce_scatter | solution.py:511
  311.8 26.3 %copy-start.22 = (bf16[512,2048]{1,0:T(8,128)(2,1)S(1)}, bf16[512,2048]{1,0:T(8,128)(2,1)}, u32[]{:S(2)}) copy-start(bf16[512,2048]{1,0:T(8,128)(2,1)} %pad_maximum_fusion.2) | copy-start | bytes 6291460
  345.9 26.1 %copy-start.7 = (f32[128,1536]{1,0:T(8,128)S(1)}, f32[128,1536]{1,0:T(8,128)}, u32[]{:S(2)}) copy-start(f32[128,1536]{1,0:T(8,128)} %copy-done.6) | copy-start | bytes 2359300
  345.9 27.6 %copy-start.19 = (f32[128,1536]{1,0:T(8,128)S(1)}, f32[128,1536]{1,0:T(8,128)}, u32[]{:S(2)}) copy-start(f32[128,1536]{1,0:T(8,128)} %shard_map.205) | copy-start | bytes 2359300
  345.9 27.6 %copy-start.27 = (bf16[1,128,1536]{2,1,0:T(8,128)(2,1)S(1)}, bf16[1,128,1536]{2,1,0:T(8,128)(2,1)}, u32[]{:S(2)}) copy-start(bf16[1,128,1536]{2,1,0:T(8,128)(2,1)} %param.27) | copy-start | bytes 1179652
  380.0 6.3 copy-start.16
  406.7 132.4 %copy-start.34 = (f32[128,48]{0,1:T(8,128)S(1)}, f32[128,48]{0,1:T(8,128)}, u32[]{:S(2)}) copy-start(f32[128,48]{0,1:T(8,128)} %copy-done.33) | copy-start | bytes 73732
  406.7 132.4 %copy-start.36 = (f32[128,48]{0,1:T(8,128)S(1)}, f32[128,48]{0,1:T(8,128)}, u32[]{:S(2)}) copy-start(f32[128,48]{0,1:T(8,128)} %get-tuple-element.70) | copy-start | bytes 73732
  406.7 133.5 %copy-start.5 = (bf16[128,8,2,640]{0,3,2,1:T(8,128)(2,1)S(1)}, bf16[128,8,2,640]{0,3,2,1:T(8,128)(2,1)}, u32[]{:S(2)}) copy-start(bf16[128,8,2,640]{0,3,2,1:T(8,128)(2,1)} %copy-done.4) | copy-start | bytes 7864324
  542.3 7.9 %copy-start.21 = (bf16[128,8,2,96]{0,3,2,1:T(8,128)(2,1)S(1)}, bf16[128,8,2,96]{0,3,2,1:T(8,128)(2,1)}, u32[]{:S(2)}) copy-start(bf16[128,8,2,96]{0,3,2,1:T(8,128)(2,1)} %copy-done.20) | copy-start | bytes 1179652
  553.7 5.9 copy-start.31
  553.7 15.3 %all-to-all-start.1 = ((bf16[4,48,2048]{2,1,0:T(8,128)(2,1)}), bf16[4,48,2048]{2,1,0:T(8,128)(2,1)S(1)}, u32[]{:S(2)}, u32[]{:S(2)}) async-start(bf16[4,48,2048]{2,1,0:T(8,128)(2,1)} %bitcast.172), calls=%async_computation.2 | async-start | bytes 1572864 | tf_op jit(solution)/shard_map/all_to_all | solution.py:523
  557.4 191.4 %reduce-scatter.6.cloned.1.call-start = ((), (), s32[]{:S(2)}) async-start(), calls=%async_computation.8 | async-start | bytes 15003648 | tf_op jit(solution)/shard_map/reduce_scatter | solution.py:577
  (26 other events, 73.6 us)
Sparse Core Ops, SparseCore 0:
  12.6 110.1 all-gather.2
  126.5 149.9 all-gather.4
  301.0 155.8 reduce-scatter.3
  460.3 108.4 reduce-scatter.7
  587.8 161.0 reduce-scatter.5

commit v7 on v6

--- a/solution.py
+++ b/solution.py
@@ -508,9 +508,7 @@
 
     grad_out = cotangent[0]
     grad_all = fsdp_gather(grad_out, n_f).reshape(group_tokens, D)
-    down_sum = lax.psum_scatter(
-        outer_rows(hidden_low, grad_all).astype(jnp.bfloat16), "ctx", scatter_dimension=0, tiled=True
-    )
+    down_term = outer_rows(hidden_low, grad_all).astype(jnp.bfloat16)
     hidden_grad = times_transposed(grad_all, down_tp)
     gate_grad = (hidden_grad * up_pre * sigmoid * (1.0 + gate_pre * (1.0 - sigmoid))).astype(
         jnp.bfloat16
@@ -518,9 +516,17 @@
     up_grad = (hidden_grad * gate_pre * sigmoid).astype(jnp.bfloat16)
     gate_up_cat = jnp.concatenate([gate_grad, up_grad], axis=1)
     gate_up_term = outer_rows(xn2_all, gate_up_cat)
-    ff_pack, gate_up_cat = lax.optimization_barrier((gate_up_term.astype(jnp.bfloat16), gate_up_cat))
-    gu_sum = lax.psum_scatter(ff_pack, "ctx", scatter_dimension=0, tiled=True)
-    gu_sum = lax.all_to_all(gu_sum.reshape(n_f, rows, 2 * units), "fsdp", 0, 0, tiled=True)
+    grad_pack = jnp.concatenate(
+        [
+            gate_up_term.astype(jnp.bfloat16).reshape(n_ctx, n_f * rows, 2 * units),
+            down_term.reshape(n_ctx, down_rows, 2 * units),
+        ],
+        axis=1,
+    ).reshape(n_ctx * (n_f * rows + down_rows), 2 * units)
+    grad_pack, gate_up_cat = lax.optimization_barrier((grad_pack, gate_up_cat))
+    grad_sum = lax.psum_scatter(grad_pack, "ctx", scatter_dimension=0, tiled=True)
+    down_sum = grad_sum[n_f * rows :].reshape(ff_rows, D)
+    gu_sum = lax.all_to_all(grad_sum[: n_f * rows].reshape(n_f, rows, 2 * units), "fsdp", 0, 0, tiled=True)
     ff_sum = jnp.transpose(
         gu_sum.reshape(n_f, rows, 2, n_ctx, chunk), (1, 2, 3, 0, 4)
     ).reshape(rows, 2 * ff)

time: 768 us -> 786 us (1.023)
  local copies, waits for them, and re-layouts: 59.1 us -> 67 us
  transfers between devices with their start and end apart: 7 -> 6, of which waited for: 5 -> 5; matrix products, arithmetic and copies ran while one was open for 18% -> 15% of each run, Pallas kernels for 34% -> 34%
where the time goes in v7:
time: 786 us; the launch traced here: 780 us
  waiting for transfers between devices  299 us (38%)
  Pallas kernels  263 us (33%)
  matrix products  77.5 us (10%)
  local copies, waits for them, and re-layouts  67 us (9%)
  other arithmetic  48.1 us (6%)
  between operations  18 us (2%)
    reduce_scatter x1, waiting for transfers between devices, body(): lax.psum_scatter(jnp.concatenate([outer_rows(normed_low, projection_cat)....  156 us
    pallas_call x1, Pallas kernels, kv_return(): pl.pallas_call(functools.partial(kv_return_kernel, n_ctx, back), out_shap...  132 us
    all_gather x1, waiting for transfers between devices, body(): lax.all_gather(jnp.concatenate([query_weight, key_weight, value_weight, o...  85.9 us
    pallas_call x2, Pallas kernels, quad_reduce(): pl.pallas_call(quad_reduce_kernel, out_shape=jax.ShapeDtypeStruct(block,...  52.5 us
    pallas_call x1, Pallas kernels, kv_share(): pl.pallas_call(functools.partial(kv_share_kernel, n_ctx, back), out_shape...  48.9 us
    all_gather x1, waiting for transfers between devices, body(): ff_stack = lax.all_gather(ff_pack, 'ctx', axis=0, tiled=False)  39.5 us
    pallas_call x2, Pallas kernels, quad_gather(): pl.pallas_call(quad_gather_kernel, out_shape=jax.ShapeDtypeStruct((4,) +...  29.8 us
    dot_general x4, matrix products, times_transposed(): lax.dot_general(left, right, (((1,), (1,)), ((), ())), preferred_element_...  22.6 us
  transfers between devices with their start and end apart: 6, of which 5 were waited for; matrix products, arithmetic and copies ran while one was open for 15% of the time, Pallas kernels for 34%

profile of v7, /device:TPU:0, one launch (start us, length us, event | category | flops | bytes accessed | tf_op | source)
XLA Modules:
  0.0 779.9 jit_solution(10130182990634148273)
XLA Ops:
  16.6 4.2 all-to-all-start
  21.2 14.6 %all-to-all-done = bf16[4,48,2,8,128]{4,3,1,2,0:T(8,128)(2,1)S(1)} async-done(((bf16[4,48,2,8,128]{4,3,1,2,0:T(8,128)(2,1)}), bf16[4,48,2,8,128]{4,3,1,2,0:T(8,128)(2,1)S(1)}, u32[]{:S(2)}, u32[]{:S(2)}) %all-to-all-start) | async-done | bytes 786464 | tf_op jit(solution)/shard_map/all_to_all | solution.py:452
  36.9 85.9 %all-gather.3.cloned.1.call-done = bf16[1536,4736]{1,0:T(8,128)(2,1)} async-done(((bf16[48,4736]{1,0:T(8,128)(2,1)}), bf16[1536,4736]{1,0:T(8,128)(2,1)}) %all-gather.3.cloned.1.call-update) | async-done | bytes 14549008 | tf_op jit(solution)/shard_map/all_gather | solution.py:408
  126.6 14.8 %shard_map.206 = bf16[4,128,1536]{2,1,0:T(8,128)(2,1)} custom-call(bf16[128,1536]{1,0:T(8,128)(2,1)} %bitcast.173), custom_call_target="tpu_custom_call" | custom-call | tf_op jit(solution)/shard_map/pallas_call | solution.py:311
  145.2 5.2 fusion.3
  152.9 48.9 %shard_map.203 = bf16[5,128,1536]{2,1,0:T(8,128)(2,1)} custom-call(bf16[128,1536]{1,0:T(8,128)(2,1)} %pad_maximum_fusion.5.kv_ref), custom_call_target="tpu_custom_call" | custom-call | tf_op jit(solution)/shard_map/pallas_call | solution.py:116
  206.3 5.5 fusion.57
  222.0 15.0 %shard_map.204 = bf16[4,128,1536]{2,1,0:T(8,128)(2,1)} custom-call(bf16[128,1536]{1,0:T(8,128)(2,1)} %multiply_convert_fusion.1.x_ref), custom_call_target="tpu_custom_call" | custom-call | tf_op jit(solution)/shard_map/pallas_call | solution.py:311
  237.0 39.5 %all-gather.5.cloned.1.call-done = bf16[8,288,2048]{2,1,0:T(8,128)(2,1)} async-done(((bf16[1,288,2048]{2,1,0:T(8,128)(2,1)}), bf16[8,288,2048]{2,1,0:T(8,128)(2,1)}) %all-gather.5.cloned.1.call-update) | async-done | bytes 9437200 | tf_op jit(solution)/shard_map/all_gather | solution.py:456
  278.6 3.7 reshape_reshape.3
  294.6 5.7 convolution_convert_fusion.1
  303.8 6.0 reshape.377
  309.8 7.8 %pad_maximum_fusion.1 = bf16[8,288,2048]{2,1,0:T(8,128)(2,1)} fusion(bf16[8,96,2048]{2,1,0:T(8,128)(2,1)} %reshape.377, bf16[8,192,2048]{2,1,0:T(8,128)(2,1)} %bitcast.148), kind=kLoop, calls=%fused_computation.3 | loop fusion | flops 18874368 | bytes 18874368 | tf_op jit(solution)/shard_map/concatenate | solution.py:519
  322.6 5.6 fusion.60.p_ref
  328.3 26.3 %shard_map.205 = f32[128,1536]{1,0:T(8,128)} custom-call(f32[4,128,1536]{2,1,0:T(8,128)} %fusion.60.p_ref), custom_call_target="tpu_custom_call" | custom-call | tf_op jit(solution)/shard_map/pallas_call | solution.py:354
  354.5 8.0 %fusion.61.p_ref = f32[4,128,1536]{2,1,0:T(8,128)} fusion(bf16[4,128,2048]{2,1,0:T(8,128)(2,1)S(1)} %bitcast.162, bf16[1536,2048,1]{1,0,2:T(8,128)(2,1)} %bitcast.146), kind=kOutput, calls=%fused_computation.135 | convolution fusion | flops 3221225472 | bytes 11534336 | tf_op jit(solution)/shard_map/dot_general | solution.py:63
  362.6 26.2 %shard_map.207 = f32[128,1536]{1,0:T(8,128)} custom-call(f32[4,128,1536]{2,1,0:T(8,128)} %fusion.61.p_ref), custom_call_target="tpu_custom_call" | custom-call | tf_op jit(solution)/shard_map/pallas_call | solution.py:354
  392.4 4.1 fusion.19
  396.9 3.9 fusion.6
  417.4 131.6 %shard_map.208 = f32[128,1536]{1,0:T(8,128)} custom-call(f32[128,1536]{1,0:T(8,128)} %fusion.40.own_ref, bf16[4,128,1536]{2,1,0:T(8,128)(2,1)} %bitcast.147), custom_call_target="tpu_custom_call" | custom-call | tf_op jit(solution)/shard_map/pallas_call | solution.py:163
  559.4 7.9 %fusion.38 = (bf16[1536]{0:T(1024)(128)(2,1)S(1)}, f32[128]{0:T(128)S(1)}, f32[128,1536]{1,0:T(8,128)}) fusion(bf16[1,128,1536]{2,1,0:T(8,128)(2,1)S(1)} %copy-done.11, f32[128]{0:T(128)S(1)} %copy-done.39, f32[1536]{0:T(1024)S(1)} %get-tuple-element.40, bf16[1536,4736]{1,0:T(8,128)(2,1)} %all-gather.3.cloned.1.call-done, ...), kind=kOutput, calls=%fused_computation.57 | convolution fusion | flops 1211693440 | bytes 11413504 | tf_op jit(solution)/shard_map/dot_general | solution.py:63
  578.8 6.1 convolution_convert_fusion
  593.8 12.9 %pad_maximum_fusion = bf16[1536,4736]{1,0:T(8,128)(2,1)} fusion(bf16[1536,128]{1,0:T(8,128)(2,1)S(1)} %scatter.4, bf16[1536,1536]{1,0:T(8,128)(2,1)} %convolution_convert_fusion.2, bf16[1536,3072]{1,0:T(8,128)(2,1)} %convolution_convert_fusion), kind=kLoop, calls=%fused_computation.1 | loop fusion | flops 43646976 | bytes 29097984 | tf_op jit(solution)/shard_map/concatenate | solution.py:584
  612.5 155.5 %reduce-scatter.5.cloned.1.call-done = bf16[48,4736]{1,0:T(8,128)(2,1)} async-done(((bf16[1536,4736]{1,0:T(8,128)(2,1)}), bf16[48,4736]{1,0:T(8,128)(2,1)}) %reduce-scatter.5.cloned.1.call-update) | async-done | bytes 454672 | tf_op jit(solution)/shard_map/reduce_scatter | solution.py:583
  (201 shorter events, 116.8 us)
Async XLA Ops:
  7.2 115.6 %all-gather.3.cloned.1.call-start = ((), (), s32[]{:S(2)}) async-start(), calls=%async_computation.4 | async-start | bytes 15003648 | tf_op jit(solution)/shard_map/all_gather | solution.py:408
  12.5 8.4 %copy-start.35 = (bf16[128,1536]{1,0:T(8,128)(2,1)S(1)}, bf16[128,1536]{1,0:T(8,128)(2,1)}, u32[]{:S(2)}) copy-start(bf16[128,1536]{1,0:T(8,128)(2,1)} %param.26) | copy-start | bytes 1179652
  16.6 19.1 %all-to-all-start = ((bf16[4,48,2,8,128]{4,3,1,2,0:T(8,128)(2,1)}), bf16[4,48,2,8,128]{4,3,1,2,0:T(8,128)(2,1)S(1)}, u32[]{:S(2)}, u32[]{:S(2)}) async-start(bf16[4,48,2,8,128]{4,3,1,2,0:T(8,128)(2,1)} %copy.107), calls=%async_computation | async-start | bytes 1572864 | tf_op jit(solution)/shard_map/all_to_all | solution.py:452
  20.8 255.6 %all-gather.5.cloned.1.call-start = ((), (), s32[]{:S(2)}) async-start(), calls=%async_computation.5 | async-start | bytes 10616832 | tf_op jit(solution)/shard_map/all_gather | solution.py:456
  21.2 105.3 %copy-start.40 = (s32[1,8]{1,0:T(1,128)S(1)}, s32[1,8]{1,0:T(1,128)}, u32[]{:S(2)}) copy-start(s32[1,8]{1,0:T(1,128)} %param.17) | copy-start | bytes 100
  36.2 105.6 %copy-start.10 = (bf16[1,128,1536]{2,1,0:T(8,128)(2,1)S(1)}, bf16[1,128,1536]{2,1,0:T(8,128)(2,1)}, u32[]{:S(2)}) copy-start(bf16[1,128,1536]{2,1,0:T(8,128)(2,1)} %param.16) | copy-start | bytes 1179652
  126.4 444.5 %reduce-scatter.3.cloned.1.call-start = ((), (), s32[]{:S(2)}) async-start(), calls=%async_computation.6 | async-start | bytes 10616832 | tf_op jit(solution)/shard_map/reduce_scatter | solution.py:527
  142.8 9.1 %copy-start.33 = (f32[128,48]{0,1:T(8,128)}, f32[128,48]{0,1:T(8,128)S(1)}, u32[]{:S(2)}) copy-start(f32[128,48]{0,1:T(8,128)S(1)} %get-tuple-element.72) | copy-start | bytes 73732
  142.8 9.1 %copy-start.37 = (f32[128,48]{0,1:T(8,128)}, f32[128,48]{0,1:T(8,128)S(1)}, u32[]{:S(2)}) copy-start(f32[128,48]{0,1:T(8,128)S(1)} %get-tuple-element.71) | copy-start | bytes 73732
  204.0 7.9 %copy-start.15 = (bf16[640,768]{0,1:T(8,128)(2,1)}, bf16[640,768]{0,1:T(8,128)(2,1)S(1)}, u32[]{:S(2)}) copy-start(bf16[640,768]{0,1:T(8,128)(2,1)S(1)} %copy.104) | copy-start | bytes 2949124
  204.7 10.4 %copy-start.13 = (bf16[640,768]{0,1:T(8,128)(2,1)}, bf16[640,768]{0,1:T(8,128)(2,1)S(1)}, u32[]{:S(2)}) copy-start(bf16[640,768]{0,1:T(8,128)(2,1)S(1)} %copy.103) | copy-start | bytes 2949124
  293.0 7.3 copy-start.41
  328.3 26.3 %copy-start.22 = (bf16[512,2048]{1,0:T(8,128)(2,1)S(1)}, bf16[512,2048]{1,0:T(8,128)(2,1)}, u32[]{:S(2)}) copy-start(bf16[512,2048]{1,0:T(8,128)(2,1)} %pad_maximum_fusion.3) | copy-start | bytes 6291460
  362.6 26.2 %copy-start.7 = (f32[128,1536]{1,0:T(8,128)S(1)}, f32[128,1536]{1,0:T(8,128)}, u32[]{:S(2)}) copy-start(f32[128,1536]{1,0:T(8,128)} %copy-done.6) | copy-start | bytes 2359300
  362.6 27.7 %copy-start.19 = (f32[128,1536]{1,0:T(8,128)S(1)}, f32[128,1536]{1,0:T(8,128)}, u32[]{:S(2)}) copy-start(f32[128,1536]{1,0:T(8,128)} %shard_map.205) | copy-start | bytes 2359300
  362.6 27.7 %copy-start.27 = (bf16[1,128,1536]{2,1,0:T(8,128)(2,1)S(1)}, bf16[1,128,1536]{2,1,0:T(8,128)(2,1)}, u32[]{:S(2)}) copy-start(bf16[1,128,1536]{2,1,0:T(8,128)(2,1)} %param.27) | copy-start | bytes 1179652
  417.4 138.8 %copy-start.34 = (f32[128,48]{0,1:T(8,128)S(1)}, f32[128,48]{0,1:T(8,128)}, u32[]{:S(2)}) copy-start(f32[128,48]{0,1:T(8,128)} %copy-done.33) | copy-start | bytes 73732
  417.4 138.8 %copy-start.36 = (f32[128,48]{0,1:T(8,128)S(1)}, f32[128,48]{0,1:T(8,128)}, u32[]{:S(2)}) copy-start(f32[128,48]{0,1:T(8,128)} %get-tuple-element.70) | copy-start | bytes 73732
  417.4 139.9 %copy-start.5 = (bf16[128,8,2,640]{0,3,2,1:T(8,128)(2,1)S(1)}, bf16[128,8,2,640]{0,3,2,1:T(8,128)(2,1)}, u32[]{:S(2)}) copy-start(bf16[128,8,2,640]{0,3,2,1:T(8,128)(2,1)} %copy-done.4) | copy-start | bytes 7864324
  559.4 7.9 %copy-start.21 = (bf16[128,8,2,96]{0,3,2,1:T(8,128)(2,1)S(1)}, bf16[128,8,2,96]{0,3,2,1:T(8,128)(2,1)}, u32[]{:S(2)}) copy-start(bf16[128,8,2,96]{0,3,2,1:T(8,128)(2,1)} %copy-done.20) | copy-start | bytes 1179652
  570.8 8.0 %copy-start.12 = (bf16[1,128,1536]{2,1,0:T(8,128)(2,1)S(1)}, bf16[1,128,1536]{2,1,0:T(8,128)(2,1)}, u32[]{:S(2)}) copy-start(bf16[1,128,1536]{2,1,0:T(8,128)(2,1)} %param.16) | copy-start | bytes 1179652
  570.8 8.0 %copy-start.31 = (bf16[128,768]{0,1:T(8,128)(2,1)S(1)}, bf16[128,768]{0,1:T(8,128)(2,1)}, u32[]{:S(2)}) copy-start(bf16[128,768]{0,1:T(8,128)(2,1)} %copy.117) | copy-start | bytes 589828
  573.0 15.1 %all-to-all-start.1 = ((bf16[4,48,2048]{2,1,0:T(8,128)(2,1)}), bf16[4,48,2048]{2,1,0:T(8,128)(2,1)S(1)}, u32[]{:S(2)}, u32[]{:S(2)}) async-start(bf16[4,48,2048]{2,1,0:T(8,128)(2,1)} %bitcast.56), calls=%async_computation.2 | async-start | bytes 1572864 | tf_op jit(solution)/shard_map/all_to_all | solution.py:529
  576.5 191.5 %reduce-scatter.5.cloned.1.call-start = ((), (), s32[]{:S(2)}) async-start(), calls=%async_computation.7 | async-start | bytes 15003648 | tf_op jit(solution)/shard_map/reduce_scatter | solution.py:583
  (25 other events, 73.9 us)
Sparse Core Ops, SparseCore 0:
  12.6 110.1 all-gather.2
  126.5 149.9 all-gather.4
  317.8 232.7 reduce-scatter.2
  606.9 161.0 reduce-scatter.4

commit v8 on v6

--- a/solution.py
+++ b/solution.py
@@ -504,7 +504,6 @@
     sigmoid = jax.nn.sigmoid(gate_pre)
     hidden_low = (gate_pre * sigmoid * up_pre).astype(jnp.bfloat16)
     ff_part = jnp.dot(hidden_low, down_tp, preferred_element_type=jnp.float32)
-    layer_out = middle + fsdp_reduce(ff_part.reshape(n_f, tok_rows, D), n_f)
 
     grad_out = cotangent[0]
     grad_all = fsdp_gather(grad_out, n_f).reshape(group_tokens, D)
@@ -519,6 +518,8 @@
     gate_up_cat = jnp.concatenate([gate_grad, up_grad], axis=1)
     gate_up_term = outer_rows(xn2_all, gate_up_cat)
     ff_pack, gate_up_cat = lax.optimization_barrier((gate_up_term.astype(jnp.bfloat16), gate_up_cat))
+    ff_part = ff_part.at[0, 0].add(ff_pack[0, 0].astype(jnp.float32) * 0.0)
+    layer_out = middle + fsdp_reduce(ff_part.reshape(n_f, tok_rows, D), n_f)
     gu_sum = lax.psum_scatter(ff_pack, "ctx", scatter_dimension=0, tiled=True)
     gu_sum = lax.all_to_all(gu_sum.reshape(n_f, rows, 2 * units), "fsdp", 0, 0, tiled=True)
     ff_sum = jnp.transpose(

time: 768 us -> 770 us (level)
  transfers between devices with their start and end apart: 7 -> 7, of which waited for: 5 -> 5; matrix products, arithmetic and copies ran while one was open for 18% -> 18% of each run, Pallas kernels for 34% -> 33%
where the time goes in v8:
time: 770 us; the launch traced here: 764 us
  waiting for transfers between devices  303 us (39%)
  Pallas kernels  249 us (32%)
  matrix products  78.8 us (10%)
  local copies, waits for them, and re-layouts  64.3 us (8%)
  other arithmetic  41.5 us (5%)
  between operations  19.5 us (3%)
  starting transfers between devices  8 us (1%)
    reduce_scatter x1, waiting for transfers between devices, body(): lax.psum_scatter(jnp.concatenate([outer_rows(normed_low, projection_cat)....  156 us
    pallas_call x1, Pallas kernels, kv_return(): pl.pallas_call(functools.partial(kv_return_kernel, n_ctx, back), out_shap...  118 us
    all_gather x1, waiting for transfers between devices, body(): lax.all_gather(jnp.concatenate([query_weight, key_weight, value_weight, o...  85.9 us
    pallas_call x2, Pallas kernels, quad_reduce(): pl.pallas_call(quad_reduce_kernel, out_shape=jax.ShapeDtypeStruct(block,...  52.3 us
    pallas_call x1, Pallas kernels, kv_share(): pl.pallas_call(functools.partial(kv_share_kernel, n_ctx, back), out_shape...  48.9 us
    all_gather x1, waiting for transfers between devices, body(): ff_stack = lax.all_gather(ff_pack, 'ctx', axis=0, tiled=False)  43.3 us
    pallas_call x2, Pallas kernels, quad_gather(): pl.pallas_call(quad_gather_kernel, out_shape=jax.ShapeDtypeStruct((4,) +...  29.7 us
    dot_general x4, matrix products, times_transposed(): lax.dot_general(left, right, (((1,), (1,)), ((), ())), preferred_element_...  24.7 us
  transfers between devices with their start and end apart: 7, of which 5 were waited for; matrix products, arithmetic and copies ran while one was open for 18% of the time, Pallas kernels for 33%

profile of v8, /device:TPU:0, one launch (start us, length us, event | category | flops | bytes accessed | tf_op | source)
XLA Modules:
  0.0 763.5 jit_solution(11559763788296387994)
XLA Ops:
  16.6 4.2 all-to-all-start
  21.2 14.6 %all-to-all-done = bf16[4,48,2,8,128]{4,3,1,2,0:T(8,128)(2,1)S(1)} async-done(((bf16[4,48,2,8,128]{4,3,1,2,0:T(8,128)(2,1)}), bf16[4,48,2,8,128]{4,3,1,2,0:T(8,128)(2,1)S(1)}, u32[]{:S(2)}, u32[]{:S(2)}) %all-to-all-start) | async-done | bytes 786464 | tf_op jit(solution)/shard_map/all_to_all | solution.py:452
  36.9 85.9 %all-gather.3.cloned.1.call-done = bf16[1536,4736]{1,0:T(8,128)(2,1)} async-done(((bf16[48,4736]{1,0:T(8,128)(2,1)}), bf16[1536,4736]{1,0:T(8,128)(2,1)}) %all-gather.3.cloned.1.call-update) | async-done | bytes 14549008 | tf_op jit(solution)/shard_map/all_gather | solution.py:408
  126.6 14.9 %shard_map.205 = bf16[4,128,1536]{2,1,0:T(8,128)(2,1)} custom-call(bf16[128,1536]{1,0:T(8,128)(2,1)} %bitcast.170), custom_call_target="tpu_custom_call" | custom-call | tf_op jit(solution)/shard_map/pallas_call | solution.py:311
  144.2 5.2 fusion.3
  151.8 48.9 %shard_map.203 = bf16[5,128,1536]{2,1,0:T(8,128)(2,1)} custom-call(bf16[128,1536]{1,0:T(8,128)(2,1)} %pad_maximum_fusion.4.kv_ref), custom_call_target="tpu_custom_call" | custom-call | tf_op jit(solution)/shard_map/pallas_call | solution.py:116
  205.6 4.5 fusion.57
  219.3 14.8 %shard_map.204 = bf16[4,128,1536]{2,1,0:T(8,128)(2,1)} custom-call(bf16[128,1536]{1,0:T(8,128)(2,1)} %multiply_convert_fusion.1.x_ref), custom_call_target="tpu_custom_call" | custom-call | tf_op jit(solution)/shard_map/pallas_call | solution.py:311
  234.2 43.3 %all-gather.5.cloned.1.call-done = bf16[8,288,2048]{2,1,0:T(8,128)(2,1)} async-done(((bf16[1,288,2048]{2,1,0:T(8,128)(2,1)}), bf16[8,288,2048]{2,1,0:T(8,128)(2,1)}) %all-gather.5.cloned.1.call-update) | async-done | bytes 9437200 | tf_op jit(solution)/shard_map/all_gather | solution.py:456
  277.4 4.0 slice.232
  281.4 6.0 reshape_reshape.3
  300.6 5.7 convolution_convert_fusion.1
  308.7 4.0 fusion.60
  317.5 8.5 %fusion.61.p_ref = f32[4,128,1536]{2,1,0:T(8,128)} fusion(bf16[4,128,2048]{2,1,0:T(8,128)(2,1)} %bitcast.159, bf16[1536,2048,1]{1,0,2:T(8,128)(2,1)} %bitcast.143), kind=kOutput, calls=%fused_computation.133 | convolution fusion | flops 3221225472 | bytes 11534336 | tf_op jit(solution)/shard_map/dot_general | solution.py:63
  326.1 26.1 %shard_map.207 = f32[128,1536]{1,0:T(8,128)} custom-call(f32[4,128,1536]{2,1,0:T(8,128)} %fusion.61.p_ref), custom_call_target="tpu_custom_call" | custom-call | tf_op jit(solution)/shard_map/pallas_call | solution.py:354
  352.2 26.1 %shard_map.206 = f32[128,1536]{1,0:T(8,128)} custom-call(f32[4,128,1536]{2,1,0:T(8,128)} %bitcast.155), custom_call_target="tpu_custom_call" | custom-call | tf_op jit(solution)/shard_map/pallas_call | solution.py:354
  382.6 4.8 fusion.19
  389.3 5.3 convolution_convert_fusion.3
  395.9 4.1 fusion.6
  416.5 117.8 %shard_map.208 = f32[128,1536]{1,0:T(8,128)} custom-call(f32[128,1536]{1,0:T(8,128)} %fusion.40.own_ref, bf16[4,128,1536]{2,1,0:T(8,128)(2,1)} %bitcast.144), custom_call_target="tpu_custom_call" | custom-call | tf_op jit(solution)/shard_map/pallas_call | solution.py:163
  544.8 7.9 %fusion.38 = (bf16[1536]{0:T(1024)(128)(2,1)S(1)}, f32[128]{0:T(128)S(1)}, f32[128,1536]{1,0:T(8,128)}) fusion(bf16[1,128,1536]{2,1,0:T(8,128)(2,1)S(1)} %copy-done.9, f32[128]{0:T(128)S(1)} %add_rsqrt_fusion.1, f32[1536]{0:T(1024)S(1)} %get-tuple-element.52, bf16[1536,4736]{1,0:T(8,128)(2,1)} %all-gather.3.cloned.1.call-done, ...), kind=kOutput, calls=%fused_computation.56 | convolution fusion | flops 1211693440 | bytes 11413504 | tf_op jit(solution)/shard_map/dot_general | solution.py:63
  562.1 6.2 convolution_convert_fusion
  577.1 13.0 %pad_maximum_fusion = bf16[1536,4736]{1,0:T(8,128)(2,1)} fusion(bf16[1536,128]{1,0:T(8,128)(2,1)S(1)} %scatter.4, bf16[1536,1536]{1,0:T(8,128)(2,1)} %convolution_convert_fusion.2, bf16[1536,3072]{1,0:T(8,128)(2,1)} %convolution_convert_fusion), kind=kLoop, calls=%fused_computation.1 | loop fusion | flops 43646976 | bytes 29097984 | tf_op jit(solution)/shard_map/concatenate | solution.py:579
  595.6 155.6 %reduce-scatter.6.cloned.1.call-done = bf16[48,4736]{1,0:T(8,128)(2,1)} async-done(((bf16[1536,4736]{1,0:T(8,128)(2,1)}), bf16[48,4736]{1,0:T(8,128)(2,1)}) %reduce-scatter.6.cloned.1.call-update) | async-done | bytes 454672 | tf_op jit(solution)/shard_map/reduce_scatter | solution.py:578
  (174 shorter events, 112.5 us)
Async XLA Ops:
  7.2 115.6 %all-gather.3.cloned.1.call-start = ((), (), s32[]{:S(2)}) async-start(), calls=%async_computation.5 | async-start | bytes 15003648 | tf_op jit(solution)/shard_map/all_gather | solution.py:408
  12.5 8.4 %copy-start.26 = (bf16[128,1536]{1,0:T(8,128)(2,1)S(1)}, bf16[128,1536]{1,0:T(8,128)(2,1)}, u32[]{:S(2)}) copy-start(bf16[128,1536]{1,0:T(8,128)(2,1)} %param.28) | copy-start | bytes 1179652
  16.6 19.1 %all-to-all-start = ((bf16[4,48,2,8,128]{4,3,1,2,0:T(8,128)(2,1)}), bf16[4,48,2,8,128]{4,3,1,2,0:T(8,128)(2,1)S(1)}, u32[]{:S(2)}, u32[]{:S(2)}) async-start(bf16[4,48,2,8,128]{4,3,1,2,0:T(8,128)(2,1)} %copy.107), calls=%async_computation | async-start | bytes 1572864 | tf_op jit(solution)/shard_map/all_to_all | solution.py:452
  20.8 256.6 %all-gather.5.cloned.1.call-start = ((), (), s32[]{:S(2)}) async-start(), calls=%async_computation.6 | async-start | bytes 10616832 | tf_op jit(solution)/shard_map/all_gather | solution.py:456
  21.2 105.2 %copy-start.27 = (s32[1,8]{1,0:T(1,128)S(1)}, s32[1,8]{1,0:T(1,128)}, u32[]{:S(2)}) copy-start(s32[1,8]{1,0:T(1,128)} %param.19) | copy-start | bytes 100
  36.2 105.7 %copy-start.7 = (bf16[1,128,1536]{2,1,0:T(8,128)(2,1)S(1)}, bf16[1,128,1536]{2,1,0:T(8,128)(2,1)}, u32[]{:S(2)}) copy-start(bf16[1,128,1536]{2,1,0:T(8,128)(2,1)} %param.18) | copy-start | bytes 1179652
  126.3 429.9 %reduce-scatter.4.cloned.1.call-start = ((), (), s32[]{:S(2)}) async-start(), calls=%async_computation.7 | async-start | bytes 7077888 | tf_op jit(solution)/shard_map/reduce_scatter | solution.py:523
  203.0 7.2 copy-start.12
  205.6 4.5 copy-start.17
  210.2 3.2 copy-start.11
  214.9 3.4 copy-start.15
  218.3 160.1 %copy-start.4 = (f32[128,1536]{1,0:T(8,128)}, f32[128,1536]{1,0:T(8,128)S(1)}, u32[]{:S(2)}) copy-start(f32[128,1536]{1,0:T(8,128)S(1)} %get-tuple-element.92) | copy-start | bytes 2359300
  287.5 3.5 copy-start.20
  291.0 3.5 copy-start.5
  291.0 4.2 copy-start.13
  291.0 4.6 copy-start.19
  306.3 286.1 %reduce-scatter.8.cloned.1.call-start = ((), (), s32[]{:S(2)}) async-start(), calls=%async_computation.9 | async-start | bytes 3538944 | tf_op jit(solution)/shard_map/reduce_scatter | solution.py:510
  395.9 5.7 copy-start.18
  416.5 126.1 %copy-start.3 = (bf16[128,8,2,640]{0,3,2,1:T(8,128)(2,1)S(1)}, bf16[128,8,2,640]{0,3,2,1:T(8,128)(2,1)}, u32[]{:S(2)}) copy-start(bf16[128,8,2,640]{0,3,2,1:T(8,128)(2,1)} %copy-done.2) | copy-start | bytes 7864324
  544.8 7.9 %copy-start.16 = (bf16[128,8,2,96]{0,3,2,1:T(8,128)(2,1)S(1)}, bf16[128,8,2,96]{0,3,2,1:T(8,128)(2,1)}, u32[]{:S(2)}) copy-start(bf16[128,8,2,96]{0,3,2,1:T(8,128)(2,1)} %copy-done.15) | copy-start | bytes 1179652
  556.2 5.9 copy-start.10
  556.2 5.9 copy-start.24
  556.3 15.3 %all-to-all-start.1 = ((bf16[4,48,2048]{2,1,0:T(8,128)(2,1)}), bf16[4,48,2048]{2,1,0:T(8,128)(2,1)S(1)}, u32[]{:S(2)}, u32[]{:S(2)}) async-start(bf16[4,48,2048]{2,1,0:T(8,128)(2,1)} %bitcast.171), calls=%async_computation.2 | async-start | bytes 1572864 | tf_op jit(solution)/shard_map/all_to_all | solution.py:524
  559.9 191.4 %reduce-scatter.6.cloned.1.call-start = ((), (), s32[]{:S(2)}) async-start(), calls=%async_computation.8 | async-start | bytes 15003648 | tf_op jit(solution)/shard_map/reduce_scatter | solution.py:578
  (12 other events, 19.7 us)
Sparse Core Ops, SparseCore 0:
  12.6 110.1 all-gather.2
  126.5 150.9 all-gather.4
  306.4 152.1 reduce-scatter.3
  462.0 108.7 reduce-scatter.7
  590.2 160.9 reduce-scatter.5

commit v9 on v7

--- a/solution.py
+++ b/solution.py
@@ -379,7 +379,99 @@
     return group_reduce(p, n_f)
 
 
+def ring_order(n, snake):
+    c = lax.axis_index("ctx")
+    if snake:
+        half = n // 2
+        y = c % 2
+        z = c // 2
+        pos = (1 - y) * z + y * (n - 1 - z)
+
+        def device_at(q):
+            q = (q + n) % n
+            h = q // half
+            return (1 - h) * 2 * q + h * (2 * (n - 1 - q) + 1)
+
+    else:
+        pos = c
+
+        def device_at(q):
+            return (q + n) % n
+
+    return c, pos, device_at
+
+
+def ring_reduce_kernel(n, snake, part_ref, out_ref, recv_buf, send_buf, send_sem, recv_sem):
+    c, pos, device_at = ring_order(n, snake)
+    f = lax.axis_index("fsdp")
+    nxt = device_at(pos + 1)
+    prv = device_at(pos - 1)
+    barrier = pltpu.get_barrier_semaphore()
+    pl.semaphore_signal(barrier, inc=1, device_id=(nxt, f), device_id_type=MESH)
+    pl.semaphore_signal(barrier, inc=1, device_id=(prv, f), device_id_type=MESH)
+    pl.semaphore_wait(barrier, 2)
+    width = part_ref.shape[2] // 2
+    steps = n - 1
+    directions = ((0, 1, nxt), (1, -1, prv))
+
+    def copy(d, s, src, dest):
+        return pltpu.make_async_remote_copy(
+            src_ref=src,
+            dst_ref=recv_buf.at[d, s],
+            send_sem=send_sem.at[d, s],
+            recv_sem=recv_sem.at[d, s],
+            device_id=(dest, f),
+            device_id_type=MESH,
+        )
+
+    sends = []
+    for d, sign, dest in directions:
+        cols = pl.ds(d * width, width)
+        first = copy(d, 0, part_ref.at[device_at(pos - sign), :, cols], dest)
+        first.start()
+        sends.append(first)
+    for s in range(1, steps):
+        for d, sign, dest in directions:
+            cols = pl.ds(d * width, width)
+            copy(d, s - 1, send_buf.at[d, s], dest).wait_recv()
+            block = device_at(pos - sign * (s + 1))
+            send_buf[d, s] = (
+                recv_buf[d, s - 1].astype(jnp.float32) + part_ref[block, :, cols].astype(jnp.float32)
+            ).astype(send_buf.dtype)
+            nxt_copy = copy(d, s, send_buf.at[d, s], dest)
+            nxt_copy.start()
+            sends.append(nxt_copy)
+    for d, sign, dest in directions:
+        cols = pl.ds(d * width, width)
+        copy(d, steps - 1, send_buf.at[d, 0], dest).wait_recv()
+        out_ref[:, cols] = recv_buf[d, steps - 1].astype(jnp.float32) + part_ref[c, :, cols].astype(
+            jnp.float32
+        )
+    for s_copy in sends:
+        s_copy.wait_send()
+
+
+def ring_reduce(part, n, snake):
+    _, rows_, cols_ = part.shape
+    return pl.pallas_call(
+        functools.partial(ring_reduce_kernel, n, snake),
+        out_shape=jax.ShapeDtypeStruct((rows_, cols_), jnp.float32),
+        in_specs=[pl.BlockSpec(memory_space=pltpu.VMEM)],
+        out_specs=pl.BlockSpec(memory_space=pltpu.VMEM),
+        scratch_shapes=[
+            pltpu.VMEM((2, n - 1, rows_, cols_ // 2), part.dtype),
+            pltpu.VMEM((2, n - 1, rows_, cols_ // 2), part.dtype),
+            pltpu.SemaphoreType.DMA((2, n - 1)),
+            pltpu.SemaphoreType.DMA((2, n - 1)),
+        ],
+        compiler_params=pltpu.CompilerParams(
+            collective_id=6, has_side_effects=True, vmem_limit_bytes=100 * 1024 * 1024 // 2
+        ),
+    )(part)
+
+
 def body(
+    snake,
     tokens,
     doc_lengths,
     attention_gain,
@@ -522,9 +614,8 @@
             down_term.reshape(n_ctx, down_rows, 2 * units),
         ],
         axis=1,
-    ).reshape(n_ctx * (n_f * rows + down_rows), 2 * units)
-    grad_pack, gate_up_cat = lax.optimization_barrier((grad_pack, gate_up_cat))
-    grad_sum = lax.psum_scatter(grad_pack, "ctx", scatter_dimension=0, tiled=True)
+    )
+    grad_sum = ring_reduce(grad_pack, n_ctx, snake).astype(jnp.bfloat16)
     down_sum = grad_sum[n_f * rows :].reshape(ff_rows, D)
     gu_sum = lax.all_to_all(grad_sum[: n_f * rows].reshape(n_f, rows, 2 * units), "fsdp", 0, 0, tiled=True)
     ff_sum = jnp.transpose(
@@ -609,11 +700,21 @@
     )
 
 
+def snake_ring(mesh):
+    column = mesh.devices[:, 0]
+    n = column.shape[0]
+    if n % 2 or n < 4:
+        return False
+    return all(
+        tuple(d.coords)[2] == i // 2 and tuple(d.coords)[1] == i % 2 for i, d in enumerate(column)
+    )
+
+
 def solution(mesh):
     weight = P(ALL, None)
     stream = P("fsdp", "ctx", None)
     return jax.shard_map(
-        body,
+        functools.partial(body, snake_ring(mesh)),
         mesh=mesh,
         in_specs=(
             stream,

time: 786 us -> 849 us (1.080)
  Pallas kernels: 263 us -> 320 us
  matrix products: 77.5 us -> 89.4 us
    pallas_call x0 -> x1, Pallas kernels: none -> 94.6 us  [ring_reduce(): pl.pallas_call(functools.partial(ring_reduce_kernel, n, snake), out_shape...]
    pallas_call x1, Pallas kernels: 132 us -> 94.1 us  [kv_return(): pl.pallas_call(functools.partial(kv_return_kernel, n_ctx, back), out_shap...]
    dot_general x4, matrix products: 22.6 us -> 34.5 us  [times_transposed(): lax.dot_general(left, right, (((1,), (1,)), ((), ())), preferred_element_...]
  transfers between devices with their start and end apart: 6 -> 5, of which waited for: 5 -> 4; matrix products, arithmetic and copies ran while one was open for 15% -> 7% of each run, Pallas kernels for 34% -> 9%
where the time goes in v9:
time: 849 us; the launch traced here: 847 us
  Pallas kernels  320 us (38%)
  waiting for transfers between devices  297 us (35%)
  matrix products  89.4 us (11%)
  local copies, waits for them, and re-layouts  68.5 us (8%)
  other arithmetic  46.4 us (5%)
  between operations  18 us (2%)
    reduce_scatter x1, waiting for transfers between devices, body(): lax.psum_scatter(jnp.concatenate([outer_rows(normed_low, projection_cat)....  158 us
    pallas_call x1, Pallas kernels, ring_reduce(): pl.pallas_call(functools.partial(ring_reduce_kernel, n, snake), out_shape...  94.6 us
    pallas_call x1, Pallas kernels, kv_return(): pl.pallas_call(functools.partial(kv_return_kernel, n_ctx, back), out_shap...  94.1 us
    all_gather x1, waiting for transfers between devices, body(): lax.all_gather(jnp.concatenate([query_weight, key_weight, value_weight, o...  85.9 us
    pallas_call x2, Pallas kernels, quad_reduce(): pl.pallas_call(quad_reduce_kernel, out_shape=jax.ShapeDtypeStruct(block,...  52.2 us
    pallas_call x1, Pallas kernels, kv_share(): pl.pallas_call(functools.partial(kv_share_kernel, n_ctx, back), out_shape...  48.9 us
    all_gather x1, waiting for transfers between devices, body(): ff_stack = lax.all_gather(ff_pack, 'ctx', axis=0, tiled=False)  38.9 us
    dot_general x4, matrix products, times_transposed(): lax.dot_general(left, right, (((1,), (1,)), ((), ())), preferred_element_...  34.5 us
  transfers between devices with their start and end apart: 5, of which 4 were waited for; matrix products, arithmetic and copies ran while one was open for 7% of the time, Pallas kernels for 9%

profile of v9, /device:TPU:0, one launch (start us, length us, event | category | flops | bytes accessed | tf_op | source)
XLA Modules:
  0.0 846.8 jit_solution(4476308670617718157)
XLA Ops:
  16.6 4.2 all-to-all-start
  21.2 14.6 %all-to-all-done = bf16[4,48,2,8,128]{4,3,1,2,0:T(8,128)(2,1)S(1)} async-done(((bf16[4,48,2,8,128]{4,3,1,2,0:T(8,128)(2,1)}), bf16[4,48,2,8,128]{4,3,1,2,0:T(8,128)(2,1)S(1)}, u32[]{:S(2)}, u32[]{:S(2)}) %all-to-all-start) | async-done | bytes 786464 | tf_op jit(solution)/shard_map/all_to_all | solution.py:544
  36.9 85.9 %all-gather.3.cloned.1.call-done = bf16[1536,4736]{1,0:T(8,128)(2,1)} async-done(((bf16[48,4736]{1,0:T(8,128)(2,1)}), bf16[1536,4736]{1,0:T(8,128)(2,1)}) %all-gather.3.cloned.1.call-update) | async-done | bytes 14549008 | tf_op jit(solution)/shard_map/all_gather | solution.py:500
  126.6 14.8 %shard_map.206 = bf16[4,128,1536]{2,1,0:T(8,128)(2,1)} custom-call(bf16[128,1536]{1,0:T(8,128)(2,1)} %bitcast.175), custom_call_target="tpu_custom_call" | custom-call | tf_op jit(solution)/shard_map/pallas_call | solution.py:311
  146.5 5.2 fusion.3
  154.1 48.9 %shard_map.203 = bf16[5,128,1536]{2,1,0:T(8,128)(2,1)} custom-call(bf16[128,1536]{1,0:T(8,128)(2,1)} %pad_maximum_fusion.5.kv_ref), custom_call_target="tpu_custom_call" | custom-call | tf_op jit(solution)/shard_map/pallas_call | solution.py:116
  207.7 5.6 fusion.57
  223.3 15.0 %shard_map.204 = bf16[4,128,1536]{2,1,0:T(8,128)(2,1)} custom-call(bf16[128,1536]{1,0:T(8,128)(2,1)} %multiply_convert_fusion.1.x_ref), custom_call_target="tpu_custom_call" | custom-call | tf_op jit(solution)/shard_map/pallas_call | solution.py:311
  238.2 38.9 %all-gather.5.cloned.1.call-done = bf16[8,288,2048]{2,1,0:T(8,128)(2,1)} async-done(((bf16[1,288,2048]{2,1,0:T(8,128)(2,1)}), bf16[8,288,2048]{2,1,0:T(8,128)(2,1)}) %all-gather.5.cloned.1.call-update) | async-done | bytes 9437200 | tf_op jit(solution)/shard_map/all_gather | solution.py:548
  279.2 3.8 reshape.391
  283.0 3.9 reshape_reshape.3
  304.7 26.2 %shard_map.205 = f32[128,1536]{1,0:T(8,128)} custom-call(f32[4,128,1536]{2,1,0:T(8,128)} %fusion.60.p_ref), custom_call_target="tpu_custom_call" | custom-call | tf_op jit(solution)/shard_map/pallas_call | solution.py:354
  331.0 7.9 fusion.61.p_ref
  338.9 26.0 %shard_map.207 = f32[128,1536]{1,0:T(8,128)} custom-call(f32[4,128,1536]{2,1,0:T(8,128)} %fusion.61.p_ref), custom_call_target="tpu_custom_call" | custom-call | tf_op jit(solution)/shard_map/pallas_call | solution.py:354
  369.1 15.4 %fusion.19 = bf16[128,1536]{1,0:T(8,128)(2,1)} fusion(bf16[1536,4736]{1,0:T(8,128)(2,1)} %all-gather.3.cloned.1.call-done, f32[128,1536]{1,0:T(8,128)S(1)} %get-tuple-element.56), kind=kOutput, calls=%fused_computation.30 | convolution fusion | flops 604372992 | bytes 5898240 | tf_op jit(solution)/shard_map/dot_general | solution.py:63
  405.5 94.1 %shard_map.208 = f32[128,1536]{1,0:T(8,128)} custom-call(f32[128,1536]{1,0:T(8,128)} %fusion.40.own_ref, bf16[4,128,1536]{2,1,0:T(8,128)(2,1)} %bitcast.146), custom_call_target="tpu_custom_call" | custom-call | tf_op jit(solution)/shard_map/pallas_call | solution.py:163
  503.1 6.6 convolution_convert_fusion.1
  513.3 4.9 reshape.379
  525.0 8.6 %fusion.38 = (bf16[1536]{0:T(1024)(128)(2,1)S(1)}, f32[128]{0:T(128)}, f32[128,1536]{1,0:T(8,128)}) fusion(bf16[1,128,1536]{2,1,0:T(8,128)(2,1)S(1)} %copy-done.10, f32[128]{0:T(128)} %copy-done.42, f32[1536]{0:T(1024)S(1)} %get-tuple-element.36, bf16[1536,4736]{1,0:T(8,128)(2,1)} %all-gather.3.cloned.1.call-done, bf16[128,768]{0,1:T(8,128)(2,1)} %copy.118, ...), kind=kOutput, calls=%fused_computation.57 | convolution fusion | flops 1211693440 | bytes 11413504 | tf_op jit(solution)/shard_map/dot_general | solution.py:63
  534.2 4.2 pad_maximum_fusion.1.part_ref
  538.4 94.6 %shard_map.209 = f32[288,2048]{1,0:T(8,128)S(1)} custom-call(bf16[8,288,2048]{2,1,0:T(8,128)(2,1)} %pad_maximum_fusion.1.part_ref), custom_call_target="tpu_custom_call" | custom-call | tf_op jit(solution)/shard_map/pallas_call | solution.py:456
  641.9 7.9 convolution_convert_fusion
  657.3 12.9 %pad_maximum_fusion = bf16[1536,4736]{1,0:T(8,128)(2,1)} fusion(bf16[1536,128]{1,0:T(8,128)(2,1)S(1)} %scatter.4, bf16[1536,1536]{1,0:T(8,128)(2,1)} %convolution_convert_fusion.2, bf16[1536,3072]{1,0:T(8,128)(2,1)} %convolution_convert_fusion), kind=kLoop, calls=%fused_computation.1 | loop fusion | flops 43646976 | bytes 29097984 | tf_op jit(solution)/shard_map/concatenate | solution.py:675
  677.1 157.7 %reduce-scatter.2.cloned.1.call-done = bf16[48,4736]{1,0:T(8,128)(2,1)} async-done(((bf16[1536,4736]{1,0:T(8,128)(2,1)}), bf16[48,4736]{1,0:T(8,128)(2,1)}) %reduce-scatter.2.cloned.1.call-update) | async-done | bytes 454672 | tf_op jit(solution)/shard_map/reduce_scatter | solution.py:674
  (213 shorter events, 121.1 us)
Async XLA Ops:
  7.2 115.6 %all-gather.3.cloned.1.call-start = ((), (), s32[]{:S(2)}) async-start(), calls=%async_computation.3 | async-start | bytes 15003648 | tf_op jit(solution)/shard_map/all_gather | solution.py:500
  16.6 19.1 %all-to-all-start = ((bf16[4,48,2,8,128]{4,3,1,2,0:T(8,128)(2,1)}), bf16[4,48,2,8,128]{4,3,1,2,0:T(8,128)(2,1)S(1)}, u32[]{:S(2)}, u32[]{:S(2)}) async-start(bf16[4,48,2,8,128]{4,3,1,2,0:T(8,128)(2,1)} %copy.108), calls=%async_computation | async-start | bytes 1572864 | tf_op jit(solution)/shard_map/all_to_all | solution.py:544
  20.8 256.3 %all-gather.5.cloned.1.call-start = ((), (), s32[]{:S(2)}) async-start(), calls=%async_computation.4 | async-start | bytes 10616832 | tf_op jit(solution)/shard_map/all_gather | solution.py:548
  21.2 105.3 %copy-start.44 = (s32[1,8]{1,0:T(1,128)S(1)}, s32[1,8]{1,0:T(1,128)}, u32[]{:S(2)}) copy-start(s32[1,8]{1,0:T(1,128)} %param.17) | copy-start | bytes 100
  36.2 106.2 %copy-start.45 = (s32[2]{0:T(128)S(1)}, s32[2]{0:T(128)}, u32[]{:S(2)}) copy-start(s32[2]{0:T(128)} %constant.107.clone.1) | copy-start | bytes 28
  36.2 106.8 %copy-start.9 = (bf16[1,128,1536]{2,1,0:T(8,128)(2,1)S(1)}, bf16[1,128,1536]{2,1,0:T(8,128)(2,1)}, u32[]{:S(2)}) copy-start(bf16[1,128,1536]{2,1,0:T(8,128)(2,1)} %param.16) | copy-start | bytes 1179652
  144.0 9.1 %copy-start.38 = (f32[128,48]{0,1:T(8,128)}, f32[128,48]{0,1:T(8,128)S(1)}, u32[]{:S(2)}) copy-start(f32[128,48]{0,1:T(8,128)S(1)} %get-tuple-element.68) | copy-start | bytes 73732
  144.0 9.1 %copy-start.40 = (f32[128,48]{0,1:T(8,128)}, f32[128,48]{0,1:T(8,128)S(1)}, u32[]{:S(2)}) copy-start(f32[128,48]{0,1:T(8,128)S(1)} %get-tuple-element.67) | copy-start | bytes 73732
  206.0 10.3 %copy-start.11 = (bf16[640,768]{0,1:T(8,128)(2,1)}, bf16[640,768]{0,1:T(8,128)(2,1)S(1)}, u32[]{:S(2)}) copy-start(bf16[640,768]{0,1:T(8,128)(2,1)S(1)} %copy.104) | copy-start | bytes 2949124
  297.7 33.2 %copy-start.31 = (bf16[512,1024]{1,0:T(8,128)(2,1)}, bf16[512,1024]{1,0:T(8,128)(2,1)S(1)}, u32[]{:S(2)}) copy-start(bf16[512,1024]{1,0:T(8,128)(2,1)S(1)} %get-tuple-element.45) | copy-start | bytes 3145732
  297.7 33.2 %copy-start.33 = (bf16[512,1024]{1,0:T(8,128)(2,1)}, bf16[512,1024]{1,0:T(8,128)(2,1)S(1)}, u32[]{:S(2)}) copy-start(bf16[512,1024]{1,0:T(8,128)(2,1)S(1)} %get-tuple-element.46) | copy-start | bytes 3145732
  338.9 26.0 %copy-start.6 = (f32[128,1536]{1,0:T(8,128)S(1)}, f32[128,1536]{1,0:T(8,128)}, u32[]{:S(2)}) copy-start(f32[128,1536]{1,0:T(8,128)} %copy-done.5) | copy-start | bytes 2359300
  338.9 28.1 %copy-start.19 = (f32[128,1536]{1,0:T(8,128)S(1)}, f32[128,1536]{1,0:T(8,128)}, u32[]{:S(2)}) copy-start(f32[128,1536]{1,0:T(8,128)} %shard_map.205) | copy-start | bytes 2359300
  338.9 28.1 %copy-start.30 = (bf16[1,128,1536]{2,1,0:T(8,128)(2,1)S(1)}, bf16[1,128,1536]{2,1,0:T(8,128)(2,1)}, u32[]{:S(2)}) copy-start(bf16[1,128,1536]{2,1,0:T(8,128)(2,1)} %param.27) | copy-start | bytes 1179652
  369.1 140.6 %copy-start.3 = (f32[128,1536]{1,0:T(8,128)}, f32[128,1536]{1,0:T(8,128)S(1)}, u32[]{:S(2)}) copy-start(f32[128,1536]{1,0:T(8,128)S(1)} %get-tuple-element.56) | copy-start | bytes 2359300
  369.1 17.4 %copy-start.1 = (bf16[128,8,2,640]{0,3,2,1:T(8,128)(2,1)S(1)}, bf16[128,8,2,640]{0,3,2,1:T(8,128)(2,1)}, u32[]{:S(2)}) copy-start(bf16[128,8,2,640]{0,3,2,1:T(8,128)(2,1)} %copy-done) | copy-start | bytes 7864324
  405.5 97.6 %copy-start.29 = (bf16[4,128,1536]{2,1,0:T(8,128)(2,1)S(1)}, bf16[4,128,1536]{2,1,0:T(8,128)(2,1)}, u32[]{:S(2)}) copy-start(bf16[4,128,1536]{2,1,0:T(8,128)(2,1)} %shard_map.204) | copy-start | bytes 4718596
  405.5 97.6 %copy-start.32 = (bf16[512,1024]{1,0:T(8,128)(2,1)S(1)}, bf16[512,1024]{1,0:T(8,128)(2,1)}, u32[]{:S(2)}) copy-start(bf16[512,1024]{1,0:T(8,128)(2,1)} %copy-done.31) | copy-start | bytes 3145732
  525.0 9.2 %slice-start = ((s8[6291456]{0:T(1024)(128)(4,1)}), s8[4194304]{0:T(1024)(128)(4,1)S(1)}, s32[]{:S(2)}) async-start(s8[6291456]{0:T(1024)(128)(4,1)} %bitcast.147), calls=%async_computation.6 | async-start | bytes 8388608
  525.0 9.2 %slice-start.1 = ((s8[6291456]{0:T(1024)(128)(4,1)}), s8[2097152]{0:T(1024)(128)(4,1)S(1)}, s32[]{:S(2)}) async-start(s8[6291456]{0:T(1024)(128)(4,1)} %bitcast.147), calls=%async_computation.7 | async-start | bytes 4194304
  633.1 8.7 %copy-start.24 = (bf16[128,16,96]{0,2,1:T(8,128)(2,1)S(1)}, bf16[128,16,96]{0,2,1:T(8,128)(2,1)}, u32[]{:S(2)}) copy-start(bf16[128,16,96]{0,2,1:T(8,128)(2,1)} %copy-done.23) | copy-start | bytes 1179652
  633.1 8.7 %copy-start.35 = (bf16[128,768]{0,1:T(8,128)(2,1)S(1)}, bf16[128,768]{0,1:T(8,128)(2,1)}, u32[]{:S(2)}) copy-start(bf16[128,768]{0,1:T(8,128)(2,1)} %copy.118) | copy-start | bytes 589828
  634.1 15.7 %all-to-all-start.1 = ((bf16[4,48,2048]{2,1,0:T(8,128)(2,1)}), bf16[4,48,2048]{2,1,0:T(8,128)(2,1)S(1)}, u32[]{:S(2)}, u32[]{:S(2)}) async-start(bf16[4,48,2048]{2,1,0:T(8,128)(2,1)} %bitcast.55), calls=%async_computation.1 | async-start | bytes 1572864 | tf_op jit(solution)/shard_map/all_to_all | solution.py:620
  637.6 197.2 %reduce-scatter.2.cloned.1.call-start = ((), (), s32[]{:S(2)}) async-start(), calls=%async_computation.5 | async-start | bytes 15003648 | tf_op jit(solution)/shard_map/reduce_scatter | solution.py:674
  (30 other events, 132.7 us)
Sparse Core Ops, SparseCore 0:
  12.6 110.1 all-gather.2
  126.5 150.5 all-gather.4
  670.4 164.3 reduce-scatter.1

commit v10 on v9

--- a/solution.py
+++ b/solution.py
@@ -615,12 +615,6 @@
         ],
         axis=1,
     )
-    grad_sum = ring_reduce(grad_pack, n_ctx, snake).astype(jnp.bfloat16)
-    down_sum = grad_sum[n_f * rows :].reshape(ff_rows, D)
-    gu_sum = lax.all_to_all(grad_sum[: n_f * rows].reshape(n_f, rows, 2 * units), "fsdp", 0, 0, tiled=True)
-    ff_sum = jnp.transpose(
-        gu_sum.reshape(n_f, rows, 2, n_ctx, chunk), (1, 2, 3, 0, 4)
-    ).reshape(rows, 2 * ff)
     normed_two_grad = fsdp_reduce(
         times_transposed(gate_up_cat, gate_up_tp).reshape(n_f, tok_rows, D), n_f
     )
@@ -652,15 +646,34 @@
         "qgrk,qgrd->kgd", probs_low, attended_grad_low, preferred_element_type=jnp.float32
     ).reshape(win, KVW)
     kv_term = jnp.concatenate([key_term, value_term], axis=1).reshape(back + 1, tok_rows, 2 * KVW)
-    kv_sum = kv_return(kv_term[back], kv_term[:back].astype(jnp.bfloat16), n_ctx, back)
-    key_grad_low = rotate(kv_sum[:, :KVW] * score_scale, query_positions, KVH, -1.0).astype(
-        jnp.bfloat16
-    )
-    value_grad_low = kv_sum[:, KVW:].astype(jnp.bfloat16)
     query_grad_low = rotate(
         query_accum.reshape(tok_rows, D) * score_scale, query_positions, H, -1.0
     ).astype(jnp.bfloat16)
-    projection_cat = jnp.concatenate([query_grad_low, key_grad_low, value_grad_low], axis=1)
+    first_pack = jnp.concatenate(
+        [
+            outer_rows(normed_low, query_grad_low).astype(jnp.bfloat16),
+            outer_rows(attended_low, branch_grad).astype(jnp.bfloat16),
+        ],
+        axis=1,
+    )
+    first_pack, grad_pack = lax.optimization_barrier((first_pack, grad_pack))
+    first_sum = lax.psum_scatter(first_pack, ALL, scatter_dimension=0, tiled=True).astype(jnp.float32)
+    grad_sum = ring_reduce(grad_pack, n_ctx, snake).astype(jnp.bfloat16)
+    down_sum = grad_sum[n_f * rows :].reshape(ff_rows, D)
+    gu_sum = lax.all_to_all(grad_sum[: n_f * rows].reshape(n_f, rows, 2 * units), "fsdp", 0, 0, tiled=True)
+    ff_sum = jnp.transpose(
+        gu_sum.reshape(n_f, rows, 2, n_ctx, chunk), (1, 2, 3, 0, 4)
+    ).reshape(rows, 2 * ff)
+    kv_own = kv_term[back].at[0, 0].add(
+        (grad_sum[0, 0].astype(jnp.float32) + first_sum[0, 0]) * 0.0
+    )
+    kv_sum = kv_return(kv_own, kv_term[:back].astype(jnp.bfloat16), n_ctx, back)
+    key_grad_low = rotate(kv_sum[:, :KVW] * score_scale, query_positions, KVH, -1.0).astype(
+        jnp.bfloat16
+    )
+    value_grad_low = kv_sum[:, KVW:].astype(jnp.bfloat16)
+    kv_grad_cat = jnp.concatenate([key_grad_low, value_grad_low], axis=1)
+    projection_cat = jnp.concatenate([query_grad_low, kv_grad_cat], axis=1)
     normed_grad = times_transposed(projection_cat, qkv_full)
     gain_one_term = jnp.sum(normed_grad * normed_one, axis=0)
     scaled_one = normed_grad * gain_one_f
@@ -670,12 +683,10 @@
     gain_term_cols = jnp.pad(
         jnp.stack([gain_one_term, gain_two_term], axis=1), ((0, 0), (0, GAIN_PAD - 2))
     )
-    gain_term_cols = gain_term_cols.at[0, GAIN_PAD - 1].set(ff_sum[0, 0].astype(jnp.float32) * 0.0)
-    attention_sum = lax.psum_scatter(
+    second_sum = lax.psum_scatter(
         jnp.concatenate(
             [
-                outer_rows(normed_low, projection_cat).astype(jnp.bfloat16),
-                outer_rows(attended_low, branch_grad).astype(jnp.bfloat16),
+                outer_rows(normed_low, kv_grad_cat).astype(jnp.bfloat16),
                 gain_term_cols.astype(jnp.bfloat16),
             ],
             axis=1,
@@ -688,12 +699,12 @@
     return (
         layer_out.astype(jnp.bfloat16)[None],
         tokens_grad[None],
-        attention_sum[:, c_g],
-        attention_sum[:, :c_k],
-        attention_sum[:, c_k:c_v],
-        attention_sum[:, c_v:c_o],
-        attention_sum[:, c_o:c_g],
-        attention_sum[:, c_g + 1],
+        second_sum[:, 2 * KVW],
+        first_sum[:, :D],
+        second_sum[:, :KVW],
+        second_sum[:, KVW : 2 * KVW],
+        first_sum[:, D:],
+        second_sum[:, 2 * KVW + 1],
         ff_sum[:, :ff],
         ff_sum[:, ff : 2 * ff],
         down_sum.astype(jnp.float32),

time: 849 us -> 825 us (0.972)
  waiting for transfers between devices: 297 us -> 256 us
  Pallas kernels: 320 us -> 358 us
  matrix products: 89.4 us -> 70.9 us
  other arithmetic: 46.4 us -> 36.3 us
    reduce_scatter x1, waiting for transfers between devices: 158 us -> 22.3 us  [body(): lax.psum_scatter(first_pack, ALL, scatter_dimension=0, tiled=True)]
    unnamed x3 -> x5, waiting for transfers between devices: 0.05 us -> 82.2 us
    pallas_call x1, Pallas kernels: 94.6 us -> 171 us  [ring_reduce(): pl.pallas_call(functools.partial(ring_reduce_kernel, n, snake), out_shape...]
    pallas_call x1, Pallas kernels: 94.1 us -> 55.6 us  [kv_return(): pl.pallas_call(functools.partial(kv_return_kernel, n_ctx, back), out_shap...]
    unnamed x104 -> x108, local copies, waits for them, and re-layouts: 7.94 us -> 21.8 us
    all_to_all x1, waiting for transfers between devices: 0.01 us -> 10.5 us  [body(): lax.all_to_all(grad_sum[:n_f * rows].reshape(n_f, rows, 2 * units), 'fsdp...]
    dot_general x4, matrix products: 34.5 us -> 24.2 us  [times_transposed(): lax.dot_general(left, right, (((1,), (1,)), ((), ())), preferred_element_...]
    dot_general x4 -> x5, matrix products: 21.6 us -> 16 us  [outer_rows(): lax.dot_general(left, right, (((0,), (0,)), ((), ())), preferred_element_...]
  transfers between devices with their start and end apart: 5 -> 6, of which waited for: 4 -> 6; matrix products, arithmetic and copies ran while one was open for 7% -> 7% of each run, Pallas kernels for 9% -> 31%
where the time goes in v10:
time: 825 us; the launch traced here: 819 us
  Pallas kernels  358 us (43%)
  waiting for transfers between devices  256 us (31%)
  local copies, waits for them, and re-layouts  72.1 us (9%)
  matrix products  70.9 us (9%)
  other arithmetic  36.3 us (4%)
  between operations  18.1 us (2%)
    pallas_call x1, Pallas kernels, ring_reduce(): pl.pallas_call(functools.partial(ring_reduce_kernel, n, snake), out_shape...  171 us
    all_gather x1, waiting for transfers between devices, body(): lax.all_gather(jnp.concatenate([query_weight, key_weight, value_weight, o...  85.9 us
    unnamed x5, waiting for transfers between devices  82.2 us
    pallas_call x1, Pallas kernels, kv_return(): pl.pallas_call(functools.partial(kv_return_kernel, n_ctx, back), out_shap...  55.6 us
    pallas_call x2, Pallas kernels, quad_reduce(): pl.pallas_call(quad_reduce_kernel, out_shape=jax.ShapeDtypeStruct(block,...  52 us
    pallas_call x1, Pallas kernels, kv_share(): pl.pallas_call(functools.partial(kv_share_kernel, n_ctx, back), out_shape...  48.9 us
    all_gather x1, waiting for transfers between devices, body(): ff_stack = lax.all_gather(ff_pack, 'ctx', axis=0, tiled=False)  40.3 us
    pallas_call x2, Pallas kernels, quad_gather(): pl.pallas_call(quad_gather_kernel, out_shape=jax.ShapeDtypeStruct((4,) +...  29.9 us
  transfers between devices with their start and end apart: 6, of which 6 were waited for; matrix products, arithmetic and copies ran while one was open for 7% of the time, Pallas kernels for 31%

profile of v10, /device:TPU:0, one launch (start us, length us, event | category | flops | bytes accessed | tf_op | source)
XLA Modules:
  0.0 818.8 jit_solution(3997932170919773431)
XLA Ops:
  16.6 4.2 all-to-all-start
  21.2 14.6 %all-to-all-done = bf16[4,48,2,8,128]{4,3,1,2,0:T(8,128)(2,1)S(1)} async-done(((bf16[4,48,2,8,128]{4,3,1,2,0:T(8,128)(2,1)}), bf16[4,48,2,8,128]{4,3,1,2,0:T(8,128)(2,1)S(1)}, u32[]{:S(2)}, u32[]{:S(2)}) %all-to-all-start) | async-done | bytes 786464 | tf_op jit(solution)/shard_map/all_to_all | solution.py:544
  36.9 85.9 %all-gather.3.cloned.1.call-done = bf16[1536,4736]{1,0:T(8,128)(2,1)} async-done(((bf16[48,4736]{1,0:T(8,128)(2,1)}), bf16[1536,4736]{1,0:T(8,128)(2,1)}) %all-gather.3.cloned.1.call-update) | async-done | bytes 14549008 | tf_op jit(solution)/shard_map/all_gather | solution.py:500
  126.6 14.8 %shard_map.206 = bf16[4,128,1536]{2,1,0:T(8,128)(2,1)} custom-call(bf16[128,1536]{1,0:T(8,128)(2,1)} %bitcast.208), custom_call_target="tpu_custom_call" | custom-call | tf_op jit(solution)/shard_map/pallas_call | solution.py:311
  145.3 5.2 fusion.3
  153.0 48.9 %shard_map.203 = bf16[5,128,1536]{2,1,0:T(8,128)(2,1)} custom-call(bf16[128,1536]{1,0:T(8,128)(2,1)} %pad_maximum_fusion.5.kv_ref), custom_call_target="tpu_custom_call" | custom-call | tf_op jit(solution)/shard_map/pallas_call | solution.py:116
  206.5 4.4 fusion.75
  221.1 15.1 %shard_map.204 = bf16[4,128,1536]{2,1,0:T(8,128)(2,1)} custom-call(bf16[128,1536]{1,0:T(8,128)(2,1)} %multiply_convert_fusion.1.x_ref), custom_call_target="tpu_custom_call" | custom-call | tf_op jit(solution)/shard_map/pallas_call | solution.py:311
  236.2 40.3 %all-gather.5.cloned.1.call-done = bf16[8,288,2048]{2,1,0:T(8,128)(2,1)} async-done(((bf16[1,288,2048]{2,1,0:T(8,128)(2,1)}), bf16[8,288,2048]{2,1,0:T(8,128)(2,1)}) %all-gather.5.cloned.1.call-update) | async-done | bytes 9437200 | tf_op jit(solution)/shard_map/all_gather | solution.py:548
  298.2 5.9 convolution_convert_fusion
  311.1 26.1 %shard_map.205 = f32[128,1536]{1,0:T(8,128)} custom-call(f32[4,128,1536]{2,1,0:T(8,128)} %fusion.78.p_ref), custom_call_target="tpu_custom_call" | custom-call | tf_op jit(solution)/shard_map/pallas_call | solution.py:354
  337.2 4.9 reshape.389
  342.2 8.5 %fusion.79.p_ref = f32[4,128,1536]{2,1,0:T(8,128)} fusion(bf16[4,128,2048]{2,1,0:T(8,128)(2,1)} %bitcast.197, bf16[1536,2048,1]{1,0,2:T(8,128)(2,1)} %bitcast.178), kind=kOutput, calls=%fused_computation.152 | convolution fusion | flops 3221225472 | bytes 11534336 | tf_op jit(solution)/shard_map/dot_general | solution.py:63
  350.6 25.9 %shard_map.207 = f32[128,1536]{1,0:T(8,128)} custom-call(f32[4,128,1536]{2,1,0:T(8,128)} %fusion.79.p_ref), custom_call_target="tpu_custom_call" | custom-call | tf_op jit(solution)/shard_map/pallas_call | solution.py:354
  385.3 4.7 fusion.19
  393.4 4.1 fusion.6
  404.6 4.7 pad_maximum_fusion
  421.9 171.3 %shard_map.208 = f32[288,2048]{1,0:T(8,128)S(1)} custom-call(bf16[8,288,2048]{2,1,0:T(8,128)(2,1)} %pad_maximum_fusion.1.part_ref), custom_call_target="tpu_custom_call" | custom-call | tf_op jit(solution)/shard_map/pallas_call | solution.py:456
  597.1 22.3 %reduce-scatter.5.cloned.1.call-done = bf16[48,3072]{1,0:T(8,128)(2,1)} async-done(((bf16[1536,3072]{1,0:T(8,128)(2,1)}), bf16[48,3072]{1,0:T(8,128)(2,1)}) %reduce-scatter.5.cloned.1.call-update) | async-done | bytes 294928 | tf_op jit(solution)/shard_map/reduce_scatter | solution.py:660
  623.8 55.6 %shard_map.209 = f32[128,1536]{1,0:T(8,128)} custom-call(f32[128,1536]{1,0:T(8,128)} %scatter-add.9.own_ref, bf16[4,128,1536]{2,1,0:T(8,128)(2,1)} %bitcast.181), custom_call_target="tpu_custom_call" | custom-call | tf_op jit(solution)/shard_map/pallas_call | solution.py:163
  682.0 8.4 %fusion.40 = (bf16[1536]{0:T(1024)(128)(2,1)S(1)}, f32[128]{0:T(128)}, f32[128,1536]{1,0:T(8,128)}) fusion(bf16[1,128,1536]{2,1,0:T(8,128)(2,1)S(1)} %copy-done.3, f32[128]{0:T(128)S(1)} %copy-done.38, f32[1536]{0:T(1024)S(1)} %get-tuple-element.95, bf16[1536,4736]{1,0:T(8,128)(2,1)} %all-gather.3.cloned.1.call-done, bf16[128,768]{0,1:T(8,128)(2,1)S(1)} %copy.135, ...), kind=kOutput, calls=%fused_computation.62 | convolution fusion | flops 1211693440 | bytes 11413504 | tf_op jit(solution)/shard_map/dot_general | solution.py:63
  694.6 7.8 copy.151
  708.2 10.5 %all-to-all-done.1 = bf16[4,48,2048]{2,1,0:T(8,128)(2,1)S(1)} async-done(((bf16[4,48,2048]{2,1,0:T(8,128)(2,1)}), bf16[4,48,2048]{2,1,0:T(8,128)(2,1)S(1)}, u32[]{:S(2)}, u32[]{:S(2)}) %all-to-all-start.1) | async-done | bytes 786464 | tf_op jit(solution)/shard_map/all_to_all | solution.py:663
  726.4 82.2 %reduce-scatter.7.cloned.1.call-done = bf16[48,1664]{1,0:T(8,128)(2,1)} async-done(((bf16[1536,1664]{1,0:T(8,128)(2,1)}), bf16[48,1664]{1,0:T(8,128)(2,1)}) %reduce-scatter.7.cloned.1.call-update) | async-done | bytes 159760
  (220 shorter events, 124.4 us)
Async XLA Ops:
  7.2 115.6 %all-gather.3.cloned.1.call-start = ((), (), s32[]{:S(2)}) async-start(), calls=%async_computation.4 | async-start | bytes 15003648 | tf_op jit(solution)/shard_map/all_gather | solution.py:500
  12.5 8.4 %copy-start.31 = (bf16[128,1536]{1,0:T(8,128)(2,1)S(1)}, bf16[128,1536]{1,0:T(8,128)(2,1)}, u32[]{:S(2)}) copy-start(bf16[128,1536]{1,0:T(8,128)(2,1)} %param.26) | copy-start | bytes 1179652
  16.6 19.1 %all-to-all-start = ((bf16[4,48,2,8,128]{4,3,1,2,0:T(8,128)(2,1)}), bf16[4,48,2,8,128]{4,3,1,2,0:T(8,128)(2,1)S(1)}, u32[]{:S(2)}, u32[]{:S(2)}) async-start(bf16[4,48,2,8,128]{4,3,1,2,0:T(8,128)(2,1)} %copy.122), calls=%async_computation | async-start | bytes 1572864 | tf_op jit(solution)/shard_map/all_to_all | solution.py:544
  20.8 255.6 %all-gather.5.cloned.1.call-start = ((), (), s32[]{:S(2)}) async-start(), calls=%async_computation.5 | async-start | bytes 10616832 | tf_op jit(solution)/shard_map/all_gather | solution.py:548
  21.2 105.3 %copy-start.43 = (s32[1,8]{1,0:T(1,128)S(1)}, s32[1,8]{1,0:T(1,128)}, u32[]{:S(2)}) copy-start(s32[1,8]{1,0:T(1,128)} %param.17) | copy-start | bytes 100
  36.2 105.7 %copy-start.3 = (bf16[1,128,1536]{2,1,0:T(8,128)(2,1)S(1)}, bf16[1,128,1536]{2,1,0:T(8,128)(2,1)}, u32[]{:S(2)}) copy-start(bf16[1,128,1536]{2,1,0:T(8,128)(2,1)} %param.16) | copy-start | bytes 1179652
  126.4 493.0 %reduce-scatter.5.cloned.1.call-start = ((), (), s32[]{:S(2)}) async-start(), calls=%async_computation.6 | async-start | bytes 9732096 | tf_op jit(solution)/shard_map/reduce_scatter | solution.py:660
  142.0 8.5 %copy-start.36 = (f32[128]{0:T(128)}, f32[128]{0:T(128)S(1)}, u32[]{:S(2)}) copy-start(f32[128]{0:T(128)S(1)} %add_rsqrt_fusion.1) | copy-start | bytes 1540
  142.8 62.0 %copy-start.28 = (f32[128,48]{0,1:T(8,128)}, f32[128,48]{0,1:T(8,128)S(1)}, u32[]{:S(2)}) copy-start(f32[128,48]{0,1:T(8,128)S(1)} %get-tuple-element.127) | copy-start | bytes 73732
  204.2 6.8 copy-start.12
  204.9 9.3 %copy-start.11 = (bf16[640,768]{0,1:T(8,128)(2,1)}, bf16[640,768]{0,1:T(8,128)(2,1)S(1)}, u32[]{:S(2)}) copy-start(bf16[640,768]{0,1:T(8,128)(2,1)S(1)} %copy.118) | copy-start | bytes 2949124
  214.2 5.1 copy-start
  289.5 4.6 copy-start.23
  376.6 5.1 copy-start.18
  385.3 8.1 copy-start.41
  391.9 8.7 %slice-start.2 = ((s8[6291456]{0:T(1024)(128)(4,1)}), s8[4194304]{0:T(1024)(128)(4,1)S(1)}, s32[]{:S(2)}) async-start(s8[6291456]{0:T(1024)(128)(4,1)} %bitcast.182), calls=%async_computation.10 | async-start | bytes 8388608
  393.4 7.2 slice-start.3
  399.1 5.5 slice-start
  409.4 399.2 %reduce-scatter.7.cloned.1.call-start = ((), (), s32[]{:S(2)}) async-start(), calls=%async_computation.7 | async-start | bytes 5271552
  597.1 84.5 %copy-start.30 = (f32[128,48]{0,1:T(8,128)S(1)}, f32[128,48]{0,1:T(8,128)}, u32[]{:S(2)}) copy-start(f32[128,48]{0,1:T(8,128)} %copy-done.28) | copy-start | bytes 73732
  597.1 84.5 %copy-start.33 = (f32[128,48]{0,1:T(8,128)S(1)}, f32[128,48]{0,1:T(8,128)}, u32[]{:S(2)}) copy-start(f32[128,48]{0,1:T(8,128)} %get-tuple-element.125) | copy-start | bytes 73732
  623.8 58.2 %copy-start.20 = (bf16[128,16,96]{0,2,1:T(8,128)(2,1)S(1)}, bf16[128,16,96]{0,2,1:T(8,128)(2,1)}, u32[]{:S(2)}) copy-start(bf16[128,16,96]{0,2,1:T(8,128)(2,1)} %copy-done.19) | copy-start | bytes 1179652
  623.8 58.2 %copy-start.38 = (f32[128]{0:T(128)S(1)}, f32[128]{0:T(128)}, u32[]{:S(2)}) copy-start(f32[128]{0:T(128)} %copy-done.36) | copy-start | bytes 1540
  703.3 15.3 %all-to-all-start.1 = ((bf16[4,48,2048]{2,1,0:T(8,128)(2,1)}), bf16[4,48,2048]{2,1,0:T(8,128)(2,1)S(1)}, u32[]{:S(2)}, u32[]{:S(2)}) async-start(bf16[4,48,2048]{2,1,0:T(8,128)(2,1)} %bitcast.58), calls=%async_computation.2 | async-start | bytes 1572864 | tf_op jit(solution)/shard_map/all_to_all | solution.py:663
  (31 other events, 81.9 us)
Sparse Core Ops, SparseCore 0:
  12.6 110.1 all-gather.2
  126.5 149.8 all-gather.4
  409.5 209.8 reduce-scatter.4
  702.5 106.0 reduce-scatter.6

commit v11 on v6

--- a/solution.py
+++ b/solution.py
@@ -504,7 +504,6 @@
     sigmoid = jax.nn.sigmoid(gate_pre)
     hidden_low = (gate_pre * sigmoid * up_pre).astype(jnp.bfloat16)
     ff_part = jnp.dot(hidden_low, down_tp, preferred_element_type=jnp.float32)
-    layer_out = middle + fsdp_reduce(ff_part.reshape(n_f, tok_rows, D), n_f)
 
     grad_out = cotangent[0]
     grad_all = fsdp_gather(grad_out, n_f).reshape(group_tokens, D)
@@ -574,19 +573,19 @@
         jnp.stack([gain_one_term, gain_two_term], axis=1), ((0, 0), (0, GAIN_PAD - 2))
     )
     gain_term_cols = gain_term_cols.at[0, GAIN_PAD - 1].set(ff_sum[0, 0].astype(jnp.float32) * 0.0)
+    attention_pack = jnp.concatenate(
+        [
+            outer_rows(normed_low, projection_cat).astype(jnp.bfloat16),
+            outer_rows(attended_low, branch_grad).astype(jnp.bfloat16),
+            gain_term_cols.astype(jnp.bfloat16),
+        ],
+        axis=1,
+    )
     attention_sum = lax.psum_scatter(
-        jnp.concatenate(
-            [
-                outer_rows(normed_low, projection_cat).astype(jnp.bfloat16),
-                outer_rows(attended_low, branch_grad).astype(jnp.bfloat16),
-                gain_term_cols.astype(jnp.bfloat16),
-            ],
-            axis=1,
-        ),
-        ALL,
-        scatter_dimension=0,
-        tiled=True,
+        attention_pack, ALL, scatter_dimension=0, tiled=True
     ).astype(jnp.float32)
+    ff_part = ff_part.at[0, 0].add(attention_pack[0, 0].astype(jnp.float32) * 0.0)
+    layer_out = middle + fsdp_reduce(ff_part.reshape(n_f, tok_rows, D), n_f)
     ff_sum = ff_sum.astype(jnp.float32)
     return (
         layer_out.astype(jnp.bfloat16)[None],

time: 768 us -> 752 us (0.979)
  waiting for transfers between devices: 299 us -> 281 us
  Pallas kernels: 256 us -> 247 us
  local copies, waits for them, and re-layouts: 59.1 us -> 66.8 us
    reduce_scatter x1, waiting for transfers between devices: 156 us -> 134 us  [body(): lax.psum_scatter(attention_pack, ALL, scatter_dimension=0, tiled=True)]
    pallas_call x1, Pallas kernels: 125 us -> 117 us  [kv_return(): pl.pallas_call(functools.partial(kv_return_kernel, n_ctx, back), out_shap...]
  transfers between devices with their start and end apart: 7 -> 7, of which waited for: 5 -> 5; matrix products, arithmetic and copies ran while one was open for 18% -> 19% of each run, Pallas kernels for 34% -> 33%
where the time goes in v11:
time: 752 us; the launch traced here: 745 us
  waiting for transfers between devices  281 us (37%)
  Pallas kernels  247 us (33%)
  matrix products  79.9 us (11%)
  local copies, waits for them, and re-layouts  66.8 us (9%)
  other arithmetic  43.4 us (6%)
  between operations  19.5 us (3%)
  starting transfers between devices  8 us (1%)
    reduce_scatter x1, waiting for transfers between devices, body(): lax.psum_scatter(attention_pack, ALL, scatter_dimension=0, tiled=True)  134 us
    pallas_call x1, Pallas kernels, kv_return(): pl.pallas_call(functools.partial(kv_return_kernel, n_ctx, back), out_shap...  117 us
    all_gather x1, waiting for transfers between devices, body(): lax.all_gather(jnp.concatenate([query_weight, key_weight, value_weight, o...  85.9 us
    pallas_call x2, Pallas kernels, quad_reduce(): pl.pallas_call(quad_reduce_kernel, out_shape=jax.ShapeDtypeStruct(block,...  51.7 us
    pallas_call x1, Pallas kernels, kv_share(): pl.pallas_call(functools.partial(kv_share_kernel, n_ctx, back), out_shape...  48.9 us
    all_gather x1, waiting for transfers between devices, body(): ff_stack = lax.all_gather(ff_pack, 'ctx', axis=0, tiled=False)  43.6 us
    pallas_call x2, Pallas kernels, quad_gather(): pl.pallas_call(quad_gather_kernel, out_shape=jax.ShapeDtypeStruct((4,) +...  29.7 us
    dot_general x4, matrix products, times_transposed(): lax.dot_general(left, right, (((1,), (1,)), ((), ())), preferred_element_...  25.5 us
  transfers between devices with their start and end apart: 7, of which 5 were waited for; matrix products, arithmetic and copies ran while one was open for 19% of the time, Pallas kernels for 33%

profile of v11, /device:TPU:0, one launch (start us, length us, event | category | flops | bytes accessed | tf_op | source)
XLA Modules:
  0.0 745.4 jit_solution(12620212719593192390)
XLA Ops:
  16.6 4.2 all-to-all-start
  21.2 14.6 %all-to-all-done = bf16[4,48,2,8,128]{4,3,1,2,0:T(8,128)(2,1)S(1)} async-done(((bf16[4,48,2,8,128]{4,3,1,2,0:T(8,128)(2,1)}), bf16[4,48,2,8,128]{4,3,1,2,0:T(8,128)(2,1)S(1)}, u32[]{:S(2)}, u32[]{:S(2)}) %all-to-all-start) | async-done | bytes 786464 | tf_op jit(solution)/shard_map/all_to_all | solution.py:452
  36.9 85.9 %all-gather.3.cloned.1.call-done = bf16[1536,4736]{1,0:T(8,128)(2,1)} async-done(((bf16[48,4736]{1,0:T(8,128)(2,1)}), bf16[1536,4736]{1,0:T(8,128)(2,1)}) %all-gather.3.cloned.1.call-update) | async-done | bytes 14549008 | tf_op jit(solution)/shard_map/all_gather | solution.py:408
  126.6 14.9 %shard_map.205 = bf16[4,128,1536]{2,1,0:T(8,128)(2,1)} custom-call(bf16[128,1536]{1,0:T(8,128)(2,1)} %bitcast.170), custom_call_target="tpu_custom_call" | custom-call | tf_op jit(solution)/shard_map/pallas_call | solution.py:311
  144.1 5.2 fusion.3
  151.7 48.9 %shard_map.203 = bf16[5,128,1536]{2,1,0:T(8,128)(2,1)} custom-call(bf16[128,1536]{1,0:T(8,128)(2,1)} %pad_maximum_fusion.4.kv_ref), custom_call_target="tpu_custom_call" | custom-call | tf_op jit(solution)/shard_map/pallas_call | solution.py:116
  205.5 4.5 fusion.57
  219.1 14.8 %shard_map.204 = bf16[4,128,1536]{2,1,0:T(8,128)(2,1)} custom-call(bf16[128,1536]{1,0:T(8,128)(2,1)} %multiply_convert_fusion.1.x_ref), custom_call_target="tpu_custom_call" | custom-call | tf_op jit(solution)/shard_map/pallas_call | solution.py:311
  233.9 43.6 %all-gather.5.cloned.1.call-done = bf16[8,288,2048]{2,1,0:T(8,128)(2,1)} async-done(((bf16[1,288,2048]{2,1,0:T(8,128)(2,1)}), bf16[8,288,2048]{2,1,0:T(8,128)(2,1)}) %all-gather.5.cloned.1.call-update) | async-done | bytes 9437200 | tf_op jit(solution)/shard_map/all_gather | solution.py:456
  277.5 4.0 slice.232
  281.6 6.0 reshape_reshape.3
  300.7 5.7 convolution_convert_fusion.1
  307.7 8.6 %fusion.61.p_ref = f32[4,128,1536]{2,1,0:T(8,128)} fusion(bf16[4,128,2048]{2,1,0:T(8,128)(2,1)} %bitcast.159, bf16[1536,2048,1]{1,0,2:T(8,128)(2,1)} %bitcast.143), kind=kOutput, calls=%fused_computation.133 | convolution fusion | flops 3221225472 | bytes 11534336 | tf_op jit(solution)/shard_map/dot_general | solution.py:63
  316.3 26.1 %shard_map.206 = f32[128,1536]{1,0:T(8,128)} custom-call(f32[4,128,1536]{2,1,0:T(8,128)} %fusion.61.p_ref), custom_call_target="tpu_custom_call" | custom-call | tf_op jit(solution)/shard_map/pallas_call | solution.py:354
  346.3 5.3 fusion.19
  353.5 5.3 convolution_convert_fusion.3
  360.1 4.1 fusion.6
  380.7 116.8 %shard_map.207 = f32[128,1536]{1,0:T(8,128)} custom-call(f32[128,1536]{1,0:T(8,128)} %fusion.40.own_ref, bf16[4,128,1536]{2,1,0:T(8,128)(2,1)} %bitcast.144), custom_call_target="tpu_custom_call" | custom-call | tf_op jit(solution)/shard_map/pallas_call | solution.py:163
  507.9 8.1 %fusion.38 = (bf16[1536]{0:T(1024)(128)(2,1)S(1)}, f32[128]{0:T(128)S(1)}, f32[128,1536]{1,0:T(8,128)}) fusion(bf16[1,128,1536]{2,1,0:T(8,128)(2,1)S(1)} %copy-done.10, f32[128]{0:T(128)S(1)} %add_rsqrt_fusion.1, f32[1536]{0:T(1024)S(1)} %get-tuple-element.52, bf16[1536,4736]{1,0:T(8,128)(2,1)} %all-gather.3.cloned.1.call-done, ...), kind=kOutput, calls=%fused_computation.56 | convolution fusion | flops 1211693440 | bytes 11413504 | tf_op jit(solution)/shard_map/dot_general | solution.py:63
  526.3 6.3 convolution_convert_fusion
  542.6 13.0 %pad_maximum_fusion = bf16[1536,4736]{1,0:T(8,128)(2,1)} fusion(bf16[1536,128]{1,0:T(8,128)(2,1)S(1)} %scatter.4, bf16[1536,1536]{1,0:T(8,128)(2,1)} %convolution_convert_fusion.2, bf16[1536,3072]{1,0:T(8,128)(2,1)} %convolution_convert_fusion), kind=kLoop, calls=%fused_computation.1 | loop fusion | flops 43646976 | bytes 29097984 | tf_op jit(solution)/shard_map/concatenate | solution.py:576
  556.8 4.0 fusion.60
  565.6 25.5 %shard_map.208 = f32[128,1536]{1,0:T(8,128)} custom-call(f32[4,128,1536]{2,1,0:T(8,128)} %bitcast.155), custom_call_target="tpu_custom_call" | custom-call | tf_op jit(solution)/shard_map/pallas_call | solution.py:354
  598.8 134.3 %reduce-scatter.6.cloned.1.call-done = bf16[48,4736]{1,0:T(8,128)(2,1)} async-done(((bf16[1536,4736]{1,0:T(8,128)(2,1)}), bf16[48,4736]{1,0:T(8,128)(2,1)}) %reduce-scatter.6.cloned.1.call-update) | async-done | bytes 454672 | tf_op jit(solution)/shard_map/reduce_scatter | solution.py:584
  (179 shorter events, 115.9 us)
Async XLA Ops:
  7.2 115.6 %all-gather.3.cloned.1.call-start = ((), (), s32[]{:S(2)}) async-start(), calls=%async_computation.5 | async-start | bytes 15003648 | tf_op jit(solution)/shard_map/all_gather | solution.py:408
  12.5 8.4 %copy-start.28 = (bf16[128,1536]{1,0:T(8,128)(2,1)S(1)}, bf16[128,1536]{1,0:T(8,128)(2,1)}, u32[]{:S(2)}) copy-start(bf16[128,1536]{1,0:T(8,128)(2,1)} %param.28) | copy-start | bytes 1179652
  16.6 19.1 %all-to-all-start = ((bf16[4,48,2,8,128]{4,3,1,2,0:T(8,128)(2,1)}), bf16[4,48,2,8,128]{4,3,1,2,0:T(8,128)(2,1)S(1)}, u32[]{:S(2)}, u32[]{:S(2)}) async-start(bf16[4,48,2,8,128]{4,3,1,2,0:T(8,128)(2,1)} %copy.107), calls=%async_computation | async-start | bytes 1572864 | tf_op jit(solution)/shard_map/all_to_all | solution.py:452
  20.8 256.7 %all-gather.5.cloned.1.call-start = ((), (), s32[]{:S(2)}) async-start(), calls=%async_computation.6 | async-start | bytes 10616832 | tf_op jit(solution)/shard_map/all_gather | solution.py:456
  21.2 105.2 %copy-start.29 = (s32[1,8]{1,0:T(1,128)S(1)}, s32[1,8]{1,0:T(1,128)}, u32[]{:S(2)}) copy-start(s32[1,8]{1,0:T(1,128)} %param.19) | copy-start | bytes 100
  36.2 105.7 %copy-start.8 = (bf16[1,128,1536]{2,1,0:T(8,128)(2,1)S(1)}, bf16[1,128,1536]{2,1,0:T(8,128)(2,1)}, u32[]{:S(2)}) copy-start(bf16[1,128,1536]{2,1,0:T(8,128)(2,1)} %param.18) | copy-start | bytes 1179652
  126.3 393.3 %reduce-scatter.4.cloned.1.call-start = ((), (), s32[]{:S(2)}) async-start(), calls=%async_computation.7 | async-start | bytes 7077888 | tf_op jit(solution)/shard_map/reduce_scatter | solution.py:521
  202.9 7.1 copy-start.13
  205.5 4.5 copy-start.20
  287.6 3.5 copy-start.23
  291.1 3.5 copy-start.6
  291.1 4.2 copy-start.14
  291.1 4.6 copy-start.22
  306.5 289.1 %reduce-scatter.8.cloned.1.call-start = ((), (), s32[]{:S(2)}) async-start(), calls=%async_computation.9 | async-start | bytes 3538944 | tf_op jit(solution)/shard_map/reduce_scatter | solution.py:510
  360.1 5.7 copy-start.21
  380.7 125.1 %copy-start.3 = (bf16[128,8,2,640]{0,3,2,1:T(8,128)(2,1)S(1)}, bf16[128,8,2,640]{0,3,2,1:T(8,128)(2,1)}, u32[]{:S(2)}) copy-start(bf16[128,8,2,640]{0,3,2,1:T(8,128)(2,1)} %copy-done.2) | copy-start | bytes 7864324
  507.9 8.2 %copy-start.19 = (bf16[128,16,96]{0,2,1:T(8,128)(2,1)}, bf16[128,16,96]{0,2,1:T(8,128)(2,1)S(1)}, u32[]{:S(2)}) copy-start(bf16[128,16,96]{0,2,1:T(8,128)(2,1)S(1)} %pad_maximum_fusion.6) | copy-start | bytes 1179652
  507.9 8.1 %copy-start.5 = (f32[128,1536]{1,0:T(8,128)S(1)}, f32[128,1536]{1,0:T(8,128)}, u32[]{:S(2)}) copy-start(f32[128,1536]{1,0:T(8,128)} %copy-done.4) | copy-start | bytes 2359300
  507.9 8.1 %copy-start.17 = (bf16[128,8,2,96]{0,3,2,1:T(8,128)(2,1)S(1)}, bf16[128,8,2,96]{0,3,2,1:T(8,128)(2,1)}, u32[]{:S(2)}) copy-start(bf16[128,8,2,96]{0,3,2,1:T(8,128)(2,1)} %copy-done.16) | copy-start | bytes 1179652
  519.6 6.7 copy-start.11
  519.6 6.7 copy-start.26
  519.6 15.3 %all-to-all-start.1 = ((bf16[4,48,2048]{2,1,0:T(8,128)(2,1)}), bf16[4,48,2048]{2,1,0:T(8,128)(2,1)S(1)}, u32[]{:S(2)}, u32[]{:S(2)}) async-start(bf16[4,48,2048]{2,1,0:T(8,128)(2,1)} %bitcast.171), calls=%async_computation.2 | async-start | bytes 1572864 | tf_op jit(solution)/shard_map/all_to_all | solution.py:522
  523.2 209.9 %reduce-scatter.6.cloned.1.call-start = ((), (), s32[]{:S(2)}) async-start(), calls=%async_computation.8 | async-start | bytes 15003648 | tf_op jit(solution)/shard_map/reduce_scatter | solution.py:584
  532.6 8.5 %copy-start.18 = (bf16[1536,128]{1,0:T(8,128)(2,1)S(1)}, bf16[1536,128]{1,0:T(8,128)(2,1)}, u32[]{:S(2)}) copy-start(bf16[1536,128]{1,0:T(8,128)(2,1)} %pad.23) | copy-start | bytes 1179652
  (14 other events, 26.1 us)
Sparse Core Ops, SparseCore 0:
  12.6 110.1 all-gather.2
  126.5 151.0 all-gather.4
  306.6 181.5 reduce-scatter.3
  491.6 71.4 reduce-scatter.7
  569.0 164.0 reduce-scatter.5

commit v12 on v11

--- a/solution.py
+++ b/solution.py
@@ -507,9 +507,7 @@
 
     grad_out = cotangent[0]
     grad_all = fsdp_gather(grad_out, n_f).reshape(group_tokens, D)
-    down_sum = lax.psum_scatter(
-        outer_rows(hidden_low, grad_all).astype(jnp.bfloat16), "ctx", scatter_dimension=0, tiled=True
-    )
+    down_term = outer_rows(hidden_low, grad_all).astype(jnp.bfloat16)
     hidden_grad = times_transposed(grad_all, down_tp)
     gate_grad = (hidden_grad * up_pre * sigmoid * (1.0 + gate_pre * (1.0 - sigmoid))).astype(
         jnp.bfloat16
@@ -517,9 +515,17 @@
     up_grad = (hidden_grad * gate_pre * sigmoid).astype(jnp.bfloat16)
     gate_up_cat = jnp.concatenate([gate_grad, up_grad], axis=1)
     gate_up_term = outer_rows(xn2_all, gate_up_cat)
-    ff_pack, gate_up_cat = lax.optimization_barrier((gate_up_term.astype(jnp.bfloat16), gate_up_cat))
-    gu_sum = lax.psum_scatter(ff_pack, "ctx", scatter_dimension=0, tiled=True)
-    gu_sum = lax.all_to_all(gu_sum.reshape(n_f, rows, 2 * units), "fsdp", 0, 0, tiled=True)
+    grad_pack = jnp.concatenate(
+        [
+            gate_up_term.astype(jnp.bfloat16).reshape(n_ctx, n_f * rows, 2 * units),
+            down_term.reshape(n_ctx, down_rows, 2 * units),
+        ],
+        axis=1,
+    ).reshape(n_ctx * (n_f * rows + down_rows), 2 * units)
+    grad_pack, gate_up_cat = lax.optimization_barrier((grad_pack, gate_up_cat))
+    grad_sum = lax.psum_scatter(grad_pack, "ctx", scatter_dimension=0, tiled=True)
+    down_sum = grad_sum[n_f * rows :].reshape(ff_rows, D)
+    gu_sum = lax.all_to_all(grad_sum[: n_f * rows].reshape(n_f, rows, 2 * units), "fsdp", 0, 0, tiled=True)
     ff_sum = jnp.transpose(
         gu_sum.reshape(n_f, rows, 2, n_ctx, chunk), (1, 2, 3, 0, 4)
     ).reshape(rows, 2 * ff)

time: 752 us -> 755 us (level)
  Pallas kernels: 247 us -> 234 us
  local copies, waits for them, and re-layouts: 66.8 us -> 75.4 us
    reduce_scatter x2 -> x1, waiting for transfers between devices: 0.01 us -> 17.9 us  [body(): lax.psum_scatter(grad_pack, 'ctx', scatter_dimension=0, tiled=True)]
    reduce_scatter x1, waiting for transfers between devices: 134 us -> 120 us  [body(): lax.psum_scatter(attention_pack, ALL, scatter_dimension=0, tiled=True)]
    pallas_call x1, Pallas kernels: 117 us -> 103 us  [kv_return(): pl.pallas_call(functools.partial(kv_return_kernel, n_ctx, back), out_shap...]
    concatenate x0 -> x1, other arithmetic: none -> 7.85 us  [body(): jnp.concatenate([gate_up_term.astype(jnp.bfloat16).reshape(n_ctx, n_f * r...]
  transfers between devices with their start and end apart: 7 -> 6, of which waited for: 5 -> 6; matrix products, arithmetic and copies ran while one was open for 19% -> 16% of each run, Pallas kernels for 33% -> 31%
where the time goes in v12:
time: 755 us; the launch traced here: 748 us
  waiting for transfers between devices  285 us (38%)
  Pallas kernels  234 us (31%)
  matrix products  76.9 us (10%)
  local copies, waits for them, and re-layouts  75.4 us (10%)
  other arithmetic  50.3 us (7%)
  between operations  19.6 us (3%)
  starting transfers between devices  7.82 us (1%)
    reduce_scatter x1, waiting for transfers between devices, body(): lax.psum_scatter(attention_pack, ALL, scatter_dimension=0, tiled=True)  120 us
    pallas_call x1, Pallas kernels, kv_return(): pl.pallas_call(functools.partial(kv_return_kernel, n_ctx, back), out_shap...  103 us
    all_gather x1, waiting for transfers between devices, body(): lax.all_gather(jnp.concatenate([query_weight, key_weight, value_weight, o...  85.9 us
    pallas_call x2, Pallas kernels, quad_reduce(): pl.pallas_call(quad_reduce_kernel, out_shape=jax.ShapeDtypeStruct(block,...  52.3 us
    pallas_call x1, Pallas kernels, kv_share(): pl.pallas_call(functools.partial(kv_share_kernel, n_ctx, back), out_shape...  48.9 us
    all_gather x1, waiting for transfers between devices, body(): ff_stack = lax.all_gather(ff_pack, 'ctx', axis=0, tiled=False)  44.3 us
    pallas_call x2, Pallas kernels, quad_gather(): pl.pallas_call(quad_gather_kernel, out_shape=jax.ShapeDtypeStruct((4,) +...  29.7 us
    dot_general x4, matrix products, times_transposed(): lax.dot_general(left, right, (((1,), (1,)), ((), ())), preferred_element_...  24.5 us
  transfers between devices with their start and end apart: 6, of which 6 were waited for; matrix products, arithmetic and copies ran while one was open for 16% of the time, Pallas kernels for 31%

profile of v12, /device:TPU:0, one launch (start us, length us, event | category | flops | bytes accessed | tf_op | source)
XLA Modules:
  0.0 748.4 jit_solution(18307803173202272736)
XLA Ops:
  16.6 4.2 all-to-all-start
  21.2 14.6 %all-to-all-done = bf16[4,48,2,8,128]{4,3,1,2,0:T(8,128)(2,1)S(1)} async-done(((bf16[4,48,2,8,128]{4,3,1,2,0:T(8,128)(2,1)}), bf16[4,48,2,8,128]{4,3,1,2,0:T(8,128)(2,1)S(1)}, u32[]{:S(2)}, u32[]{:S(2)}) %all-to-all-start) | async-done | bytes 786464 | tf_op jit(solution)/shard_map/all_to_all | solution.py:452
  36.9 85.9 %all-gather.3.cloned.1.call-done = bf16[1536,4736]{1,0:T(8,128)(2,1)} async-done(((bf16[48,4736]{1,0:T(8,128)(2,1)}), bf16[1536,4736]{1,0:T(8,128)(2,1)}) %all-gather.3.cloned.1.call-update) | async-done | bytes 14549008 | tf_op jit(solution)/shard_map/all_gather | solution.py:408
  126.6 14.8 %shard_map.205 = bf16[4,128,1536]{2,1,0:T(8,128)(2,1)} custom-call(bf16[128,1536]{1,0:T(8,128)(2,1)} %bitcast.175), custom_call_target="tpu_custom_call" | custom-call | tf_op jit(solution)/shard_map/pallas_call | solution.py:311
  145.2 5.2 fusion.3
  151.7 48.9 %shard_map.203 = bf16[5,128,1536]{2,1,0:T(8,128)(2,1)} custom-call(bf16[128,1536]{1,0:T(8,128)(2,1)} %pad_maximum_fusion.5.kv_ref), custom_call_target="tpu_custom_call" | custom-call | tf_op jit(solution)/shard_map/pallas_call | solution.py:116
  204.9 4.4 fusion.57
  218.3 14.9 %shard_map.204 = bf16[4,128,1536]{2,1,0:T(8,128)(2,1)} custom-call(bf16[128,1536]{1,0:T(8,128)(2,1)} %multiply_convert_fusion.1.x_ref), custom_call_target="tpu_custom_call" | custom-call | tf_op jit(solution)/shard_map/pallas_call | solution.py:311
  233.2 44.3 %all-gather.5.cloned.1.call-done = bf16[8,288,2048]{2,1,0:T(8,128)(2,1)} async-done(((bf16[1,288,2048]{2,1,0:T(8,128)(2,1)}), bf16[8,288,2048]{2,1,0:T(8,128)(2,1)}) %all-gather.5.cloned.1.call-update) | async-done | bytes 9437200 | tf_op jit(solution)/shard_map/all_gather | solution.py:456
  281.5 6.0 reshape_reshape.3
  298.3 5.8 convolution_convert_fusion.1
  309.0 6.0 reshape.406
  315.1 7.8 %pad_maximum_fusion.1 = bf16[8,288,2048]{2,1,0:T(8,128)(2,1)} fusion(bf16[8,96,2048]{2,1,0:T(8,128)(2,1)} %reshape.406, bf16[8,192,2048]{2,1,0:T(8,128)(2,1)} %bitcast.148), kind=kLoop, calls=%fused_computation.3 | loop fusion | flops 18874368 | bytes 18874368 | tf_op jit(solution)/shard_map/concatenate | solution.py:518
  324.2 8.5 %fusion.61.p_ref = f32[4,128,1536]{2,1,0:T(8,128)} fusion(bf16[4,128,2048]{2,1,0:T(8,128)(2,1)} %bitcast.164, bf16[1536,2048,1]{1,0,2:T(8,128)(2,1)} %bitcast.146), kind=kOutput, calls=%fused_computation.135 | convolution fusion | flops 3221225472 | bytes 11534336 | tf_op jit(solution)/shard_map/dot_general | solution.py:63
  332.7 26.2 %shard_map.206 = f32[128,1536]{1,0:T(8,128)} custom-call(f32[4,128,1536]{2,1,0:T(8,128)} %fusion.61.p_ref), custom_call_target="tpu_custom_call" | custom-call | tf_op jit(solution)/shard_map/pallas_call | solution.py:354
  362.7 5.4 fusion.19
  371.4 4.1 fusion.6
  391.9 102.8 %shard_map.207 = f32[128,1536]{1,0:T(8,128)} custom-call(f32[128,1536]{1,0:T(8,128)} %fusion.40.own_ref, bf16[4,128,1536]{2,1,0:T(8,128)(2,1)} %bitcast.147), custom_call_target="tpu_custom_call" | custom-call | tf_op jit(solution)/shard_map/pallas_call | solution.py:163
  505.1 8.0 %fusion.38 = (bf16[1536]{0:T(1024)(128)(2,1)S(1)}, f32[128]{0:T(128)S(1)}, f32[128,1536]{1,0:T(8,128)}) fusion(bf16[1,128,1536]{2,1,0:T(8,128)(2,1)S(1)} %copy-done.10, f32[128]{0:T(128)S(1)} %copy-done.37, f32[1536]{0:T(1024)S(1)} %get-tuple-element.52, bf16[1536,4736]{1,0:T(8,128)(2,1)} %all-gather.3.cloned.1.call-done, ...), kind=kOutput, calls=%fused_computation.57 | convolution fusion | flops 1211693440 | bytes 11413504 | tf_op jit(solution)/shard_map/dot_general | solution.py:63
  516.7 17.9 %reduce-scatter.3.cloned.1.call-done = bf16[288,2048]{1,0:T(8,128)(2,1)} async-done(((bf16[2304,2048]{1,0:T(8,128)(2,1)}), bf16[288,2048]{1,0:T(8,128)(2,1)}) %reduce-scatter.3.cloned.1.call-update) | async-done | bytes 1179664 | tf_op jit(solution)/shard_map/reduce_scatter | solution.py:526
  543.3 6.3 convolution_convert_fusion
  559.5 13.0 %pad_maximum_fusion = bf16[1536,4736]{1,0:T(8,128)(2,1)} fusion(bf16[1536,128]{1,0:T(8,128)(2,1)S(1)} %scatter.4, bf16[1536,1536]{1,0:T(8,128)(2,1)} %convolution_convert_fusion.2, bf16[1536,3072]{1,0:T(8,128)(2,1)} %convolution_convert_fusion), kind=kLoop, calls=%fused_computation.1 | loop fusion | flops 43646976 | bytes 29097984 | tf_op jit(solution)/shard_map/concatenate | solution.py:582
  582.4 26.1 %shard_map.208 = f32[128,1536]{1,0:T(8,128)} custom-call(f32[4,128,1536]{2,1,0:T(8,128)} %bitcast.160), custom_call_target="tpu_custom_call" | custom-call | tf_op jit(solution)/shard_map/pallas_call | solution.py:354
  616.3 119.8 %reduce-scatter.5.cloned.1.call-done = bf16[48,4736]{1,0:T(8,128)(2,1)} async-done(((bf16[1536,4736]{1,0:T(8,128)(2,1)}), bf16[48,4736]{1,0:T(8,128)(2,1)}) %reduce-scatter.5.cloned.1.call-update) | async-done | bytes 454672 | tf_op jit(solution)/shard_map/reduce_scatter | solution.py:590
  (201 shorter events, 127.9 us)
Async XLA Ops:
  7.2 115.6 %all-gather.3.cloned.1.call-start = ((), (), s32[]{:S(2)}) async-start(), calls=%async_computation.4 | async-start | bytes 15003648 | tf_op jit(solution)/shard_map/all_gather | solution.py:408
  12.5 8.4 %copy-start.31 = (bf16[128,1536]{1,0:T(8,128)(2,1)S(1)}, bf16[128,1536]{1,0:T(8,128)(2,1)}, u32[]{:S(2)}) copy-start(bf16[128,1536]{1,0:T(8,128)(2,1)} %param.28) | copy-start | bytes 1179652
  16.6 19.1 %all-to-all-start = ((bf16[4,48,2,8,128]{4,3,1,2,0:T(8,128)(2,1)}), bf16[4,48,2,8,128]{4,3,1,2,0:T(8,128)(2,1)S(1)}, u32[]{:S(2)}, u32[]{:S(2)}) async-start(bf16[4,48,2,8,128]{4,3,1,2,0:T(8,128)(2,1)} %copy.107), calls=%async_computation | async-start | bytes 1572864 | tf_op jit(solution)/shard_map/all_to_all | solution.py:452
  20.8 256.7 %all-gather.5.cloned.1.call-start = ((), (), s32[]{:S(2)}) async-start(), calls=%async_computation.5 | async-start | bytes 10616832 | tf_op jit(solution)/shard_map/all_gather | solution.py:456
  21.2 105.3 %copy-start.38 = (s32[1,8]{1,0:T(1,128)S(1)}, s32[1,8]{1,0:T(1,128)}, u32[]{:S(2)}) copy-start(s32[1,8]{1,0:T(1,128)} %param.19) | copy-start | bytes 100
  36.2 105.6 %copy-start.8 = (bf16[1,128,1536]{2,1,0:T(8,128)(2,1)S(1)}, bf16[1,128,1536]{2,1,0:T(8,128)(2,1)}, u32[]{:S(2)}) copy-start(bf16[1,128,1536]{2,1,0:T(8,128)(2,1)} %param.18) | copy-start | bytes 1179652
  126.4 408.2 %reduce-scatter.3.cloned.1.call-start = ((), (), s32[]{:S(2)}) async-start(), calls=%async_computation.6 | async-start | bytes 10616832 | tf_op jit(solution)/shard_map/reduce_scatter | solution.py:526
  142.0 8.4 %copy-start.36 = (f32[128]{0:T(128)}, f32[128]{0:T(128)S(1)}, u32[]{:S(2)}) copy-start(f32[128]{0:T(128)S(1)} %add_rsqrt_fusion.1) | copy-start | bytes 1540
  142.8 7.9 %copy-start.29 = (f32[128,48]{0,1:T(8,128)}, f32[128,48]{0,1:T(8,128)S(1)}, u32[]{:S(2)}) copy-start(f32[128,48]{0,1:T(8,128)S(1)} %get-tuple-element.82) | copy-start | bytes 73732
  142.8 7.9 %copy-start.33 = (f32[128,48]{0,1:T(8,128)}, f32[128,48]{0,1:T(8,128)S(1)}, u32[]{:S(2)}) copy-start(f32[128,48]{0,1:T(8,128)S(1)} %get-tuple-element.81) | copy-start | bytes 73732
  150.4 50.3 %copy-start.15 = (f32[128,3072]{1,0:T(8,128)}, f32[128,3072]{1,0:T(8,128)S(1)}, u32[]{:S(2)}) copy-start(f32[128,3072]{1,0:T(8,128)S(1)} %fusion.3) | copy-start | bytes 4718596
  204.4 4.9 copy-start.13
  298.3 7.3 copy-start.40
  371.4 5.6 copy-start.22
  391.9 109.9 %copy-start.32 = (f32[128,48]{0,1:T(8,128)S(1)}, f32[128,48]{0,1:T(8,128)}, u32[]{:S(2)}) copy-start(f32[128,48]{0,1:T(8,128)} %get-tuple-element.80) | copy-start | bytes 73732
  391.9 111.0 %copy-start.3 = (bf16[128,8,2,640]{0,3,2,1:T(8,128)(2,1)S(1)}, bf16[128,8,2,640]{0,3,2,1:T(8,128)(2,1)}, u32[]{:S(2)}) copy-start(bf16[128,8,2,640]{0,3,2,1:T(8,128)(2,1)} %copy-done.2) | copy-start | bytes 7864324
  505.0 8.1 %copy-start.20 = (bf16[128,16,96]{0,2,1:T(8,128)(2,1)}, bf16[128,16,96]{0,2,1:T(8,128)(2,1)S(1)}, u32[]{:S(2)}) copy-start(bf16[128,16,96]{0,2,1:T(8,128)(2,1)S(1)} %pad_maximum_fusion.7) | copy-start | bytes 1179652
  505.1 8.1 %copy-start.5 = (f32[128,1536]{1,0:T(8,128)S(1)}, f32[128,1536]{1,0:T(8,128)}, u32[]{:S(2)}) copy-start(f32[128,1536]{1,0:T(8,128)} %copy-done.4) | copy-start | bytes 2359300
  505.1 8.0 %copy-start.18 = (bf16[128,8,2,96]{0,3,2,1:T(8,128)(2,1)S(1)}, bf16[128,8,2,96]{0,3,2,1:T(8,128)(2,1)}, u32[]{:S(2)}) copy-start(bf16[128,8,2,96]{0,3,2,1:T(8,128)(2,1)} %copy-done.17) | copy-start | bytes 1179652
  516.7 26.6 %copy-start.11 = (bf16[1,128,1536]{2,1,0:T(8,128)(2,1)S(1)}, bf16[1,128,1536]{2,1,0:T(8,128)(2,1)}, u32[]{:S(2)}) copy-start(bf16[1,128,1536]{2,1,0:T(8,128)(2,1)} %param.18) | copy-start | bytes 1179652
  516.7 26.6 %copy-start.27 = (bf16[128,768]{0,1:T(8,128)(2,1)S(1)}, bf16[128,768]{0,1:T(8,128)(2,1)}, u32[]{:S(2)}) copy-start(bf16[128,768]{0,1:T(8,128)(2,1)} %copy.117) | copy-start | bytes 589828
  536.7 15.1 %all-to-all-start.1 = ((bf16[4,48,2048]{2,1,0:T(8,128)(2,1)}), bf16[4,48,2048]{2,1,0:T(8,128)(2,1)S(1)}, u32[]{:S(2)}, u32[]{:S(2)}) async-start(bf16[4,48,2048]{2,1,0:T(8,128)(2,1)} %bitcast.157), calls=%async_computation.2 | async-start | bytes 1572864 | tf_op jit(solution)/shard_map/all_to_all | solution.py:528
  540.2 196.0 %reduce-scatter.5.cloned.1.call-start = ((), (), s32[]{:S(2)}) async-start(), calls=%async_computation.7 | async-start | bytes 15003648 | tf_op jit(solution)/shard_map/reduce_scatter | solution.py:590
  549.6 8.5 %copy-start.19 = (bf16[1536,128]{1,0:T(8,128)(2,1)S(1)}, bf16[1536,128]{1,0:T(8,128)(2,1)}, u32[]{:S(2)}) copy-start(bf16[1536,128]{1,0:T(8,128)(2,1)} %pad.23) | copy-start | bytes 1179652
  (24 other events, 57.9 us)
Sparse Core Ops, SparseCore 0:
  12.6 110.1 all-gather.2
  126.5 150.9 all-gather.4
  323.1 211.4 reduce-scatter.2
  572.6 163.5 reduce-scatter.4

commit v13 on v11

--- a/solution.py
+++ b/solution.py
@@ -507,9 +507,10 @@
 
     grad_out = cotangent[0]
     grad_all = fsdp_gather(grad_out, n_f).reshape(group_tokens, D)
-    down_sum = lax.psum_scatter(
-        outer_rows(hidden_low, grad_all).astype(jnp.bfloat16), "ctx", scatter_dimension=0, tiled=True
-    )
+    down_term, grad_all = lax.optimization_barrier(
+        (outer_rows(hidden_low, grad_all).astype(jnp.bfloat16), grad_all)
+    )
+    down_sum = lax.psum_scatter(down_term, "ctx", scatter_dimension=0, tiled=True)
     hidden_grad = times_transposed(grad_all, down_tp)
     gate_grad = (hidden_grad * up_pre * sigmoid * (1.0 + gate_pre * (1.0 - sigmoid))).astype(
         jnp.bfloat16
@@ -554,7 +555,8 @@
         "qgrk,qgrd->kgd", probs_low, attended_grad_low, preferred_element_type=jnp.float32
     ).reshape(win, KVW)
     kv_term = jnp.concatenate([key_term, value_term], axis=1).reshape(back + 1, tok_rows, 2 * KVW)
-    kv_sum = kv_return(kv_term[back], kv_term[:back].astype(jnp.bfloat16), n_ctx, back)
+    kv_own = kv_term[back].at[0, 0].add(down_sum[0, 0].astype(jnp.float32) * 0.0)
+    kv_sum = kv_return(kv_own, kv_term[:back].astype(jnp.bfloat16), n_ctx, back)
     key_grad_low = rotate(kv_sum[:, :KVW] * score_scale, query_positions, KVH, -1.0).astype(
         jnp.bfloat16
     )

time: 752 us -> 777 us (1.033)
  waiting for transfers between devices: 281 us -> 311 us
    reduce_scatter x1, waiting for transfers between devices: 0.01 us -> 33.4 us  [body(): gu_sum = lax.psum_scatter(ff_pack, 'ctx', scatter_dimension=0, tiled=True)]
    reduce_scatter x1, waiting for transfers between devices: 134 us -> 122 us  [body(): lax.psum_scatter(attention_pack, ALL, scatter_dimension=0, tiled=True)]
    reduce_scatter x1, waiting for transfers between devices: 0.01 us -> 9.65 us  [body(): lax.psum_scatter(down_term, 'ctx', scatter_dimension=0, tiled=True)]
  transfers between devices with their start and end apart: 7 -> 7, of which waited for: 5 -> 7; matrix products, arithmetic and copies ran while one was open for 19% -> 18% of each run, Pallas kernels for 33% -> 31%
where the time goes in v13:
time: 777 us; the launch traced here: 770 us
  waiting for transfers between devices  311 us (40%)
  Pallas kernels  242 us (31%)
  matrix products  80.8 us (10%)
  local copies, waits for them, and re-layouts  67.5 us (9%)
  other arithmetic  40.1 us (5%)
  between operations  20.8 us (3%)
  starting transfers between devices  7.86 us (1%)
    reduce_scatter x1, waiting for transfers between devices, body(): lax.psum_scatter(attention_pack, ALL, scatter_dimension=0, tiled=True)  122 us
    pallas_call x1, Pallas kernels, kv_return(): pl.pallas_call(functools.partial(kv_return_kernel, n_ctx, back), out_shap...  111 us
    all_gather x1, waiting for transfers between devices, body(): lax.all_gather(jnp.concatenate([query_weight, key_weight, value_weight, o...  85.9 us
    pallas_call x2, Pallas kernels, quad_reduce(): pl.pallas_call(quad_reduce_kernel, out_shape=jax.ShapeDtypeStruct(block,...  52.3 us
    pallas_call x1, Pallas kernels, kv_share(): pl.pallas_call(functools.partial(kv_share_kernel, n_ctx, back), out_shape...  48.9 us
    all_gather x1, waiting for transfers between devices, body(): ff_stack = lax.all_gather(ff_pack, 'ctx', axis=0, tiled=False)  43.6 us
    reduce_scatter x1, waiting for transfers between devices, body(): gu_sum = lax.psum_scatter(ff_pack, 'ctx', scatter_dimension=0, tiled=True)  33.4 us
    pallas_call x2, Pallas kernels, quad_gather(): pl.pallas_call(quad_gather_kernel, out_shape=jax.ShapeDtypeStruct((4,) +...  29.7 us
  transfers between devices with their start and end apart: 7, of which 7 were waited for; matrix products, arithmetic and copies ran while one was open for 18% of the time, Pallas kernels for 31%

profile of v13, /device:TPU:0, one launch (start us, length us, event | category | flops | bytes accessed | tf_op | source)
XLA Modules:
  0.0 770.1 jit_solution(16516631312675381009)
XLA Ops:
  16.6 4.2 all-to-all-start
  21.2 14.6 %all-to-all-done = bf16[4,48,2,8,128]{4,3,1,2,0:T(8,128)(2,1)S(1)} async-done(((bf16[4,48,2,8,128]{4,3,1,2,0:T(8,128)(2,1)}), bf16[4,48,2,8,128]{4,3,1,2,0:T(8,128)(2,1)S(1)}, u32[]{:S(2)}, u32[]{:S(2)}) %all-to-all-start) | async-done | bytes 786464 | tf_op jit(solution)/shard_map/all_to_all | solution.py:452
  36.9 85.9 %all-gather.3.cloned.1.call-done = bf16[1536,4736]{1,0:T(8,128)(2,1)} async-done(((bf16[48,4736]{1,0:T(8,128)(2,1)}), bf16[1536,4736]{1,0:T(8,128)(2,1)}) %all-gather.3.cloned.1.call-update) | async-done | bytes 14549008 | tf_op jit(solution)/shard_map/all_gather | solution.py:408
  126.6 14.9 %shard_map.205 = bf16[4,128,1536]{2,1,0:T(8,128)(2,1)} custom-call(bf16[128,1536]{1,0:T(8,128)(2,1)} %bitcast.157), custom_call_target="tpu_custom_call" | custom-call | tf_op jit(solution)/shard_map/pallas_call | solution.py:311
  144.1 5.2 fusion.3
  151.8 48.9 %shard_map.203 = bf16[5,128,1536]{2,1,0:T(8,128)(2,1)} custom-call(bf16[128,1536]{1,0:T(8,128)(2,1)} %pad_maximum_fusion.4.kv_ref), custom_call_target="tpu_custom_call" | custom-call | tf_op jit(solution)/shard_map/pallas_call | solution.py:116
  205.6 4.4 fusion.52
  219.0 14.9 %shard_map.204 = bf16[4,128,1536]{2,1,0:T(8,128)(2,1)} custom-call(bf16[128,1536]{1,0:T(8,128)(2,1)} %multiply_convert_fusion.3.x_ref), custom_call_target="tpu_custom_call" | custom-call | tf_op jit(solution)/shard_map/pallas_call | solution.py:311
  233.9 43.6 %all-gather.5.cloned.1.call-done = bf16[8,288,2048]{2,1,0:T(8,128)(2,1)} async-done(((bf16[1,288,2048]{2,1,0:T(8,128)(2,1)}), bf16[8,288,2048]{2,1,0:T(8,128)(2,1)}) %all-gather.5.cloned.1.call-update) | async-done | bytes 9437200 | tf_op jit(solution)/shard_map/all_gather | solution.py:456
  294.8 6.2 reshape_reshape.3
  301.0 6.0 multiply_convert_fusion.1
  309.0 5.5 convolution_convert_fusion.1
  315.8 8.5 %fusion.56.p_ref = f32[4,128,1536]{2,1,0:T(8,128)} fusion(bf16[4,128,2048]{2,1,0:T(8,128)(2,1)} %bitcast.146, bf16[1536,2048,1]{1,0,2:T(8,128)(2,1)} %bitcast.130), kind=kOutput, calls=%fused_computation.128 | convolution fusion | flops 3221225472 | bytes 11534336 | tf_op jit(solution)/shard_map/dot_general | solution.py:63
  324.4 26.2 %shard_map.206 = f32[128,1536]{1,0:T(8,128)} custom-call(f32[4,128,1536]{2,1,0:T(8,128)} %fusion.56.p_ref), custom_call_target="tpu_custom_call" | custom-call | tf_op jit(solution)/shard_map/pallas_call | solution.py:354
  354.4 4.8 fusion.19
  362.4 4.0 fusion.6
  389.5 9.6 %reduce-scatter.4.cloned.1.call-done = bf16[128,1536]{1,0:T(8,128)(2,1)} async-done(((bf16[1024,1536]{1,0:T(8,128)(2,1)}), bf16[128,1536]{1,0:T(8,128)(2,1)}) %reduce-scatter.4.cloned.1.call-update) | async-done | bytes 393232 | tf_op jit(solution)/shard_map/reduce_scatter | solution.py:513
  403.0 111.2 %shard_map.207 = f32[128,1536]{1,0:T(8,128)} custom-call(f32[128,1536]{1,0:T(8,128)} %scatter-add.11.own_ref, bf16[4,128,1536]{2,1,0:T(8,128)(2,1)} %bitcast.131), custom_call_target="tpu_custom_call" | custom-call | tf_op jit(solution)/shard_map/pallas_call | solution.py:163
  516.6 7.8 %fusion.33 = (bf16[1536]{0:T(1024)(128)(2,1)S(1)}, f32[128]{0:T(128)S(1)}, f32[128,1536]{1,0:T(8,128)}) fusion(bf16[1,128,1536]{2,1,0:T(8,128)(2,1)S(1)} %copy-done.9, f32[128]{0:T(128)S(1)} %add_rsqrt_fusion.1, f32[1536]{0:T(1024)S(1)} %get-tuple-element.68, bf16[1536,4736]{1,0:T(8,128)(2,1)} %all-gather.3.cloned.1.call-done, ...), kind=kOutput, calls=%fused_computation.51 | convolution fusion | flops 1211693440 | bytes 11413504 | tf_op jit(solution)/shard_map/dot_general | solution.py:63
  524.5 33.4 %reduce-scatter.6.cloned.1.call-done = bf16[192,2048]{1,0:T(8,128)(2,1)} async-done(((bf16[1536,2048]{1,0:T(8,128)(2,1)}), bf16[192,2048]{1,0:T(8,128)(2,1)}) %reduce-scatter.6.cloned.1.call-update) | async-done | bytes 786448 | tf_op jit(solution)/shard_map/reduce_scatter | solution.py:522
  564.4 7.0 convolution_convert_fusion
  580.6 13.3 %pad_maximum_fusion = bf16[1536,4736]{1,0:T(8,128)(2,1)} fusion(bf16[1536,128]{1,0:T(8,128)(2,1)S(1)} %scatter.4, bf16[1536,1536]{1,0:T(8,128)(2,1)} %convolution_convert_fusion.2, bf16[1536,3072]{1,0:T(8,128)(2,1)} %convolution_convert_fusion), kind=kLoop, calls=%fused_computation.1 | loop fusion | flops 43646976 | bytes 29097984 | tf_op jit(solution)/shard_map/concatenate | solution.py:578
  603.9 26.1 %shard_map.208 = f32[128,1536]{1,0:T(8,128)} custom-call(f32[4,128,1536]{2,1,0:T(8,128)} %bitcast.142), custom_call_target="tpu_custom_call" | custom-call | tf_op jit(solution)/shard_map/pallas_call | solution.py:354
  635.5 122.3 %reduce-scatter.8.cloned.1.call-done = bf16[48,4736]{1,0:T(8,128)(2,1)} async-done(((bf16[1536,4736]{1,0:T(8,128)(2,1)}), bf16[48,4736]{1,0:T(8,128)(2,1)}) %reduce-scatter.8.cloned.1.call-update) | async-done | bytes 454672 | tf_op jit(solution)/shard_map/reduce_scatter | solution.py:586
  (181 shorter events, 120.9 us)
Async XLA Ops:
  7.2 115.6 %all-gather.3.cloned.1.call-start = ((), (), s32[]{:S(2)}) async-start(), calls=%async_computation.5 | async-start | bytes 15003648 | tf_op jit(solution)/shard_map/all_gather | solution.py:408
  13.7 7.1 copy-start.26
  16.6 19.1 %all-to-all-start = ((bf16[4,48,2,8,128]{4,3,1,2,0:T(8,128)(2,1)}), bf16[4,48,2,8,128]{4,3,1,2,0:T(8,128)(2,1)S(1)}, u32[]{:S(2)}, u32[]{:S(2)}) async-start(bf16[4,48,2,8,128]{4,3,1,2,0:T(8,128)(2,1)} %copy.106), calls=%async_computation | async-start | bytes 1572864 | tf_op jit(solution)/shard_map/all_to_all | solution.py:452
  20.8 256.6 %all-gather.5.cloned.1.call-start = ((), (), s32[]{:S(2)}) async-start(), calls=%async_computation.6 | async-start | bytes 10616832 | tf_op jit(solution)/shard_map/all_gather | solution.py:456
  35.9 90.5 %copy-start.28 = (s32[1,8]{1,0:T(1,128)S(1)}, s32[1,8]{1,0:T(1,128)}, u32[]{:S(2)}) copy-start(s32[1,8]{1,0:T(1,128)} %param.21) | copy-start | bytes 100
  36.7 105.1 %copy-start.7 = (bf16[1,128,1536]{2,1,0:T(8,128)(2,1)S(1)}, bf16[1,128,1536]{2,1,0:T(8,128)(2,1)}, u32[]{:S(2)}) copy-start(bf16[1,128,1536]{2,1,0:T(8,128)(2,1)} %param.20) | copy-start | bytes 1179652
  126.3 272.8 %reduce-scatter.4.cloned.1.call-start = ((), (), s32[]{:S(2)}) async-start(), calls=%async_computation.7 | async-start | bytes 3538944 | tf_op jit(solution)/shard_map/reduce_scatter | solution.py:513
  203.0 7.0 copy-start.12
  205.6 4.4 copy-start.18
  210.0 3.2 copy-start.11
  214.7 3.4 copy-start.14
  277.5 3.5 copy-start.21
  280.9 3.4 copy-start.5
  290.8 267.0 %reduce-scatter.6.cloned.1.call-start = ((), (), s32[]{:S(2)}) async-start(), calls=%async_computation.8 | async-start | bytes 7077888 | tf_op jit(solution)/shard_map/reduce_scatter | solution.py:522
  362.4 5.6 copy-start.19
  379.7 3.7 copy-start
  403.0 113.6 %copy-start.9 = (bf16[1,128,1536]{2,1,0:T(8,128)(2,1)S(1)}, bf16[1,128,1536]{2,1,0:T(8,128)(2,1)}, u32[]{:S(2)}) copy-start(bf16[1,128,1536]{2,1,0:T(8,128)(2,1)} %param.20) | copy-start | bytes 1179652
  403.0 113.7 %copy-start.17 = (bf16[128,16,96]{0,2,1:T(8,128)(2,1)S(1)}, bf16[128,16,96]{0,2,1:T(8,128)(2,1)}, u32[]{:S(2)}) copy-start(bf16[128,16,96]{0,2,1:T(8,128)(2,1)} %pad_maximum_fusion.6) | copy-start | bytes 1179652
  557.8 15.1 %all-to-all-start.1 = ((bf16[4,48,2048]{2,1,0:T(8,128)(2,1)}), bf16[4,48,2048]{2,1,0:T(8,128)(2,1)S(1)}, u32[]{:S(2)}, u32[]{:S(2)}) async-start(bf16[4,48,2048]{2,1,0:T(8,128)(2,1)} %bitcast.158), calls=%async_computation.3 | async-start | bytes 1572864 | tf_op jit(solution)/shard_map/all_to_all | solution.py:523
  561.3 196.5 %reduce-scatter.8.cloned.1.call-start = ((), (), s32[]{:S(2)}) async-start(), calls=%async_computation.9 | async-start | bytes 15003648 | tf_op jit(solution)/shard_map/reduce_scatter | solution.py:586
  571.4 7.8 %copy-start.16 = (bf16[1536,128]{1,0:T(8,128)(2,1)S(1)}, bf16[1536,128]{1,0:T(8,128)(2,1)}, u32[]{:S(2)}) copy-start(bf16[1536,128]{1,0:T(8,128)(2,1)} %pad.27) | copy-start | bytes 1179652
  599.6 30.4 %copy-start.27 = (bf16[128,1536]{1,0:T(8,128)(2,1)S(1)}, bf16[128,1536]{1,0:T(8,128)(2,1)}, u32[]{:S(2)}) copy-start(bf16[128,1536]{1,0:T(8,128)(2,1)} %reduce-scatter.4.cloned.1.call-done) | copy-start | bytes 1179652
  603.9 29.2 %copy-start.4 = (f32[128,1536]{1,0:T(8,128)S(1)}, f32[128,1536]{1,0:T(8,128)}, u32[]{:S(2)}) copy-start(f32[128,1536]{1,0:T(8,128)} %copy-done.2) | copy-start | bytes 2359300
  630.0 3.0 copy-start.25
  (13 other events, 19.1 us)
Sparse Core Ops, SparseCore 0:
  12.6 110.1 all-gather.2
  126.5 150.9 all-gather.4
  290.9 108.1 reduce-scatter.3
  402.6 155.1 reduce-scatter.5
  594.0 163.7 reduce-scatter.7

commit v14 on v13

--- a/solution.py
+++ b/solution.py
@@ -574,7 +574,6 @@
     gain_term_cols = jnp.pad(
         jnp.stack([gain_one_term, gain_two_term], axis=1), ((0, 0), (0, GAIN_PAD - 2))
     )
-    gain_term_cols = gain_term_cols.at[0, GAIN_PAD - 1].set(ff_sum[0, 0].astype(jnp.float32) * 0.0)
     attention_pack = jnp.concatenate(
         [
             outer_rows(normed_low, projection_cat).astype(jnp.bfloat16),

time: 777 us -> 747 us (0.961)
  waiting for transfers between devices: 311 us -> 292 us
    reduce_scatter x1, waiting for transfers between devices: 33.4 us -> 0.01 us  [body(): gu_sum = lax.psum_scatter(ff_pack, 'ctx', scatter_dimension=0, tiled=True)]
  transfers between devices with their start and end apart: 7 -> 7, of which waited for: 7 -> 6; matrix products, arithmetic and copies ran while one was open for 18% -> 20% of each run, Pallas kernels for 31% -> 33%
where the time goes in v14:
time: 747 us; the launch traced here: 740 us
  waiting for transfers between devices  292 us (39%)
  Pallas kernels  242 us (32%)
  matrix products  81.5 us (11%)
  local copies, waits for them, and re-layouts  63.2 us (8%)
  other arithmetic  34.8 us (5%)
  between operations  18.8 us (3%)
  starting transfers between devices  8.26 us (1%)
    reduce_scatter x1, waiting for transfers between devices, body(): lax.psum_scatter(attention_pack, ALL, scatter_dimension=0, tiled=True)  129 us
    pallas_call x1, Pallas kernels, kv_return(): pl.pallas_call(functools.partial(kv_return_kernel, n_ctx, back), out_shap...  111 us
    all_gather x1, waiting for transfers between devices, body(): lax.all_gather(jnp.concatenate([query_weight, key_weight, value_weight, o...  85.9 us
    pallas_call x2, Pallas kernels, quad_reduce(): pl.pallas_call(quad_reduce_kernel, out_shape=jax.ShapeDtypeStruct(block,...  52.3 us
    pallas_call x1, Pallas kernels, kv_share(): pl.pallas_call(functools.partial(kv_share_kernel, n_ctx, back), out_shape...  48.9 us
    all_gather x1, waiting for transfers between devices, body(): ff_stack = lax.all_gather(ff_pack, 'ctx', axis=0, tiled=False)  43.5 us
    pallas_call x2, Pallas kernels, quad_gather(): pl.pallas_call(quad_gather_kernel, out_shape=jax.ShapeDtypeStruct((4,) +...  29.7 us
    dot_general x4, matrix products, times_transposed(): lax.dot_general(left, right, (((1,), (1,)), ((), ())), preferred_element_...  27.1 us
  transfers between devices with their start and end apart: 7, of which 6 were waited for; matrix products, arithmetic and copies ran while one was open for 20% of the time, Pallas kernels for 33%

profile of v14, /device:TPU:0, one launch (start us, length us, event | category | flops | bytes accessed | tf_op | source)
XLA Modules:
  0.0 740.4 jit_solution(14479526496131869291)
XLA Ops:
  16.6 4.2 all-to-all-start
  21.2 14.6 %all-to-all-done = bf16[4,48,2,8,128]{4,3,1,2,0:T(8,128)(2,1)S(1)} async-done(((bf16[4,48,2,8,128]{4,3,1,2,0:T(8,128)(2,1)}), bf16[4,48,2,8,128]{4,3,1,2,0:T(8,128)(2,1)S(1)}, u32[]{:S(2)}, u32[]{:S(2)}) %all-to-all-start) | async-done | bytes 786464 | tf_op jit(solution)/shard_map/all_to_all | solution.py:452
  36.9 85.9 %all-gather.3.cloned.1.call-done = bf16[1536,4736]{1,0:T(8,128)(2,1)} async-done(((bf16[48,4736]{1,0:T(8,128)(2,1)}), bf16[1536,4736]{1,0:T(8,128)(2,1)}) %all-gather.3.cloned.1.call-update) | async-done | bytes 14549008 | tf_op jit(solution)/shard_map/all_gather | solution.py:408
  126.6 14.9 %shard_map.205 = bf16[4,128,1536]{2,1,0:T(8,128)(2,1)} custom-call(bf16[128,1536]{1,0:T(8,128)(2,1)} %bitcast.159), custom_call_target="tpu_custom_call" | custom-call | tf_op jit(solution)/shard_map/pallas_call | solution.py:311
  144.1 5.2 fusion.5
  151.8 48.9 %shard_map.203 = bf16[5,128,1536]{2,1,0:T(8,128)(2,1)} custom-call(bf16[128,1536]{1,0:T(8,128)(2,1)} %pad_maximum_fusion.3.kv_ref), custom_call_target="tpu_custom_call" | custom-call | tf_op jit(solution)/shard_map/pallas_call | solution.py:116
  205.6 4.4 fusion.53
  219.0 14.8 %shard_map.204 = bf16[4,128,1536]{2,1,0:T(8,128)(2,1)} custom-call(bf16[128,1536]{1,0:T(8,128)(2,1)} %multiply_convert_fusion.3.x_ref), custom_call_target="tpu_custom_call" | custom-call | tf_op jit(solution)/shard_map/pallas_call | solution.py:311
  233.9 43.5 %all-gather.5.cloned.1.call-done = bf16[8,288,2048]{2,1,0:T(8,128)(2,1)} async-done(((bf16[1,288,2048]{2,1,0:T(8,128)(2,1)}), bf16[8,288,2048]{2,1,0:T(8,128)(2,1)}) %all-gather.5.cloned.1.call-update) | async-done | bytes 9437200 | tf_op jit(solution)/shard_map/all_gather | solution.py:456
  295.2 6.0 reshape_reshape.3
  301.2 6.0 multiply_convert_fusion.1
  309.2 5.5 convolution_convert_fusion.1
  314.8 8.5 %fusion.57.p_ref = f32[4,128,1536]{2,1,0:T(8,128)} fusion(bf16[4,128,2048]{2,1,0:T(8,128)(2,1)} %bitcast.148, bf16[1536,2048,1]{1,0,2:T(8,128)(2,1)} %bitcast.131), kind=kOutput, calls=%fused_computation.128 | convolution fusion | flops 3221225472 | bytes 11534336 | tf_op jit(solution)/shard_map/dot_general | solution.py:63
  323.3 26.1 %shard_map.206 = f32[128,1536]{1,0:T(8,128)} custom-call(f32[4,128,1536]{2,1,0:T(8,128)} %fusion.57.p_ref), custom_call_target="tpu_custom_call" | custom-call | tf_op jit(solution)/shard_map/pallas_call | solution.py:354
  353.3 4.8 fusion.21
  361.4 5.6 fusion.8
  389.7 9.8 %reduce-scatter.4.cloned.1.call-done = bf16[128,1536]{1,0:T(8,128)(2,1)} async-done(((bf16[1024,1536]{1,0:T(8,128)(2,1)}), bf16[128,1536]{1,0:T(8,128)(2,1)}) %reduce-scatter.4.cloned.1.call-update) | async-done | bytes 393232 | tf_op jit(solution)/shard_map/reduce_scatter | solution.py:513
  403.3 111.4 %shard_map.207 = f32[128,1536]{1,0:T(8,128)} custom-call(f32[128,1536]{1,0:T(8,128)} %scatter-add.11.own_ref, bf16[4,128,1536]{2,1,0:T(8,128)(2,1)} %bitcast.134), custom_call_target="tpu_custom_call" | custom-call | tf_op jit(solution)/shard_map/pallas_call | solution.py:163
  517.2 7.8 %fusion.35 = (bf16[1536]{0:T(1024)(128)(2,1)S(1)}, f32[128]{0:T(128)S(1)}, f32[128,1536]{1,0:T(8,128)}) fusion(bf16[1,128,1536]{2,1,0:T(8,128)(2,1)S(1)} %copy-done.9, f32[128]{0:T(128)S(1)} %add_rsqrt_fusion.1, f32[1536]{0:T(1024)S(1)} %get-tuple-element.56, bf16[1536,4736]{1,0:T(8,128)(2,1)} %all-gather.3.cloned.1.call-done, ...), kind=kOutput, calls=%fused_computation.54 | convolution fusion | flops 1211693440 | bytes 11413504 | tf_op jit(solution)/shard_map/dot_general | solution.py:63
  525.3 4.9 convolution_convert_fusion
  533.8 7.5 %fusion.2 = bf16[1536,4736]{1,0:T(8,128)(2,1)} fusion(bf16[1536,2]{1,0:T(8,128)(2,1)S(1)} %copy.119, bf16[1536,1536]{1,0:T(8,128)(2,1)S(1)} %bitcast.126, bf16[1536,3072]{1,0:T(8,128)(2,1)S(1)} %convolution_convert_fusion), kind=kLoop, calls=%fused_computation.3 | loop fusion | flops 58195968 | bytes 28710912 | tf_op jit(solution)/shard_map/concatenate | solution.py:577
  552.2 26.1 %shard_map.208 = f32[128,1536]{1,0:T(8,128)} custom-call(f32[4,128,1536]{2,1,0:T(8,128)} %bitcast.144), custom_call_target="tpu_custom_call" | custom-call | tf_op jit(solution)/shard_map/pallas_call | solution.py:354
  587.3 8.4 %all-to-all-done.1 = bf16[4,48,2048]{2,1,0:T(8,128)(2,1)S(1)} async-done(((bf16[4,48,2048]{2,1,0:T(8,128)(2,1)}), bf16[4,48,2048]{2,1,0:T(8,128)(2,1)S(1)}, u32[]{:S(2)}, u32[]{:S(2)}) %all-to-all-start.1) | async-done | bytes 786464 | tf_op jit(solution)/shard_map/all_to_all | solution.py:523
  598.9 129.3 %reduce-scatter.6.cloned.1.call-done = bf16[48,4736]{1,0:T(8,128)(2,1)} async-done(((bf16[1536,4736]{1,0:T(8,128)(2,1)}), bf16[48,4736]{1,0:T(8,128)(2,1)}) %reduce-scatter.6.cloned.1.call-update) | async-done | bytes 454672 | tf_op jit(solution)/shard_map/reduce_scatter | solution.py:585
  (175 shorter events, 117.5 us)
Async XLA Ops:
  7.2 115.6 %all-gather.3.cloned.1.call-start = ((), (), s32[]{:S(2)}) async-start(), calls=%async_computation.5 | async-start | bytes 15003648 | tf_op jit(solution)/shard_map/all_gather | solution.py:408
  13.7 7.1 copy-start.26
  16.6 19.1 %all-to-all-start = ((bf16[4,48,2,8,128]{4,3,1,2,0:T(8,128)(2,1)}), bf16[4,48,2,8,128]{4,3,1,2,0:T(8,128)(2,1)S(1)}, u32[]{:S(2)}, u32[]{:S(2)}) async-start(bf16[4,48,2,8,128]{4,3,1,2,0:T(8,128)(2,1)} %copy.107), calls=%async_computation | async-start | bytes 1572864 | tf_op jit(solution)/shard_map/all_to_all | solution.py:452
  20.8 256.6 %all-gather.5.cloned.1.call-start = ((), (), s32[]{:S(2)}) async-start(), calls=%async_computation.6 | async-start | bytes 10616832 | tf_op jit(solution)/shard_map/all_gather | solution.py:456
  35.9 90.5 %copy-start.27 = (s32[1,8]{1,0:T(1,128)S(1)}, s32[1,8]{1,0:T(1,128)}, u32[]{:S(2)}) copy-start(s32[1,8]{1,0:T(1,128)} %param.19) | copy-start | bytes 100
  36.7 105.1 %copy-start.7 = (bf16[1,128,1536]{2,1,0:T(8,128)(2,1)S(1)}, bf16[1,128,1536]{2,1,0:T(8,128)(2,1)}, u32[]{:S(2)}) copy-start(bf16[1,128,1536]{2,1,0:T(8,128)(2,1)} %param.18) | copy-start | bytes 1179652
  126.3 273.1 %reduce-scatter.4.cloned.1.call-start = ((), (), s32[]{:S(2)}) async-start(), calls=%async_computation.7 | async-start | bytes 3538944 | tf_op jit(solution)/shard_map/reduce_scatter | solution.py:513
  203.0 7.0 copy-start.12
  205.6 4.4 copy-start.17
  214.8 3.4 copy-start.14
  277.4 3.5 copy-start.20
  280.9 3.4 copy-start.5
  291.0 289.5 %reduce-scatter.8.cloned.1.call-start = ((), (), s32[]{:S(2)}) async-start(), calls=%async_computation.9 | async-start | bytes 7077888 | tf_op jit(solution)/shard_map/reduce_scatter | solution.py:522
  314.8 413.4 %reduce-scatter.6.cloned.1.call-start = ((), (), s32[]{:S(2)}) async-start(), calls=%async_computation.8 | async-start | bytes 15003648 | tf_op jit(solution)/shard_map/reduce_scatter | solution.py:585
  361.4 5.6 copy-start.18
  379.9 3.7 copy-start.1
  403.3 113.9 %copy-start.9 = (bf16[1,128,1536]{2,1,0:T(8,128)(2,1)S(1)}, bf16[1,128,1536]{2,1,0:T(8,128)(2,1)}, u32[]{:S(2)}) copy-start(bf16[1,128,1536]{2,1,0:T(8,128)(2,1)} %param.18) | copy-start | bytes 1179652
  403.3 113.9 %copy-start.16 = (bf16[128,16,96]{0,2,1:T(8,128)(2,1)S(1)}, bf16[128,16,96]{0,2,1:T(8,128)(2,1)}, u32[]{:S(2)}) copy-start(bf16[128,16,96]{0,2,1:T(8,128)(2,1)} %pad_maximum_fusion.5) | copy-start | bytes 1179652
  525.0 8.7 %slice-start = ((s8[4718592]{0:T(1024)(128)(4,1)}), s8[524288]{0:T(1024)(128)(4,1)S(1)}, s32[]{:S(2)}) async-start(s8[4718592]{0:T(1024)(128)(4,1)} %bitcast.125), calls=%async_computation.10 | async-start | bytes 1048576
  525.3 8.5 %slice-start.1 = ((s8[4718592]{0:T(1024)(128)(4,1)}), s8[4194304]{0:T(1024)(128)(4,1)S(1)}, s32[]{:S(2)}) async-start(s8[4718592]{0:T(1024)(128)(4,1)} %bitcast.125), calls=%async_computation.11 | async-start | bytes 8388608
  530.2 3.6 copy-start
  578.3 7.8 %copy-start.4 = (f32[128,1536]{1,0:T(8,128)S(1)}, f32[128,1536]{1,0:T(8,128)}, u32[]{:S(2)}) copy-start(f32[128,1536]{1,0:T(8,128)} %copy-done.2) | copy-start | bytes 2359300
  580.4 5.7 copy-start.25
  580.4 15.3 %all-to-all-start.1 = ((bf16[4,48,2048]{2,1,0:T(8,128)(2,1)}), bf16[4,48,2048]{2,1,0:T(8,128)(2,1)S(1)}, u32[]{:S(2)}, u32[]{:S(2)}) async-start(bf16[4,48,2048]{2,1,0:T(8,128)(2,1)} %bitcast.160), calls=%async_computation.4 | async-start | bytes 1572864 | tf_op jit(solution)/shard_map/all_to_all | solution.py:523
  (13 other events, 21.4 us)
Sparse Core Ops, SparseCore 0:
  12.6 110.1 all-gather.2
  126.5 150.9 all-gather.4
  291.1 108.3 reduce-scatter.3
  402.9 155.1 reduce-scatter.7
  564.1 164.0 reduce-scatter.5

commit v15 on v14

--- a/solution.py
+++ b/solution.py
@@ -338,12 +338,12 @@
     to_diagonal.start()
     to_partner.wait_recv()
     to_diagonal.wait_recv()
-    sum_buf[...] = p_ref[across] + near_buf[1]
+    sum_buf[...] = (p_ref[across] + near_buf[1]).astype(sum_buf.dtype)
     to_across = copy(sum_buf, far_buf, across, 2)
     to_across.start()
     out_ref[...] = p_ref[f] + near_buf[0]
     to_across.wait_recv()
-    out_ref[...] += far_buf[...]
+    out_ref[...] += far_buf[...].astype(out_ref.dtype)
     to_partner.wait_send()
     to_diagonal.wait_send()
     to_across.wait_send()
@@ -358,8 +358,8 @@
         out_specs=pl.BlockSpec(memory_space=pltpu.VMEM),
         scratch_shapes=[
             pltpu.VMEM((2,) + block, p.dtype),
-            pltpu.VMEM(block, p.dtype),
-            pltpu.VMEM(block, p.dtype),
+            pltpu.VMEM(block, jnp.bfloat16),
+            pltpu.VMEM(block, jnp.bfloat16),
             pltpu.SemaphoreType.DMA((3,)),
             pltpu.SemaphoreType.DMA((3,)),
         ],

time: 747 us -> 750 us (level)
  waiting for transfers between devices: 292 us -> 312 us
  Pallas kernels: 242 us -> 225 us
    pallas_call x2, Pallas kernels: 52.3 us -> 35.4 us  [quad_reduce(): pl.pallas_call(quad_reduce_kernel, out_shape=jax.ShapeDtypeStruct(block,...]
    reduce_scatter x1, waiting for transfers between devices: 129 us -> 141 us  [body(): lax.psum_scatter(attention_pack, ALL, scatter_dimension=0, tiled=True)]
    reduce_scatter x1, waiting for transfers between devices: 9.75 us -> 18.1 us  [body(): lax.psum_scatter(down_term, 'ctx', scatter_dimension=0, tiled=True)]
  transfers between devices with their start and end apart: 7 -> 7, of which waited for: 6 -> 6; matrix products, arithmetic and copies ran while one was open for 20% -> 20% of each run, Pallas kernels for 33% -> 30%
where the time goes in v15:
time: 750 us; the launch traced here: 743 us
  waiting for transfers between devices  312 us (42%)
  Pallas kernels  225 us (30%)
  matrix products  81.6 us (11%)
  local copies, waits for them, and re-layouts  63.4 us (8%)
  other arithmetic  34.7 us (5%)
  between operations  18.8 us (3%)
  starting transfers between devices  8.22 us (1%)
    reduce_scatter x1, waiting for transfers between devices, body(): lax.psum_scatter(attention_pack, ALL, scatter_dimension=0, tiled=True)  141 us
    pallas_call x1, Pallas kernels, kv_return(): pl.pallas_call(functools.partial(kv_return_kernel, n_ctx, back), out_shap...  111 us
    all_gather x1, waiting for transfers between devices, body(): lax.all_gather(jnp.concatenate([query_weight, key_weight, value_weight, o...  85.9 us
    pallas_call x1, Pallas kernels, kv_share(): pl.pallas_call(functools.partial(kv_share_kernel, n_ctx, back), out_shape...  48.9 us
    all_gather x1, waiting for transfers between devices, body(): ff_stack = lax.all_gather(ff_pack, 'ctx', axis=0, tiled=False)  43.5 us
    pallas_call x2, Pallas kernels, quad_reduce(): pl.pallas_call(quad_reduce_kernel, out_shape=jax.ShapeDtypeStruct(block,...  35.4 us
    pallas_call x2, Pallas kernels, quad_gather(): pl.pallas_call(quad_gather_kernel, out_shape=jax.ShapeDtypeStruct((4,) +...  29.7 us
    dot_general x4, matrix products, times_transposed(): lax.dot_general(left, right, (((1,), (1,)), ((), ())), preferred_element_...  27.1 us
  transfers between devices with their start and end apart: 7, of which 6 were waited for; matrix products, arithmetic and copies ran while one was open for 20% of the time, Pallas kernels for 30%

profile of v15, /device:TPU:0, one launch (start us, length us, event | category | flops | bytes accessed | tf_op | source)
XLA Modules:
  0.0 743.4 jit_solution(8292438414628847511)
XLA Ops:
  16.6 4.2 all-to-all-start
  21.2 14.6 %all-to-all-done = bf16[4,48,2,8,128]{4,3,1,2,0:T(8,128)(2,1)S(1)} async-done(((bf16[4,48,2,8,128]{4,3,1,2,0:T(8,128)(2,1)}), bf16[4,48,2,8,128]{4,3,1,2,0:T(8,128)(2,1)S(1)}, u32[]{:S(2)}, u32[]{:S(2)}) %all-to-all-start) | async-done | bytes 786464 | tf_op jit(solution)/shard_map/all_to_all | solution.py:452
  36.9 85.9 %all-gather.3.cloned.1.call-done = bf16[1536,4736]{1,0:T(8,128)(2,1)} async-done(((bf16[48,4736]{1,0:T(8,128)(2,1)}), bf16[1536,4736]{1,0:T(8,128)(2,1)}) %all-gather.3.cloned.1.call-update) | async-done | bytes 14549008 | tf_op jit(solution)/shard_map/all_gather | solution.py:408
  126.6 14.9 %shard_map.205 = bf16[4,128,1536]{2,1,0:T(8,128)(2,1)} custom-call(bf16[128,1536]{1,0:T(8,128)(2,1)} %bitcast.159), custom_call_target="tpu_custom_call" | custom-call | tf_op jit(solution)/shard_map/pallas_call | solution.py:311
  144.1 5.2 fusion.5
  151.8 48.9 %shard_map.203 = bf16[5,128,1536]{2,1,0:T(8,128)(2,1)} custom-call(bf16[128,1536]{1,0:T(8,128)(2,1)} %pad_maximum_fusion.3.kv_ref), custom_call_target="tpu_custom_call" | custom-call | tf_op jit(solution)/shard_map/pallas_call | solution.py:116
  205.6 4.4 fusion.53
  219.0 14.8 %shard_map.204 = bf16[4,128,1536]{2,1,0:T(8,128)(2,1)} custom-call(bf16[128,1536]{1,0:T(8,128)(2,1)} %multiply_convert_fusion.3.x_ref), custom_call_target="tpu_custom_call" | custom-call | tf_op jit(solution)/shard_map/pallas_call | solution.py:311
  233.9 43.5 %all-gather.5.cloned.1.call-done = bf16[8,288,2048]{2,1,0:T(8,128)(2,1)} async-done(((bf16[1,288,2048]{2,1,0:T(8,128)(2,1)}), bf16[8,288,2048]{2,1,0:T(8,128)(2,1)}) %all-gather.5.cloned.1.call-update) | async-done | bytes 9437200 | tf_op jit(solution)/shard_map/all_gather | solution.py:456
  295.2 6.0 reshape_reshape.3
  301.2 6.0 multiply_convert_fusion.1
  309.2 5.5 convolution_convert_fusion.1
  314.8 8.5 %fusion.57.p_ref = f32[4,128,1536]{2,1,0:T(8,128)} fusion(bf16[4,128,2048]{2,1,0:T(8,128)(2,1)} %bitcast.148, bf16[1536,2048,1]{1,0,2:T(8,128)(2,1)} %bitcast.131), kind=kOutput, calls=%fused_computation.128 | convolution fusion | flops 3221225472 | bytes 11534336 | tf_op jit(solution)/shard_map/dot_general | solution.py:63
  323.3 17.7 %shard_map.206 = f32[128,1536]{1,0:T(8,128)} custom-call(f32[4,128,1536]{2,1,0:T(8,128)} %fusion.57.p_ref), custom_call_target="tpu_custom_call" | custom-call | tf_op jit(solution)/shard_map/pallas_call | solution.py:354
  344.8 4.8 fusion.21
  352.9 5.6 fusion.8
  381.4 18.1 %reduce-scatter.4.cloned.1.call-done = bf16[128,1536]{1,0:T(8,128)(2,1)} async-done(((bf16[1024,1536]{1,0:T(8,128)(2,1)}), bf16[128,1536]{1,0:T(8,128)(2,1)}) %reduce-scatter.4.cloned.1.call-update) | async-done | bytes 393232 | tf_op jit(solution)/shard_map/reduce_scatter | solution.py:513
  403.3 111.1 %shard_map.207 = f32[128,1536]{1,0:T(8,128)} custom-call(f32[128,1536]{1,0:T(8,128)} %scatter-add.11.own_ref, bf16[4,128,1536]{2,1,0:T(8,128)(2,1)} %bitcast.134), custom_call_target="tpu_custom_call" | custom-call | tf_op jit(solution)/shard_map/pallas_call | solution.py:163
  516.9 7.8 %fusion.35 = (bf16[1536]{0:T(1024)(128)(2,1)S(1)}, f32[128]{0:T(128)S(1)}, f32[128,1536]{1,0:T(8,128)}) fusion(bf16[1,128,1536]{2,1,0:T(8,128)(2,1)S(1)} %copy-done.9, f32[128]{0:T(128)S(1)} %add_rsqrt_fusion.1, f32[1536]{0:T(1024)S(1)} %get-tuple-element.56, bf16[1536,4736]{1,0:T(8,128)(2,1)} %all-gather.3.cloned.1.call-done, ...), kind=kOutput, calls=%fused_computation.54 | convolution fusion | flops 1211693440 | bytes 11413504 | tf_op jit(solution)/shard_map/dot_general | solution.py:63
  525.1 4.9 convolution_convert_fusion
  533.7 7.5 %fusion.2 = bf16[1536,4736]{1,0:T(8,128)(2,1)} fusion(bf16[1536,2]{1,0:T(8,128)(2,1)S(1)} %copy.119, bf16[1536,1536]{1,0:T(8,128)(2,1)S(1)} %bitcast.126, bf16[1536,3072]{1,0:T(8,128)(2,1)S(1)} %convolution_convert_fusion), kind=kLoop, calls=%fused_computation.3 | loop fusion | flops 58195968 | bytes 28710912 | tf_op jit(solution)/shard_map/concatenate | solution.py:577
  552.0 17.7 %shard_map.208 = f32[128,1536]{1,0:T(8,128)} custom-call(f32[4,128,1536]{2,1,0:T(8,128)} %bitcast.144), custom_call_target="tpu_custom_call" | custom-call | tf_op jit(solution)/shard_map/pallas_call | solution.py:354
  578.6 8.4 %all-to-all-done.1 = bf16[4,48,2048]{2,1,0:T(8,128)(2,1)S(1)} async-done(((bf16[4,48,2048]{2,1,0:T(8,128)(2,1)}), bf16[4,48,2048]{2,1,0:T(8,128)(2,1)S(1)}, u32[]{:S(2)}, u32[]{:S(2)}) %all-to-all-start.1) | async-done | bytes 786464 | tf_op jit(solution)/shard_map/all_to_all | solution.py:523
  590.2 141.0 %reduce-scatter.6.cloned.1.call-done = bf16[48,4736]{1,0:T(8,128)(2,1)} async-done(((bf16[1536,4736]{1,0:T(8,128)(2,1)}), bf16[48,4736]{1,0:T(8,128)(2,1)}) %reduce-scatter.6.cloned.1.call-update) | async-done | bytes 454672 | tf_op jit(solution)/shard_map/reduce_scatter | solution.py:585
  (175 shorter events, 117.5 us)
Async XLA Ops:
  7.2 115.6 %all-gather.3.cloned.1.call-start = ((), (), s32[]{:S(2)}) async-start(), calls=%async_computation.5 | async-start | bytes 15003648 | tf_op jit(solution)/shard_map/all_gather | solution.py:408
  13.7 7.1 copy-start.26
  16.6 19.1 %all-to-all-start = ((bf16[4,48,2,8,128]{4,3,1,2,0:T(8,128)(2,1)}), bf16[4,48,2,8,128]{4,3,1,2,0:T(8,128)(2,1)S(1)}, u32[]{:S(2)}, u32[]{:S(2)}) async-start(bf16[4,48,2,8,128]{4,3,1,2,0:T(8,128)(2,1)} %copy.107), calls=%async_computation | async-start | bytes 1572864 | tf_op jit(solution)/shard_map/all_to_all | solution.py:452
  20.8 256.6 %all-gather.5.cloned.1.call-start = ((), (), s32[]{:S(2)}) async-start(), calls=%async_computation.6 | async-start | bytes 10616832 | tf_op jit(solution)/shard_map/all_gather | solution.py:456
  35.9 90.5 %copy-start.27 = (s32[1,8]{1,0:T(1,128)S(1)}, s32[1,8]{1,0:T(1,128)}, u32[]{:S(2)}) copy-start(s32[1,8]{1,0:T(1,128)} %param.19) | copy-start | bytes 100
  36.7 105.1 %copy-start.7 = (bf16[1,128,1536]{2,1,0:T(8,128)(2,1)S(1)}, bf16[1,128,1536]{2,1,0:T(8,128)(2,1)}, u32[]{:S(2)}) copy-start(bf16[1,128,1536]{2,1,0:T(8,128)(2,1)} %param.18) | copy-start | bytes 1179652
  126.3 273.2 %reduce-scatter.4.cloned.1.call-start = ((), (), s32[]{:S(2)}) async-start(), calls=%async_computation.7 | async-start | bytes 3538944 | tf_op jit(solution)/shard_map/reduce_scatter | solution.py:513
  203.0 7.0 copy-start.12
  205.6 4.4 copy-start.17
  214.8 3.4 copy-start.14
  277.4 3.5 copy-start.20
  280.9 3.4 copy-start.5
  291.0 280.8 %reduce-scatter.8.cloned.1.call-start = ((), (), s32[]{:S(2)}) async-start(), calls=%async_computation.9 | async-start | bytes 7077888 | tf_op jit(solution)/shard_map/reduce_scatter | solution.py:522
  314.8 416.4 %reduce-scatter.6.cloned.1.call-start = ((), (), s32[]{:S(2)}) async-start(), calls=%async_computation.8 | async-start | bytes 15003648 | tf_op jit(solution)/shard_map/reduce_scatter | solution.py:585
  352.9 5.6 copy-start.18
  371.6 3.7 copy-start.1
  403.3 113.6 %copy-start.9 = (bf16[1,128,1536]{2,1,0:T(8,128)(2,1)S(1)}, bf16[1,128,1536]{2,1,0:T(8,128)(2,1)}, u32[]{:S(2)}) copy-start(bf16[1,128,1536]{2,1,0:T(8,128)(2,1)} %param.18) | copy-start | bytes 1179652
  403.3 113.6 %copy-start.16 = (bf16[128,16,96]{0,2,1:T(8,128)(2,1)S(1)}, bf16[128,16,96]{0,2,1:T(8,128)(2,1)}, u32[]{:S(2)}) copy-start(bf16[128,16,96]{0,2,1:T(8,128)(2,1)} %pad_maximum_fusion.5) | copy-start | bytes 1179652
  524.8 8.9 %slice-start = ((s8[4718592]{0:T(1024)(128)(4,1)}), s8[524288]{0:T(1024)(128)(4,1)S(1)}, s32[]{:S(2)}) async-start(s8[4718592]{0:T(1024)(128)(4,1)} %bitcast.125), calls=%async_computation.10 | async-start | bytes 1048576
  525.1 8.6 %slice-start.1 = ((s8[4718592]{0:T(1024)(128)(4,1)}), s8[4194304]{0:T(1024)(128)(4,1)S(1)}, s32[]{:S(2)}) async-start(s8[4718592]{0:T(1024)(128)(4,1)} %bitcast.125), calls=%async_computation.11 | async-start | bytes 8388608
  530.0 3.7 copy-start
  569.7 7.7 %copy-start.4 = (f32[128,1536]{1,0:T(8,128)S(1)}, f32[128,1536]{1,0:T(8,128)}, u32[]{:S(2)}) copy-start(f32[128,1536]{1,0:T(8,128)} %copy-done.2) | copy-start | bytes 2359300
  571.8 5.6 copy-start.25
  571.8 15.3 %all-to-all-start.1 = ((bf16[4,48,2048]{2,1,0:T(8,128)(2,1)}), bf16[4,48,2048]{2,1,0:T(8,128)(2,1)S(1)}, u32[]{:S(2)}, u32[]{:S(2)}) async-start(bf16[4,48,2048]{2,1,0:T(8,128)(2,1)} %bitcast.160), calls=%async_computation.4 | async-start | bytes 1572864 | tf_op jit(solution)/shard_map/all_to_all | solution.py:523
  (13 other events, 21.4 us)
Sparse Core Ops, SparseCore 0:
  12.6 110.1 all-gather.2
  126.5 150.9 all-gather.4
  291.1 108.3 reduce-scatter.3
  402.9 158.3 reduce-scatter.7
  567.2 163.9 reduce-scatter.5

commit v16 on v12

--- a/solution.py
+++ b/solution.py
@@ -578,7 +578,6 @@
     gain_term_cols = jnp.pad(
         jnp.stack([gain_one_term, gain_two_term], axis=1), ((0, 0), (0, GAIN_PAD - 2))
     )
-    gain_term_cols = gain_term_cols.at[0, GAIN_PAD - 1].set(ff_sum[0, 0].astype(jnp.float32) * 0.0)
     attention_pack = jnp.concatenate(
         [
             outer_rows(normed_low, projection_cat).astype(jnp.bfloat16),

time: 755 us -> 727 us (0.963)
  waiting for transfers between devices: 285 us -> 272 us
    reduce_scatter x1, waiting for transfers between devices: 17.9 us -> 0.01 us  [body(): lax.psum_scatter(grad_pack, 'ctx', scatter_dimension=0, tiled=True)]
    reduce_scatter x1, waiting for transfers between devices: 120 us -> 128 us  [body(): lax.psum_scatter(attention_pack, ALL, scatter_dimension=0, tiled=True)]
  transfers between devices with their start and end apart: 6 -> 6, of which waited for: 6 -> 4; matrix products, arithmetic and copies ran while one was open for 16% -> 17% of each run, Pallas kernels for 31% -> 33%
where the time goes in v16:
time: 727 us; the launch traced here: 720 us
  waiting for transfers between devices  272 us (37%)
  Pallas kernels  236 us (32%)
  matrix products  72.1 us (10%)
  local copies, waits for them, and re-layouts  71.9 us (10%)
  other arithmetic  43.1 us (6%)
  between operations  17.3 us (2%)
  starting transfers between devices  7.84 us (1%)
    reduce_scatter x1, waiting for transfers between devices, body(): lax.psum_scatter(attention_pack, ALL, scatter_dimension=0, tiled=True)  128 us
    pallas_call x1, Pallas kernels, kv_return(): pl.pallas_call(functools.partial(kv_return_kernel, n_ctx, back), out_shap...  105 us
    all_gather x1, waiting for transfers between devices, body(): lax.all_gather(jnp.concatenate([query_weight, key_weight, value_weight, o...  85.9 us
    pallas_call x2, Pallas kernels, quad_reduce(): pl.pallas_call(quad_reduce_kernel, out_shape=jax.ShapeDtypeStruct(block,...  52.3 us
    pallas_call x1, Pallas kernels, kv_share(): pl.pallas_call(functools.partial(kv_share_kernel, n_ctx, back), out_shape...  48.9 us
    all_gather x1, waiting for transfers between devices, body(): ff_stack = lax.all_gather(ff_pack, 'ctx', axis=0, tiled=False)  43.9 us
    pallas_call x2, Pallas kernels, quad_gather(): pl.pallas_call(quad_gather_kernel, out_shape=jax.ShapeDtypeStruct((4,) +...  29.7 us
    dot_general x4, matrix products, times_transposed(): lax.dot_general(left, right, (((1,), (1,)), ((), ())), preferred_element_...  23.8 us
  transfers between devices with their start and end apart: 6, of which 4 were waited for; matrix products, arithmetic and copies ran while one was open for 17% of the time, Pallas kernels for 33%

profile of v16, /device:TPU:0, one launch (start us, length us, event | category | flops | bytes accessed | tf_op | source)
XLA Modules:
  0.0 720.3 jit_solution(7108169848176037461)
XLA Ops:
  16.6 4.2 all-to-all-start
  21.2 14.6 %all-to-all-done = bf16[4,48,2,8,128]{4,3,1,2,0:T(8,128)(2,1)S(1)} async-done(((bf16[4,48,2,8,128]{4,3,1,2,0:T(8,128)(2,1)}), bf16[4,48,2,8,128]{4,3,1,2,0:T(8,128)(2,1)S(1)}, u32[]{:S(2)}, u32[]{:S(2)}) %all-to-all-start) | async-done | bytes 786464 | tf_op jit(solution)/shard_map/all_to_all | solution.py:452
  36.9 85.9 %all-gather.3.cloned.1.call-done = bf16[1536,4736]{1,0:T(8,128)(2,1)} async-done(((bf16[48,4736]{1,0:T(8,128)(2,1)}), bf16[1536,4736]{1,0:T(8,128)(2,1)}) %all-gather.3.cloned.1.call-update) | async-done | bytes 14549008 | tf_op jit(solution)/shard_map/all_gather | solution.py:408
  126.6 14.8 %shard_map.205 = bf16[4,128,1536]{2,1,0:T(8,128)(2,1)} custom-call(bf16[128,1536]{1,0:T(8,128)(2,1)} %bitcast.172), custom_call_target="tpu_custom_call" | custom-call | tf_op jit(solution)/shard_map/pallas_call | solution.py:311
  144.0 5.2 fusion.5
  151.6 48.9 %shard_map.203 = bf16[5,128,1536]{2,1,0:T(8,128)(2,1)} custom-call(bf16[128,1536]{1,0:T(8,128)(2,1)} %pad_maximum_fusion.4.kv_ref), custom_call_target="tpu_custom_call" | custom-call | tf_op jit(solution)/shard_map/pallas_call | solution.py:116
  205.5 4.4 fusion.58
  218.9 14.9 %shard_map.204 = bf16[4,128,1536]{2,1,0:T(8,128)(2,1)} custom-call(bf16[128,1536]{1,0:T(8,128)(2,1)} %multiply_convert_fusion.1.x_ref), custom_call_target="tpu_custom_call" | custom-call | tf_op jit(solution)/shard_map/pallas_call | solution.py:311
  233.8 43.9 %all-gather.5.cloned.1.call-done = bf16[8,288,2048]{2,1,0:T(8,128)(2,1)} async-done(((bf16[1,288,2048]{2,1,0:T(8,128)(2,1)}), bf16[8,288,2048]{2,1,0:T(8,128)(2,1)}) %all-gather.5.cloned.1.call-update) | async-done | bytes 9437200 | tf_op jit(solution)/shard_map/all_gather | solution.py:456
  277.7 4.0 slice.212
  281.7 6.0 reshape_reshape.3
  300.0 5.7 convolution_convert_fusion.1
  309.2 6.0 reshape.368
  315.2 7.9 %pad_maximum_fusion = bf16[8,288,2048]{2,1,0:T(8,128)(2,1)} fusion(bf16[8,96,2048]{2,1,0:T(8,128)(2,1)} %reshape.368, bf16[8,192,2048]{2,1,0:T(8,128)(2,1)} %bitcast.147), kind=kLoop, calls=%fused_computation.5 | loop fusion | flops 18874368 | bytes 18874368 | tf_op jit(solution)/shard_map/concatenate | solution.py:518
  323.1 8.5 %fusion.62.p_ref = f32[4,128,1536]{2,1,0:T(8,128)} fusion(bf16[4,128,2048]{2,1,0:T(8,128)(2,1)} %bitcast.161, bf16[1536,2048,1]{1,0,2:T(8,128)(2,1)} %bitcast.144), kind=kOutput, calls=%fused_computation.134 | convolution fusion | flops 3221225472 | bytes 11534336 | tf_op jit(solution)/shard_map/dot_general | solution.py:63
  331.6 26.2 %shard_map.206 = f32[128,1536]{1,0:T(8,128)} custom-call(f32[4,128,1536]{2,1,0:T(8,128)} %fusion.62.p_ref), custom_call_target="tpu_custom_call" | custom-call | tf_op jit(solution)/shard_map/pallas_call | solution.py:354
  361.6 4.8 fusion.21
  369.6 4.1 fusion.8
  390.5 104.8 %shard_map.207 = f32[128,1536]{1,0:T(8,128)} custom-call(f32[128,1536]{1,0:T(8,128)} %fusion.42.own_ref, bf16[4,128,1536]{2,1,0:T(8,128)(2,1)} %bitcast.146), custom_call_target="tpu_custom_call" | custom-call | tf_op jit(solution)/shard_map/pallas_call | solution.py:163
  505.6 8.0 %fusion.40 = (bf16[1536]{0:T(1024)(128)(2,1)S(1)}, f32[128]{0:T(128)S(1)}, f32[128,1536]{1,0:T(8,128)}) fusion(bf16[1,128,1536]{2,1,0:T(8,128)(2,1)S(1)} %copy-done.11, f32[128]{0:T(128)S(1)} %add_rsqrt_fusion.1, f32[1536]{0:T(1024)S(1)} %get-tuple-element.40, bf16[1536,4736]{1,0:T(8,128)(2,1)} %all-gather.3.cloned.1.call-done, ...), kind=kOutput, calls=%fused_computation.59 | convolution fusion | flops 1211693440 | bytes 11413504 | tf_op jit(solution)/shard_map/dot_general | solution.py:63
  515.4 4.9 convolution_convert_fusion
  523.8 7.5 %fusion.2 = bf16[1536,4736]{1,0:T(8,128)(2,1)} fusion(bf16[1536,2]{1,0:T(8,128)(2,1)S(1)} %copy.139, bf16[1536,1536]{1,0:T(8,128)(2,1)S(1)} %convolution_convert_fusion.2, bf16[1536,3072]{1,0:T(8,128)(2,1)S(1)} %convolution_convert_fusion), kind=kLoop, calls=%fused_computation.3 | loop fusion | flops 58195968 | bytes 28710912 | tf_op jit(solution)/shard_map/concatenate | solution.py:581
  541.2 26.1 %shard_map.208 = f32[128,1536]{1,0:T(8,128)} custom-call(f32[4,128,1536]{2,1,0:T(8,128)} %bitcast.157), custom_call_target="tpu_custom_call" | custom-call | tf_op jit(solution)/shard_map/pallas_call | solution.py:354
  577.3 127.8 %reduce-scatter.3.cloned.1.call-done = bf16[48,4736]{1,0:T(8,128)(2,1)} async-done(((bf16[1536,4736]{1,0:T(8,128)(2,1)}), bf16[48,4736]{1,0:T(8,128)(2,1)}) %reduce-scatter.3.cloned.1.call-update) | async-done | bytes 454672 | tf_op jit(solution)/shard_map/reduce_scatter | solution.py:589
  (179 shorter events, 114.0 us)
Async XLA Ops:
  7.2 115.6 %all-gather.3.cloned.1.call-start = ((), (), s32[]{:S(2)}) async-start(), calls=%async_computation.4 | async-start | bytes 15003648 | tf_op jit(solution)/shard_map/all_gather | solution.py:408
  12.5 8.4 %copy-start.30 = (bf16[128,1536]{1,0:T(8,128)(2,1)S(1)}, bf16[128,1536]{1,0:T(8,128)(2,1)}, u32[]{:S(2)}) copy-start(bf16[128,1536]{1,0:T(8,128)(2,1)} %param.26) | copy-start | bytes 1179652
  16.6 19.1 %all-to-all-start = ((bf16[4,48,2,8,128]{4,3,1,2,0:T(8,128)(2,1)}), bf16[4,48,2,8,128]{4,3,1,2,0:T(8,128)(2,1)S(1)}, u32[]{:S(2)}, u32[]{:S(2)}) async-start(bf16[4,48,2,8,128]{4,3,1,2,0:T(8,128)(2,1)} %copy.127), calls=%async_computation | async-start | bytes 1572864 | tf_op jit(solution)/shard_map/all_to_all | solution.py:452
  20.8 256.9 %all-gather.5.cloned.1.call-start = ((), (), s32[]{:S(2)}) async-start(), calls=%async_computation.5 | async-start | bytes 10616832 | tf_op jit(solution)/shard_map/all_gather | solution.py:456
  21.2 105.3 %copy-start.31 = (s32[1,8]{1,0:T(1,128)S(1)}, s32[1,8]{1,0:T(1,128)}, u32[]{:S(2)}) copy-start(s32[1,8]{1,0:T(1,128)} %param.17) | copy-start | bytes 100
  36.2 105.6 %copy-start.9 = (bf16[1,128,1536]{2,1,0:T(8,128)(2,1)S(1)}, bf16[1,128,1536]{2,1,0:T(8,128)(2,1)}, u32[]{:S(2)}) copy-start(bf16[1,128,1536]{2,1,0:T(8,128)(2,1)} %param.16) | copy-start | bytes 1179652
  126.4 444.2 %reduce-scatter.5.cloned.1.call-start = ((), (), s32[]{:S(2)}) async-start(), calls=%async_computation.7 | async-start | bytes 10616832 | tf_op jit(solution)/shard_map/reduce_scatter | solution.py:526
  202.8 7.0 copy-start.14
  205.5 4.4 copy-start.19
  209.9 3.2 copy-start.13
  214.6 3.4 copy-start.17
  287.7 3.5 copy-start.22
  291.2 3.5 copy-start.7
  291.2 4.2 copy-start.15
  291.2 4.6 copy-start.21
  298.4 7.3 %copy-start.32 = (bf16[512,1024]{1,0:T(8,128)(2,1)}, bf16[512,1024]{1,0:T(8,128)(2,1)S(1)}, u32[]{:S(2)}) copy-start(bf16[512,1024]{1,0:T(8,128)(2,1)S(1)} %get-tuple-element.51) | copy-start | bytes 3145732
  323.1 382.0 %reduce-scatter.3.cloned.1.call-start = ((), (), s32[]{:S(2)}) async-start(), calls=%async_computation.6 | async-start | bytes 15003648 | tf_op jit(solution)/shard_map/reduce_scatter | solution.py:589
  369.6 5.6 copy-start.20
  390.5 113.0 %copy-start.4 = (bf16[128,8,2,640]{0,3,2,1:T(8,128)(2,1)S(1)}, bf16[128,8,2,640]{0,3,2,1:T(8,128)(2,1)}, u32[]{:S(2)}) copy-start(bf16[128,8,2,640]{0,3,2,1:T(8,128)(2,1)} %copy-done.3) | copy-start | bytes 7864324
  505.6 8.3 %copy-start.6 = (f32[128,1536]{1,0:T(8,128)S(1)}, f32[128,1536]{1,0:T(8,128)}, u32[]{:S(2)}) copy-start(f32[128,1536]{1,0:T(8,128)} %copy-done.5) | copy-start | bytes 2359300
  505.6 8.3 %copy-start.18 = (bf16[128,8,2,96]{0,3,2,1:T(8,128)(2,1)S(1)}, bf16[128,8,2,96]{0,3,2,1:T(8,128)(2,1)}, u32[]{:S(2)}) copy-start(bf16[128,8,2,96]{0,3,2,1:T(8,128)(2,1)} %copy-done.17) | copy-start | bytes 1179652
  520.3 3.5 copy-start
  538.0 31.4 %copy-start.25 = (f32[128,1536]{1,0:T(8,128)S(1)}, f32[128,1536]{1,0:T(8,128)}, u32[]{:S(2)}) copy-start(f32[128,1536]{1,0:T(8,128)} %get-tuple-element.77) | copy-start | bytes 2359300
  573.8 136.6 %all-to-all-start.1 = ((bf16[4,48,2048]{2,1,0:T(8,128)(2,1)}), bf16[4,48,2048]{2,1,0:T(8,128)(2,1)S(1)}, u32[]{:S(2)}, u32[]{:S(2)}) async-start(bf16[4,48,2048]{2,1,0:T(8,128)(2,1)} %bitcast.55), calls=%async_computation.3 | async-start | bytes 1572864 | tf_op jit(solution)/shard_map/all_to_all | solution.py:528
  (16 other events, 26.7 us)
Sparse Core Ops, SparseCore 0:
  12.6 110.1 all-gather.2
  126.5 151.1 all-gather.4
  323.2 211.8 reduce-scatter.4
  541.1 164.0 reduce-scatter.2

commit v17 on v16

--- a/solution.py
+++ b/solution.py
@@ -338,12 +338,12 @@
     to_diagonal.start()
     to_partner.wait_recv()
     to_diagonal.wait_recv()
-    sum_buf[...] = p_ref[across] + near_buf[1]
+    sum_buf[...] = (p_ref[across] + near_buf[1]).astype(sum_buf.dtype)
     to_across = copy(sum_buf, far_buf, across, 2)
     to_across.start()
     out_ref[...] = p_ref[f] + near_buf[0]
     to_across.wait_recv()
-    out_ref[...] += far_buf[...]
+    out_ref[...] += far_buf[...].astype(out_ref.dtype)
     to_partner.wait_send()
     to_diagonal.wait_send()
     to_across.wait_send()
@@ -358,8 +358,8 @@
         out_specs=pl.BlockSpec(memory_space=pltpu.VMEM),
         scratch_shapes=[
             pltpu.VMEM((2,) + block, p.dtype),
-            pltpu.VMEM(block, p.dtype),
-            pltpu.VMEM(block, p.dtype),
+            pltpu.VMEM(block, jnp.bfloat16),
+            pltpu.VMEM(block, jnp.bfloat16),
             pltpu.SemaphoreType.DMA((3,)),
             pltpu.SemaphoreType.DMA((3,)),
         ],

time: 727 us -> 733 us (level)
  waiting for transfers between devices: 272 us -> 287 us
  Pallas kernels: 236 us -> 227 us
    pallas_call x2, Pallas kernels: 52.3 us -> 35.4 us  [quad_reduce(): pl.pallas_call(quad_reduce_kernel, out_shape=jax.ShapeDtypeStruct(block,...]
    reduce_scatter x1, waiting for transfers between devices: 128 us -> 143 us  [body(): lax.psum_scatter(attention_pack, ALL, scatter_dimension=0, tiled=True)]
    pallas_call x1, Pallas kernels: 105 us -> 113 us  [kv_return(): pl.pallas_call(functools.partial(kv_return_kernel, n_ctx, back), out_shap...]
  transfers between devices with their start and end apart: 6 -> 6, of which waited for: 4 -> 4; matrix products, arithmetic and copies ran while one was open for 17% -> 17% of each run, Pallas kernels for 33% -> 31%
where the time goes in v17:
time: 733 us; the launch traced here: 727 us
  waiting for transfers between devices  287 us (39%)
  Pallas kernels  227 us (31%)
  matrix products  72.4 us (10%)
  local copies, waits for them, and re-layouts  71.5 us (10%)
  other arithmetic  43.2 us (6%)
  between operations  17.3 us (2%)
  starting transfers between devices  7.86 us (1%)
    reduce_scatter x1, waiting for transfers between devices, body(): lax.psum_scatter(attention_pack, ALL, scatter_dimension=0, tiled=True)  143 us
    pallas_call x1, Pallas kernels, kv_return(): pl.pallas_call(functools.partial(kv_return_kernel, n_ctx, back), out_shap...  113 us
    all_gather x1, waiting for transfers between devices, body(): lax.all_gather(jnp.concatenate([query_weight, key_weight, value_weight, o...  85.9 us
    pallas_call x1, Pallas kernels, kv_share(): pl.pallas_call(functools.partial(kv_share_kernel, n_ctx, back), out_shape...  48.9 us
    all_gather x1, waiting for transfers between devices, body(): ff_stack = lax.all_gather(ff_pack, 'ctx', axis=0, tiled=False)  43.9 us
    pallas_call x2, Pallas kernels, quad_reduce(): pl.pallas_call(quad_reduce_kernel, out_shape=jax.ShapeDtypeStruct(block,...  35.4 us
    pallas_call x2, Pallas kernels, quad_gather(): pl.pallas_call(quad_gather_kernel, out_shape=jax.ShapeDtypeStruct((4,) +...  29.7 us
    dot_general x4, matrix products, times_transposed(): lax.dot_general(left, right, (((1,), (1,)), ((), ())), preferred_element_...  23.8 us
  transfers between devices with their start and end apart: 6, of which 4 were waited for; matrix products, arithmetic and copies ran while one was open for 17% of the time, Pallas kernels for 31%

profile of v17, /device:TPU:0, one launch (start us, length us, event | category | flops | bytes accessed | tf_op | source)
XLA Modules:
  0.0 726.8 jit_solution(5330485080862659579)
XLA Ops:
  16.6 4.2 all-to-all-start
  21.2 14.6 %all-to-all-done = bf16[4,48,2,8,128]{4,3,1,2,0:T(8,128)(2,1)S(1)} async-done(((bf16[4,48,2,8,128]{4,3,1,2,0:T(8,128)(2,1)}), bf16[4,48,2,8,128]{4,3,1,2,0:T(8,128)(2,1)S(1)}, u32[]{:S(2)}, u32[]{:S(2)}) %all-to-all-start) | async-done | bytes 786464 | tf_op jit(solution)/shard_map/all_to_all | solution.py:452
  36.9 85.9 %all-gather.3.cloned.1.call-done = bf16[1536,4736]{1,0:T(8,128)(2,1)} async-done(((bf16[48,4736]{1,0:T(8,128)(2,1)}), bf16[1536,4736]{1,0:T(8,128)(2,1)}) %all-gather.3.cloned.1.call-update) | async-done | bytes 14549008 | tf_op jit(solution)/shard_map/all_gather | solution.py:408
  126.6 14.8 %shard_map.205 = bf16[4,128,1536]{2,1,0:T(8,128)(2,1)} custom-call(bf16[128,1536]{1,0:T(8,128)(2,1)} %bitcast.172), custom_call_target="tpu_custom_call" | custom-call | tf_op jit(solution)/shard_map/pallas_call | solution.py:311
  144.0 5.2 fusion.5
  151.6 48.9 %shard_map.203 = bf16[5,128,1536]{2,1,0:T(8,128)(2,1)} custom-call(bf16[128,1536]{1,0:T(8,128)(2,1)} %pad_maximum_fusion.4.kv_ref), custom_call_target="tpu_custom_call" | custom-call | tf_op jit(solution)/shard_map/pallas_call | solution.py:116
  205.5 4.4 fusion.58
  218.9 14.9 %shard_map.204 = bf16[4,128,1536]{2,1,0:T(8,128)(2,1)} custom-call(bf16[128,1536]{1,0:T(8,128)(2,1)} %multiply_convert_fusion.1.x_ref), custom_call_target="tpu_custom_call" | custom-call | tf_op jit(solution)/shard_map/pallas_call | solution.py:311
  233.8 43.9 %all-gather.5.cloned.1.call-done = bf16[8,288,2048]{2,1,0:T(8,128)(2,1)} async-done(((bf16[1,288,2048]{2,1,0:T(8,128)(2,1)}), bf16[8,288,2048]{2,1,0:T(8,128)(2,1)}) %all-gather.5.cloned.1.call-update) | async-done | bytes 9437200 | tf_op jit(solution)/shard_map/all_gather | solution.py:456
  277.7 4.0 slice.212
  281.7 6.0 reshape_reshape.3
  300.0 5.9 convolution_convert_fusion.1
  309.4 6.0 reshape.368
  315.4 7.9 %pad_maximum_fusion = bf16[8,288,2048]{2,1,0:T(8,128)(2,1)} fusion(bf16[8,96,2048]{2,1,0:T(8,128)(2,1)} %reshape.368, bf16[8,192,2048]{2,1,0:T(8,128)(2,1)} %bitcast.147), kind=kLoop, calls=%fused_computation.5 | loop fusion | flops 18874368 | bytes 18874368 | tf_op jit(solution)/shard_map/concatenate | solution.py:518
  323.3 8.5 %fusion.62.p_ref = f32[4,128,1536]{2,1,0:T(8,128)} fusion(bf16[4,128,2048]{2,1,0:T(8,128)(2,1)} %bitcast.161, bf16[1536,2048,1]{1,0,2:T(8,128)(2,1)} %bitcast.144), kind=kOutput, calls=%fused_computation.134 | convolution fusion | flops 3221225472 | bytes 11534336 | tf_op jit(solution)/shard_map/dot_general | solution.py:63
  331.8 17.7 %shard_map.206 = f32[128,1536]{1,0:T(8,128)} custom-call(f32[4,128,1536]{2,1,0:T(8,128)} %fusion.62.p_ref), custom_call_target="tpu_custom_call" | custom-call | tf_op jit(solution)/shard_map/pallas_call | solution.py:354
  353.4 4.7 fusion.21
  361.4 4.1 fusion.8
  382.0 113.4 %shard_map.207 = f32[128,1536]{1,0:T(8,128)} custom-call(f32[128,1536]{1,0:T(8,128)} %fusion.42.own_ref, bf16[4,128,1536]{2,1,0:T(8,128)(2,1)} %bitcast.146), custom_call_target="tpu_custom_call" | custom-call | tf_op jit(solution)/shard_map/pallas_call | solution.py:163
  505.8 8.0 %fusion.40 = (bf16[1536]{0:T(1024)(128)(2,1)S(1)}, f32[128]{0:T(128)S(1)}, f32[128,1536]{1,0:T(8,128)}) fusion(bf16[1,128,1536]{2,1,0:T(8,128)(2,1)S(1)} %copy-done.11, f32[128]{0:T(128)S(1)} %add_rsqrt_fusion.1, f32[1536]{0:T(1024)S(1)} %get-tuple-element.40, bf16[1536,4736]{1,0:T(8,128)(2,1)} %all-gather.3.cloned.1.call-done, ...), kind=kOutput, calls=%fused_computation.59 | convolution fusion | flops 1211693440 | bytes 11413504 | tf_op jit(solution)/shard_map/dot_general | solution.py:63
  515.6 4.9 convolution_convert_fusion
  524.0 7.5 %fusion.2 = bf16[1536,4736]{1,0:T(8,128)(2,1)} fusion(bf16[1536,2]{1,0:T(8,128)(2,1)S(1)} %copy.139, bf16[1536,1536]{1,0:T(8,128)(2,1)S(1)} %convolution_convert_fusion.2, bf16[1536,3072]{1,0:T(8,128)(2,1)S(1)} %convolution_convert_fusion), kind=kLoop, calls=%fused_computation.3 | loop fusion | flops 58195968 | bytes 28710912 | tf_op jit(solution)/shard_map/concatenate | solution.py:581
  541.3 17.7 %shard_map.208 = f32[128,1536]{1,0:T(8,128)} custom-call(f32[4,128,1536]{2,1,0:T(8,128)} %bitcast.157), custom_call_target="tpu_custom_call" | custom-call | tf_op jit(solution)/shard_map/pallas_call | solution.py:354
  568.9 142.7 %reduce-scatter.3.cloned.1.call-done = bf16[48,4736]{1,0:T(8,128)(2,1)} async-done(((bf16[1536,4736]{1,0:T(8,128)(2,1)}), bf16[48,4736]{1,0:T(8,128)(2,1)}) %reduce-scatter.3.cloned.1.call-update) | async-done | bytes 454672 | tf_op jit(solution)/shard_map/reduce_scatter | solution.py:589
  (179 shorter events, 113.6 us)
Async XLA Ops:
  7.2 115.6 %all-gather.3.cloned.1.call-start = ((), (), s32[]{:S(2)}) async-start(), calls=%async_computation.4 | async-start | bytes 15003648 | tf_op jit(solution)/shard_map/all_gather | solution.py:408
  12.5 8.4 %copy-start.30 = (bf16[128,1536]{1,0:T(8,128)(2,1)S(1)}, bf16[128,1536]{1,0:T(8,128)(2,1)}, u32[]{:S(2)}) copy-start(bf16[128,1536]{1,0:T(8,128)(2,1)} %param.26) | copy-start | bytes 1179652
  16.6 19.1 %all-to-all-start = ((bf16[4,48,2,8,128]{4,3,1,2,0:T(8,128)(2,1)}), bf16[4,48,2,8,128]{4,3,1,2,0:T(8,128)(2,1)S(1)}, u32[]{:S(2)}, u32[]{:S(2)}) async-start(bf16[4,48,2,8,128]{4,3,1,2,0:T(8,128)(2,1)} %copy.127), calls=%async_computation | async-start | bytes 1572864 | tf_op jit(solution)/shard_map/all_to_all | solution.py:452
  20.8 256.8 %all-gather.5.cloned.1.call-start = ((), (), s32[]{:S(2)}) async-start(), calls=%async_computation.5 | async-start | bytes 10616832 | tf_op jit(solution)/shard_map/all_gather | solution.py:456
  21.2 105.3 %copy-start.31 = (s32[1,8]{1,0:T(1,128)S(1)}, s32[1,8]{1,0:T(1,128)}, u32[]{:S(2)}) copy-start(s32[1,8]{1,0:T(1,128)} %param.17) | copy-start | bytes 100
  36.2 105.6 %copy-start.9 = (bf16[1,128,1536]{2,1,0:T(8,128)(2,1)S(1)}, bf16[1,128,1536]{2,1,0:T(8,128)(2,1)}, u32[]{:S(2)}) copy-start(bf16[1,128,1536]{2,1,0:T(8,128)(2,1)} %param.16) | copy-start | bytes 1179652
  126.4 435.8 %reduce-scatter.5.cloned.1.call-start = ((), (), s32[]{:S(2)}) async-start(), calls=%async_computation.7 | async-start | bytes 10616832 | tf_op jit(solution)/shard_map/reduce_scatter | solution.py:526
  202.8 7.0 copy-start.14
  205.5 4.4 copy-start.19
  209.9 3.2 copy-start.13
  214.6 3.4 copy-start.17
  287.7 3.5 copy-start.22
  291.2 3.5 copy-start.7
  291.2 4.2 copy-start.15
  291.2 4.6 copy-start.21
  298.4 7.5 %copy-start.32 = (bf16[512,1024]{1,0:T(8,128)(2,1)}, bf16[512,1024]{1,0:T(8,128)(2,1)S(1)}, u32[]{:S(2)}) copy-start(bf16[512,1024]{1,0:T(8,128)(2,1)S(1)} %get-tuple-element.51) | copy-start | bytes 3145732
  323.3 388.4 %reduce-scatter.3.cloned.1.call-start = ((), (), s32[]{:S(2)}) async-start(), calls=%async_computation.6 | async-start | bytes 15003648 | tf_op jit(solution)/shard_map/reduce_scatter | solution.py:589
  361.3 5.7 copy-start.20
  382.0 121.8 %copy-start.4 = (bf16[128,8,2,640]{0,3,2,1:T(8,128)(2,1)S(1)}, bf16[128,8,2,640]{0,3,2,1:T(8,128)(2,1)}, u32[]{:S(2)}) copy-start(bf16[128,8,2,640]{0,3,2,1:T(8,128)(2,1)} %copy-done.3) | copy-start | bytes 7864324
  505.8 8.3 %copy-start.6 = (f32[128,1536]{1,0:T(8,128)S(1)}, f32[128,1536]{1,0:T(8,128)}, u32[]{:S(2)}) copy-start(f32[128,1536]{1,0:T(8,128)} %copy-done.5) | copy-start | bytes 2359300
  505.8 8.3 %copy-start.18 = (bf16[128,8,2,96]{0,3,2,1:T(8,128)(2,1)S(1)}, bf16[128,8,2,96]{0,3,2,1:T(8,128)(2,1)}, u32[]{:S(2)}) copy-start(bf16[128,8,2,96]{0,3,2,1:T(8,128)(2,1)} %copy-done.17) | copy-start | bytes 1179652
  520.5 3.5 copy-start
  538.2 22.8 %copy-start.25 = (f32[128,1536]{1,0:T(8,128)S(1)}, f32[128,1536]{1,0:T(8,128)}, u32[]{:S(2)}) copy-start(f32[128,1536]{1,0:T(8,128)} %get-tuple-element.77) | copy-start | bytes 2359300
  565.4 151.5 %all-to-all-start.1 = ((bf16[4,48,2048]{2,1,0:T(8,128)(2,1)}), bf16[4,48,2048]{2,1,0:T(8,128)(2,1)S(1)}, u32[]{:S(2)}, u32[]{:S(2)}) async-start(bf16[4,48,2048]{2,1,0:T(8,128)(2,1)} %bitcast.55), calls=%async_computation.3 | async-start | bytes 1572864 | tf_op jit(solution)/shard_map/all_to_all | solution.py:528
  (16 other events, 26.6 us)
Sparse Core Ops, SparseCore 0:
  12.6 110.1 all-gather.2
  126.5 151.1 all-gather.4
  323.4 218.3 reduce-scatter.4
  547.7 163.9 reduce-scatter.2

commit v18 on v16

--- a/solution.py
+++ b/solution.py
@@ -503,7 +503,6 @@
     up_pre = gate_up[:, units:]
     sigmoid = jax.nn.sigmoid(gate_pre)
     hidden_low = (gate_pre * sigmoid * up_pre).astype(jnp.bfloat16)
-    ff_part = jnp.dot(hidden_low, down_tp, preferred_element_type=jnp.float32)
 
     grad_out = cotangent[0]
     grad_all = fsdp_gather(grad_out, n_f).reshape(group_tokens, D)
@@ -589,7 +588,8 @@
     attention_sum = lax.psum_scatter(
         attention_pack, ALL, scatter_dimension=0, tiled=True
     ).astype(jnp.float32)
-    ff_part = ff_part.at[0, 0].add(attention_pack[0, 0].astype(jnp.float32) * 0.0)
+    late_hidden = hidden_low.at[0, 0].add(attention_pack[0, 0] * 0)
+    ff_part = jnp.dot(late_hidden, down_tp, preferred_element_type=jnp.float32)
     layer_out = middle + fsdp_reduce(ff_part.reshape(n_f, tok_rows, D), n_f)
     ff_sum = ff_sum.astype(jnp.float32)
     return (

time: 727 us -> 729 us (level)
  waiting for transfers between devices: 272 us -> 260 us
    reduce_scatter x1, waiting for transfers between devices: 128 us -> 119 us  [body(): lax.psum_scatter(attention_pack, ALL, scatter_dimension=0, tiled=True)]
    unnamed x74 -> x95, local copies, waits for them, and re-layouts: 14.6 us -> 14.1 us
  transfers between devices with their start and end apart: 6 -> 6, of which waited for: 4 -> 4; matrix products, arithmetic and copies ran while one was open for 17% -> 19% of each run, Pallas kernels for 33% -> 33%
where the time goes in v18:
time: 729 us; the launch traced here: 723 us
  waiting for transfers between devices  260 us (36%)
  Pallas kernels  239 us (33%)
  matrix products  78.2 us (11%)
  local copies, waits for them, and re-layouts  73.8 us (10%)
  other arithmetic  46.8 us (6%)
  between operations  17.4 us (2%)
  starting transfers between devices  7.84 us (1%)
    reduce_scatter x1, waiting for transfers between devices, body(): lax.psum_scatter(attention_pack, ALL, scatter_dimension=0, tiled=True)  119 us
    pallas_call x1, Pallas kernels, kv_return(): pl.pallas_call(functools.partial(kv_return_kernel, n_ctx, back), out_shap...  107 us
    all_gather x1, waiting for transfers between devices, body(): lax.all_gather(jnp.concatenate([query_weight, key_weight, value_weight, o...  87.5 us
    pallas_call x2, Pallas kernels, quad_reduce(): pl.pallas_call(quad_reduce_kernel, out_shape=jax.ShapeDtypeStruct(block,...  53.2 us
    pallas_call x1, Pallas kernels, kv_share(): pl.pallas_call(functools.partial(kv_share_kernel, n_ctx, back), out_shape...  48.9 us
    all_gather x1, waiting for transfers between devices, body(): ff_stack = lax.all_gather(ff_pack, 'ctx', axis=0, tiled=False)  38.5 us
    pallas_call x2, Pallas kernels, quad_gather(): pl.pallas_call(quad_gather_kernel, out_shape=jax.ShapeDtypeStruct((4,) +...  29.8 us
    dot_general x4, matrix products, times_transposed(): lax.dot_general(left, right, (((1,), (1,)), ((), ())), preferred_element_...  24.3 us
  transfers between devices with their start and end apart: 6, of which 4 were waited for; matrix products, arithmetic and copies ran while one was open for 19% of the time, Pallas kernels for 33%

profile of v18, /device:TPU:0, one launch (start us, length us, event | category | flops | bytes accessed | tf_op | source)
XLA Modules:
  0.0 722.9 jit_solution(2598576276211957716)
XLA Ops:
  15.2 4.2 all-to-all-start
  19.8 14.6 %all-to-all-done = bf16[4,48,2,8,128]{4,3,2,1,0:T(8,128)(2,1)S(1)} async-done(((bf16[4,48,2,8,128]{4,3,2,1,0:T(8,128)(2,1)}), bf16[4,48,2,8,128]{4,3,2,1,0:T(8,128)(2,1)S(1)}, u32[]{:S(2)}, u32[]{:S(2)}) %all-to-all-start) | async-done | bytes 786464 | tf_op jit(solution)/shard_map/all_to_all | solution.py:452
  35.3 87.5 %all-gather.3.cloned.1.call-done = bf16[1536,4736]{1,0:T(8,128)(2,1)} async-done(((bf16[48,4736]{1,0:T(8,128)(2,1)}), bf16[1536,4736]{1,0:T(8,128)(2,1)}) %all-gather.3.cloned.1.call-update) | async-done | bytes 14549008 | tf_op jit(solution)/shard_map/all_gather | solution.py:408
  126.7 14.8 %shard_map.205 = bf16[4,128,1536]{2,1,0:T(8,128)(2,1)} custom-call(bf16[128,1536]{1,0:T(8,128)(2,1)} %bitcast.171), custom_call_target="tpu_custom_call" | custom-call | tf_op jit(solution)/shard_map/pallas_call | solution.py:311
  145.3 5.2 fusion.5
  152.7 48.9 %shard_map.203 = bf16[5,128,1536]{2,1,0:T(8,128)(2,1)} custom-call(bf16[128,1536]{1,0:T(8,128)(2,1)} %pad_maximum_fusion.4.kv_ref), custom_call_target="tpu_custom_call" | custom-call | tf_op jit(solution)/shard_map/pallas_call | solution.py:116
  208.8 4.4 fusion.58
  223.3 15.0 %shard_map.204 = bf16[4,128,1536]{2,1,0:T(8,128)(2,1)} custom-call(bf16[128,1536]{1,0:T(8,128)(2,1)} %multiply_convert_fusion.1.x_ref), custom_call_target="tpu_custom_call" | custom-call | tf_op jit(solution)/shard_map/pallas_call | solution.py:311
  238.3 38.5 %all-gather.5.cloned.1.call-done = bf16[8,288,2048]{2,1,0:T(8,128)(2,1)} async-done(((bf16[1,288,2048]{2,1,0:T(8,128)(2,1)}), bf16[8,288,2048]{2,1,0:T(8,128)(2,1)}) %all-gather.5.cloned.1.call-update) | async-done | bytes 9437200 | tf_op jit(solution)/shard_map/all_gather | solution.py:456
  294.9 5.8 convolution_convert_fusion.1
  304.2 6.0 reshape.366
  310.3 7.8 %pad_maximum_fusion = bf16[8,288,2048]{2,1,0:T(8,128)(2,1)} fusion(bf16[8,96,2048]{2,1,0:T(8,128)(2,1)} %reshape.366, bf16[8,192,2048]{2,1,0:T(8,128)(2,1)} %bitcast.147), kind=kLoop, calls=%fused_computation.5 | loop fusion | flops 18874368 | bytes 18874368 | tf_op jit(solution)/shard_map/concatenate | solution.py:517
  318.2 8.5 %fusion.61.p_ref = f32[4,128,1536]{2,1,0:T(8,128)} fusion(bf16[4,128,2048]{2,1,0:T(8,128)(2,1)} %bitcast.160, bf16[1536,2048,1]{1,0,2:T(8,128)(2,1)} %bitcast.144), kind=kOutput, calls=%fused_computation.133 | convolution fusion | flops 3221225472 | bytes 11534336 | tf_op jit(solution)/shard_map/dot_general | solution.py:63
  326.7 26.2 %shard_map.206 = f32[128,1536]{1,0:T(8,128)} custom-call(f32[4,128,1536]{2,1,0:T(8,128)} %fusion.61.p_ref), custom_call_target="tpu_custom_call" | custom-call | tf_op jit(solution)/shard_map/pallas_call | solution.py:354
  357.7 4.7 fusion.21
  364.4 4.1 fusion.63
  373.2 4.1 fusion.8
  387.9 107.0 %shard_map.207 = f32[128,1536]{1,0:T(8,128)} custom-call(f32[128,1536]{1,0:T(8,128)} %fusion.42.own_ref, bf16[4,128,1536]{2,1,0:T(8,128)(2,1)} %bitcast.146), custom_call_target="tpu_custom_call" | custom-call | tf_op jit(solution)/shard_map/pallas_call | solution.py:163
  506.2 8.5 %fusion.40 = (bf16[1536]{0:T(1024)(128)(2,1)S(1)}, f32[128]{0:T(128)}, f32[128,1536]{1,0:T(8,128)}) fusion(bf16[1,128,1536]{2,1,0:T(8,128)(2,1)S(1)} %copy-done.11, f32[128]{0:T(128)S(1)} %copy-done.39, f32[1536]{0:T(1024)S(1)} %get-tuple-element.40, bf16[1536,4736]{1,0:T(8,128)(2,1)} %all-gather.3.cloned.1.call-done, bf16[128,768]{0,1:T(8,128)(2,1)S(1)} %copy-done.25, ...), kind=kOutput, calls=%fused_computation.59 | convolution fusion | flops 1211693440 | bytes 11413504 | tf_op jit(solution)/shard_map/dot_general | solution.py:63
  519.8 4.9 convolution_convert_fusion
  528.2 7.5 %fusion.2 = bf16[1536,4736]{1,0:T(8,128)(2,1)} fusion(bf16[1536,2]{1,0:T(8,128)(2,1)S(1)} %copy-done.16, bf16[1536,1536]{1,0:T(8,128)(2,1)S(1)} %convolution_convert_fusion.2, bf16[1536,3072]{1,0:T(8,128)(2,1)S(1)} %convolution_convert_fusion), kind=kLoop, calls=%fused_computation.3 | loop fusion | flops 58195968 | bytes 28710912 | tf_op jit(solution)/shard_map/concatenate | solution.py:580
  544.5 5.8 fusion.64.p_ref
  550.3 27.0 %shard_map.208 = f32[128,1536]{1,0:T(8,128)} custom-call(f32[4,128,1536]{2,1,0:T(8,128)} %fusion.64.p_ref), custom_call_target="tpu_custom_call" | custom-call | tf_op jit(solution)/shard_map/pallas_call | solution.py:354
  588.4 119.3 %reduce-scatter.3.cloned.1.call-done = bf16[48,4736]{1,0:T(8,128)(2,1)} async-done(((bf16[1536,4736]{1,0:T(8,128)(2,1)}), bf16[48,4736]{1,0:T(8,128)(2,1)}) %reduce-scatter.3.cloned.1.call-update) | async-done | bytes 454672 | tf_op jit(solution)/shard_map/reduce_scatter | solution.py:588
  (202 shorter events, 125.2 us)
Async XLA Ops:
  7.2 6.7 copy-start.31
  7.2 115.7 %all-gather.3.cloned.1.call-start = ((), (), s32[]{:S(2)}) async-start(), calls=%async_computation.4 | async-start | bytes 15003648 | tf_op jit(solution)/shard_map/all_gather | solution.py:408
  12.5 7.0 copy-start.32
  15.2 19.1 %all-to-all-start = ((bf16[4,48,2,8,128]{4,3,2,1,0:T(8,128)(2,1)}), bf16[4,48,2,8,128]{4,3,2,1,0:T(8,128)(2,1)S(1)}, u32[]{:S(2)}, u32[]{:S(2)}) async-start(bf16[4,48,2,8,128]{4,3,2,1,0:T(8,128)(2,1)} %maximum_bitcast_fusion.1), calls=%async_computation | async-start | bytes 1572864 | tf_op jit(solution)/shard_map/all_to_all | solution.py:452
  19.5 107.0 %copy-start.43 = (s32[1,8]{1,0:T(1,128)S(1)}, s32[1,8]{1,0:T(1,128)}, u32[]{:S(2)}) copy-start(s32[1,8]{1,0:T(1,128)} %param.17) | copy-start | bytes 100
  19.5 257.3 %all-gather.5.cloned.1.call-start = ((), (), s32[]{:S(2)}) async-start(), calls=%async_computation.5 | async-start | bytes 10616832 | tf_op jit(solution)/shard_map/all_gather | solution.py:456
  34.7 107.2 %copy-start.11 = (bf16[1,128,1536]{2,1,0:T(8,128)(2,1)S(1)}, bf16[1,128,1536]{2,1,0:T(8,128)(2,1)}, u32[]{:S(2)}) copy-start(bf16[1,128,1536]{2,1,0:T(8,128)(2,1)} %param.16) | copy-start | bytes 1179652
  126.4 454.2 %reduce-scatter.5.cloned.1.call-start = ((), (), s32[]{:S(2)}) async-start(), calls=%async_computation.7 | async-start | bytes 10616832 | tf_op jit(solution)/shard_map/reduce_scatter | solution.py:525
  142.1 8.4 %copy-start.38 = (f32[128]{0:T(128)}, f32[128]{0:T(128)S(1)}, u32[]{:S(2)}) copy-start(f32[128]{0:T(128)S(1)} %add_rsqrt_fusion.1) | copy-start | bytes 1540
  142.9 64.3 %copy-start.29 = (f32[128,48]{0,1:T(8,128)}, f32[128,48]{0,1:T(8,128)S(1)}, u32[]{:S(2)}) copy-start(f32[128,48]{0,1:T(8,128)S(1)} %get-tuple-element.70) | copy-start | bytes 73732
  203.9 9.4 %copy-start.13 = (bf16[640,768]{0,1:T(8,128)(2,1)}, bf16[640,768]{0,1:T(8,128)(2,1)S(1)}, u32[]{:S(2)}) copy-start(bf16[640,768]{0,1:T(8,128)(2,1)S(1)} %copy.111) | copy-start | bytes 2949124
  207.2 9.3 %copy-start.12 = (bf16[640,768]{0,1:T(8,128)(2,1)}, bf16[640,768]{0,1:T(8,128)(2,1)S(1)}, u32[]{:S(2)}) copy-start(bf16[640,768]{0,1:T(8,128)(2,1)S(1)} %copy.110) | copy-start | bytes 2949124
  216.4 5.1 copy-start.1
  293.4 7.4 %copy-start.42 = (bf16[512,1024]{1,0:T(8,128)(2,1)}, bf16[512,1024]{1,0:T(8,128)(2,1)S(1)}, u32[]{:S(2)}) copy-start(bf16[512,1024]{1,0:T(8,128)(2,1)S(1)} %get-tuple-element.51) | copy-start | bytes 3145732
  318.1 389.6 %reduce-scatter.3.cloned.1.call-start = ((), (), s32[]{:S(2)}) async-start(), calls=%async_computation.6 | async-start | bytes 15003648 | tf_op jit(solution)/shard_map/reduce_scatter | solution.py:588
  373.2 5.7 copy-start.20
  506.1 8.6 %copy-start.17 = (bf16[128,16,96]{0,2,1:T(8,128)(2,1)}, bf16[128,16,96]{0,2,1:T(8,128)(2,1)S(1)}, u32[]{:S(2)}) copy-start(bf16[128,16,96]{0,2,1:T(8,128)(2,1)S(1)} %pad_maximum_fusion.6) | copy-start | bytes 1179652
  506.2 8.5 %copy-start.35 = (bf16[1536]{0:T(1024)(128)(2,1)S(1)}, bf16[1536]{0:T(1024)(128)(2,1)}, u32[]{:S(2)}) copy-start(bf16[1536]{0:T(1024)(128)(2,1)} %get-tuple-element.41) | copy-start | bytes 9220
  519.7 8.5 %copy-start.16 = (bf16[1536,2]{1,0:T(8,128)(2,1)S(1)}, bf16[1536,2]{1,0:T(8,128)(2,1)}, u32[]{:S(2)}) copy-start(bf16[1536,2]{1,0:T(8,128)(2,1)} %copy.126) | copy-start | bytes 18436
  550.3 27.0 %copy-start.44 = (f32[128]{0:T(128)S(1)}, f32[128]{0:T(128)}, u32[]{:S(2)}) copy-start(f32[128]{0:T(128)} %get-tuple-element.44) | copy-start | bytes 1540
  550.3 27.1 %copy-start.5 = (f32[128,1536]{1,0:T(8,128)S(1)}, f32[128,1536]{1,0:T(8,128)}, u32[]{:S(2)}) copy-start(f32[128,1536]{1,0:T(8,128)} %copy-done.4) | copy-start | bytes 2359300
  550.3 29.1 %copy-start.8 = (f32[128,1536]{1,0:T(8,128)S(1)}, f32[128,1536]{1,0:T(8,128)}, u32[]{:S(2)}) copy-start(f32[128,1536]{1,0:T(8,128)} %copy-done.7) | copy-start | bytes 2359300
  550.3 29.1 %copy-start.24 = (f32[128,1536]{1,0:T(8,128)S(1)}, f32[128,1536]{1,0:T(8,128)}, u32[]{:S(2)}) copy-start(f32[128,1536]{1,0:T(8,128)} %get-tuple-element.77) | copy-start | bytes 2359300
  582.7 130.3 %all-to-all-start.1 = ((bf16[4,48,2048]{2,1,0:T(8,128)(2,1)}), bf16[4,48,2048]{2,1,0:T(8,128)(2,1)S(1)}, u32[]{:S(2)}, u32[]{:S(2)}) async-start(bf16[4,48,2048]{2,1,0:T(8,128)(2,1)} %bitcast.55), calls=%async_computation.3 | async-start | bytes 1572864 | tf_op jit(solution)/shard_map/all_to_all | solution.py:527
  (27 other events, 78.1 us)
Sparse Core Ops, SparseCore 0:
  12.6 110.1 all-gather.2
  126.6 150.1 all-gather.4
  318.3 219.4 reduce-scatter.4
  543.7 163.9 reduce-scatter.2

commit v19 on v16

--- a/solution.py
+++ b/solution.py
@@ -163,7 +163,7 @@
     return pl.pallas_call(
         functools.partial(kv_return_kernel, n_ctx, back),
         out_shape=jax.ShapeDtypeStruct(own.shape, own.dtype),
-        in_specs=[pl.BlockSpec(memory_space=pltpu.VMEM)] * 2,
+        in_specs=[pl.BlockSpec(memory_space=pltpu.VMEM), pl.BlockSpec(memory_space=pl.ANY)],
         out_specs=pl.BlockSpec(memory_space=pltpu.VMEM),
         scratch_shapes=[
             pltpu.VMEM(g.shape, g.dtype),

time: 727 us -> 727 us (level)
  no operation moved by 1% of the time
where the time goes in v19:
time: 727 us; the launch traced here: 720 us
  waiting for transfers between devices  272 us (37%)
  Pallas kernels  236 us (32%)
  matrix products  72.2 us (10%)
  local copies, waits for them, and re-layouts  71.9 us (10%)
  other arithmetic  43.1 us (6%)
  between operations  17.3 us (2%)
  starting transfers between devices  7.84 us (1%)
    reduce_scatter x1, waiting for transfers between devices, body(): lax.psum_scatter(attention_pack, ALL, scatter_dimension=0, tiled=True)  128 us
    pallas_call x1, Pallas kernels, kv_return(): pl.pallas_call(functools.partial(kv_return_kernel, n_ctx, back), out_shap...  105 us
    all_gather x1, waiting for transfers between devices, body(): lax.all_gather(jnp.concatenate([query_weight, key_weight, value_weight, o...  85.9 us
    pallas_call x2, Pallas kernels, quad_reduce(): pl.pallas_call(quad_reduce_kernel, out_shape=jax.ShapeDtypeStruct(block,...  52.3 us
    pallas_call x1, Pallas kernels, kv_share(): pl.pallas_call(functools.partial(kv_share_kernel, n_ctx, back), out_shape...  48.9 us
    all_gather x1, waiting for transfers between devices, body(): ff_stack = lax.all_gather(ff_pack, 'ctx', axis=0, tiled=False)  43.9 us
    pallas_call x2, Pallas kernels, quad_gather(): pl.pallas_call(quad_gather_kernel, out_shape=jax.ShapeDtypeStruct((4,) +...  29.7 us
    dot_general x4, matrix products, times_transposed(): lax.dot_general(left, right, (((1,), (1,)), ((), ())), preferred_element_...  23.8 us
  transfers between devices with their start and end apart: 6, of which 4 were waited for; matrix products, arithmetic and copies ran while one was open for 17% of the time, Pallas kernels for 33%

profile of v19, /device:TPU:0, one launch (start us, length us, event | category | flops | bytes accessed | tf_op | source)
XLA Modules:
  0.0 720.2 jit_solution(5586434624124023782)
XLA Ops:
  16.6 4.2 all-to-all-start
  21.2 14.6 %all-to-all-done = bf16[4,48,2,8,128]{4,3,1,2,0:T(8,128)(2,1)S(1)} async-done(((bf16[4,48,2,8,128]{4,3,1,2,0:T(8,128)(2,1)}), bf16[4,48,2,8,128]{4,3,1,2,0:T(8,128)(2,1)S(1)}, u32[]{:S(2)}, u32[]{:S(2)}) %all-to-all-start) | async-done | bytes 786464 | tf_op jit(solution)/shard_map/all_to_all | solution.py:452
  36.9 85.9 %all-gather.3.cloned.1.call-done = bf16[1536,4736]{1,0:T(8,128)(2,1)} async-done(((bf16[48,4736]{1,0:T(8,128)(2,1)}), bf16[1536,4736]{1,0:T(8,128)(2,1)}) %all-gather.3.cloned.1.call-update) | async-done | bytes 14549008 | tf_op jit(solution)/shard_map/all_gather | solution.py:408
  126.6 14.8 %shard_map.205 = bf16[4,128,1536]{2,1,0:T(8,128)(2,1)} custom-call(bf16[128,1536]{1,0:T(8,128)(2,1)} %bitcast.172), custom_call_target="tpu_custom_call" | custom-call | tf_op jit(solution)/shard_map/pallas_call | solution.py:311
  144.0 5.2 fusion.5
  151.6 48.9 %shard_map.203 = bf16[5,128,1536]{2,1,0:T(8,128)(2,1)} custom-call(bf16[128,1536]{1,0:T(8,128)(2,1)} %pad_maximum_fusion.4.kv_ref), custom_call_target="tpu_custom_call" | custom-call | tf_op jit(solution)/shard_map/pallas_call | solution.py:116
  205.5 4.4 fusion.58
  218.9 14.9 %shard_map.204 = bf16[4,128,1536]{2,1,0:T(8,128)(2,1)} custom-call(bf16[128,1536]{1,0:T(8,128)(2,1)} %multiply_convert_fusion.1.x_ref), custom_call_target="tpu_custom_call" | custom-call | tf_op jit(solution)/shard_map/pallas_call | solution.py:311
  233.8 43.9 %all-gather.5.cloned.1.call-done = bf16[8,288,2048]{2,1,0:T(8,128)(2,1)} async-done(((bf16[1,288,2048]{2,1,0:T(8,128)(2,1)}), bf16[8,288,2048]{2,1,0:T(8,128)(2,1)}) %all-gather.5.cloned.1.call-update) | async-done | bytes 9437200 | tf_op jit(solution)/shard_map/all_gather | solution.py:456
  277.7 4.0 slice.212
  281.7 6.0 reshape_reshape.3
  300.0 5.7 convolution_convert_fusion.1
  309.2 6.0 reshape.368
  315.2 7.9 %pad_maximum_fusion = bf16[8,288,2048]{2,1,0:T(8,128)(2,1)} fusion(bf16[8,96,2048]{2,1,0:T(8,128)(2,1)} %reshape.368, bf16[8,192,2048]{2,1,0:T(8,128)(2,1)} %bitcast.147), kind=kLoop, calls=%fused_computation.5 | loop fusion | flops 18874368 | bytes 18874368 | tf_op jit(solution)/shard_map/concatenate | solution.py:518
  323.1 8.5 %fusion.62.p_ref = f32[4,128,1536]{2,1,0:T(8,128)} fusion(bf16[4,128,2048]{2,1,0:T(8,128)(2,1)} %bitcast.161, bf16[1536,2048,1]{1,0,2:T(8,128)(2,1)} %bitcast.144), kind=kOutput, calls=%fused_computation.134 | convolution fusion | flops 3221225472 | bytes 11534336 | tf_op jit(solution)/shard_map/dot_general | solution.py:63
  331.6 26.2 %shard_map.206 = f32[128,1536]{1,0:T(8,128)} custom-call(f32[4,128,1536]{2,1,0:T(8,128)} %fusion.62.p_ref), custom_call_target="tpu_custom_call" | custom-call | tf_op jit(solution)/shard_map/pallas_call | solution.py:354
  361.6 4.8 fusion.21
  369.6 4.1 fusion.8
  390.5 104.8 %shard_map.207 = f32[128,1536]{1,0:T(8,128)} custom-call(f32[128,1536]{1,0:T(8,128)} %fusion.42.own_ref, bf16[4,128,1536]{2,1,0:T(8,128)(2,1)} %bitcast.146), custom_call_target="tpu_custom_call" | custom-call | tf_op jit(solution)/shard_map/pallas_call | solution.py:163
  505.6 8.0 %fusion.40 = (bf16[1536]{0:T(1024)(128)(2,1)S(1)}, f32[128]{0:T(128)S(1)}, f32[128,1536]{1,0:T(8,128)}) fusion(bf16[1,128,1536]{2,1,0:T(8,128)(2,1)S(1)} %copy-done.11, f32[128]{0:T(128)S(1)} %add_rsqrt_fusion.1, f32[1536]{0:T(1024)S(1)} %get-tuple-element.40, bf16[1536,4736]{1,0:T(8,128)(2,1)} %all-gather.3.cloned.1.call-done, ...), kind=kOutput, calls=%fused_computation.59 | convolution fusion | flops 1211693440 | bytes 11413504 | tf_op jit(solution)/shard_map/dot_general | solution.py:63
  515.4 4.9 convolution_convert_fusion
  523.8 7.5 %fusion.2 = bf16[1536,4736]{1,0:T(8,128)(2,1)} fusion(bf16[1536,2]{1,0:T(8,128)(2,1)S(1)} %copy.139, bf16[1536,1536]{1,0:T(8,128)(2,1)S(1)} %convolution_convert_fusion.2, bf16[1536,3072]{1,0:T(8,128)(2,1)S(1)} %convolution_convert_fusion), kind=kLoop, calls=%fused_computation.3 | loop fusion | flops 58195968 | bytes 28710912 | tf_op jit(solution)/shard_map/concatenate | solution.py:581
  541.2 26.1 %shard_map.208 = f32[128,1536]{1,0:T(8,128)} custom-call(f32[4,128,1536]{2,1,0:T(8,128)} %bitcast.157), custom_call_target="tpu_custom_call" | custom-call | tf_op jit(solution)/shard_map/pallas_call | solution.py:354
  577.3 127.8 %reduce-scatter.3.cloned.1.call-done = bf16[48,4736]{1,0:T(8,128)(2,1)} async-done(((bf16[1536,4736]{1,0:T(8,128)(2,1)}), bf16[48,4736]{1,0:T(8,128)(2,1)}) %reduce-scatter.3.cloned.1.call-update) | async-done | bytes 454672 | tf_op jit(solution)/shard_map/reduce_scatter | solution.py:589
  (179 shorter events, 114.0 us)
Async XLA Ops:
  7.2 115.6 %all-gather.3.cloned.1.call-start = ((), (), s32[]{:S(2)}) async-start(), calls=%async_computation.4 | async-start | bytes 15003648 | tf_op jit(solution)/shard_map/all_gather | solution.py:408
  12.5 8.4 %copy-start.30 = (bf16[128,1536]{1,0:T(8,128)(2,1)S(1)}, bf16[128,1536]{1,0:T(8,128)(2,1)}, u32[]{:S(2)}) copy-start(bf16[128,1536]{1,0:T(8,128)(2,1)} %param.26) | copy-start | bytes 1179652
  16.6 19.1 %all-to-all-start = ((bf16[4,48,2,8,128]{4,3,1,2,0:T(8,128)(2,1)}), bf16[4,48,2,8,128]{4,3,1,2,0:T(8,128)(2,1)S(1)}, u32[]{:S(2)}, u32[]{:S(2)}) async-start(bf16[4,48,2,8,128]{4,3,1,2,0:T(8,128)(2,1)} %copy.127), calls=%async_computation | async-start | bytes 1572864 | tf_op jit(solution)/shard_map/all_to_all | solution.py:452
  20.8 256.9 %all-gather.5.cloned.1.call-start = ((), (), s32[]{:S(2)}) async-start(), calls=%async_computation.5 | async-start | bytes 10616832 | tf_op jit(solution)/shard_map/all_gather | solution.py:456
  21.2 105.3 %copy-start.31 = (s32[1,8]{1,0:T(1,128)S(1)}, s32[1,8]{1,0:T(1,128)}, u32[]{:S(2)}) copy-start(s32[1,8]{1,0:T(1,128)} %param.17) | copy-start | bytes 100
  36.2 105.6 %copy-start.9 = (bf16[1,128,1536]{2,1,0:T(8,128)(2,1)S(1)}, bf16[1,128,1536]{2,1,0:T(8,128)(2,1)}, u32[]{:S(2)}) copy-start(bf16[1,128,1536]{2,1,0:T(8,128)(2,1)} %param.16) | copy-start | bytes 1179652
  126.4 444.2 %reduce-scatter.5.cloned.1.call-start = ((), (), s32[]{:S(2)}) async-start(), calls=%async_computation.7 | async-start | bytes 10616832 | tf_op jit(solution)/shard_map/reduce_scatter | solution.py:526
  202.8 7.0 copy-start.14
  205.5 4.4 copy-start.19
  209.9 3.2 copy-start.13
  214.6 3.4 copy-start.17
  287.7 3.5 copy-start.22
  291.2 3.5 copy-start.7
  291.2 4.2 copy-start.15
  291.2 4.6 copy-start.21
  298.4 7.3 %copy-start.32 = (bf16[512,1024]{1,0:T(8,128)(2,1)}, bf16[512,1024]{1,0:T(8,128)(2,1)S(1)}, u32[]{:S(2)}) copy-start(bf16[512,1024]{1,0:T(8,128)(2,1)S(1)} %get-tuple-element.51) | copy-start | bytes 3145732
  323.1 382.0 %reduce-scatter.3.cloned.1.call-start = ((), (), s32[]{:S(2)}) async-start(), calls=%async_computation.6 | async-start | bytes 15003648 | tf_op jit(solution)/shard_map/reduce_scatter | solution.py:589
  369.6 5.6 copy-start.20
  390.5 113.0 %copy-start.4 = (bf16[128,8,2,640]{0,3,2,1:T(8,128)(2,1)S(1)}, bf16[128,8,2,640]{0,3,2,1:T(8,128)(2,1)}, u32[]{:S(2)}) copy-start(bf16[128,8,2,640]{0,3,2,1:T(8,128)(2,1)} %copy-done.3) | copy-start | bytes 7864324
  505.6 8.3 %copy-start.6 = (f32[128,1536]{1,0:T(8,128)S(1)}, f32[128,1536]{1,0:T(8,128)}, u32[]{:S(2)}) copy-start(f32[128,1536]{1,0:T(8,128)} %copy-done.5) | copy-start | bytes 2359300
  505.6 8.3 %copy-start.18 = (bf16[128,8,2,96]{0,3,2,1:T(8,128)(2,1)S(1)}, bf16[128,8,2,96]{0,3,2,1:T(8,128)(2,1)}, u32[]{:S(2)}) copy-start(bf16[128,8,2,96]{0,3,2,1:T(8,128)(2,1)} %copy-done.17) | copy-start | bytes 1179652
  520.2 3.5 copy-start
  538.0 31.4 %copy-start.25 = (f32[128,1536]{1,0:T(8,128)S(1)}, f32[128,1536]{1,0:T(8,128)}, u32[]{:S(2)}) copy-start(f32[128,1536]{1,0:T(8,128)} %get-tuple-element.77) | copy-start | bytes 2359300
  573.8 136.6 %all-to-all-start.1 = ((bf16[4,48,2048]{2,1,0:T(8,128)(2,1)}), bf16[4,48,2048]{2,1,0:T(8,128)(2,1)S(1)}, u32[]{:S(2)}, u32[]{:S(2)}) async-start(bf16[4,48,2048]{2,1,0:T(8,128)(2,1)} %bitcast.55), calls=%async_computation.3 | async-start | bytes 1572864 | tf_op jit(solution)/shard_map/all_to_all | solution.py:528
  (16 other events, 26.7 us)
Sparse Core Ops, SparseCore 0:
  12.6 110.1 all-gather.2
  126.5 151.1 all-gather.4
  323.2 211.8 reduce-scatter.4
  541.1 163.9 reduce-scatter.2
